TPU v7x, 32 devices: a whole 2x2x4 slice. The times are simulated.
32 devices in a mesh: dp: 8 (over y, x, core), mp: 4 (over z).
Axes of the slice: x: 2, y: 2, z: 4, core: 2. Of those that a mesh axis runs over, the one named last changes fastest.
Arguments:
- frames: bfloat16 [4096, 1024], P(('dp', 'mp')), may hold values from -6 to 6
- codes_embed: bfloat16 [12288, 1024], P(('dp', 'mp')), may hold values from -6 to 6
- lengths: int32 [8, 8], P('dp'), may hold values from 1 to 384, 448 in all within a row
- cotangent: bfloat16 [12288, 1024], P(('dp', 'mp')), may hold values from -6 to 6
- frame_gain_a: bfloat16 [1024], replicated, may hold values from 0.099609375 to 1.8984375
- frame_qkv: bfloat16 [3, 1024, 1024], P(None, None, 'mp'), may hold values from -0.1875 to 0.1875
- frame_wout: bfloat16 [1024, 1024], P('mp'), may hold values from -1.5 to 1.5
- frame_gain_b: bfloat16 [1024], replicated, may hold values from 0.099609375 to 1.8984375
- frame_wup: bfloat16 [1024, 4096], P(None, 'mp'), may hold values from -0.1875 to 0.1875
- frame_bup: bfloat16 [4096], P('mp'), may hold values from -3 to 3
- frame_wdown: bfloat16 [4096, 1024], P('mp'), may hold values from -0.09375 to 0.09375
- frame_bdown: bfloat16 [1024], replicated, may hold values from -3 to 3
- token_gain_a: bfloat16 [1024], replicated, may hold values from 0.099609375 to 1.8984375
- token_qkv: bfloat16 [3, 1024, 1024], P(None, None, 'mp'), may hold values from -0.1875 to 0.1875
- token_wout: bfloat16 [1024, 1024], P('mp'), may hold values from -0.25 to 0.25
- token_gain_b: bfloat16 [1024], replicated, may hold values from 0.099609375 to 1.8984375
- token_wup: bfloat16 [1024, 4096], P(None, 'mp'), may hold values from -0.1875 to 0.1875
- token_bup: bfloat16 [4096], P('mp'), may hold values from -3 to 3
- token_wdown: bfloat16 [4096, 1024], P('mp'), may hold values from -0.09375 to 0.09375
- token_bdown: bfloat16 [1024], replicated, may hold values from -3 to 3
Outputs:
- output: bfloat16 [12288, 1024], P(('dp', 'mp'))
- frames_grad: float32 [4096, 1024], P(('dp', 'mp'))
- frame_gain_a_grad: float32 [1024], P(('dp', 'mp'))
- frame_qkv_grad: float32 [3, 1024, 1024], P(None, 'dp', 'mp')
- frame_wout_grad: float32 [1024, 1024], P('mp', 'dp')
- frame_gain_b_grad: float32 [1024], P(('dp', 'mp'))
- frame_wup_grad: float32 [1024, 4096], P('dp', 'mp')
- frame_bup_grad: float32 [4096], P(('dp', 'mp'))
- frame_wdown_grad: float32 [4096, 1024], P('mp', 'dp')
- frame_bdown_grad: float32 [1024], P(('dp', 'mp'))
- token_gain_a_grad: float32 [1024], P(('dp', 'mp'))
- token_qkv_grad: float32 [3, 1024, 1024], P(None, 'dp', 'mp')
- token_wout_grad: float32 [1024, 1024], P('mp', 'dp')
- token_gain_b_grad: float32 [1024], P(('dp', 'mp'))
- token_wup_grad: float32 [1024, 4096], P('dp', 'mp')
- token_bup_grad: float32 [4096], P(('dp', 'mp'))
- token_wdown_grad: float32 [4096, 1024], P('mp', 'dp')
- token_bdown_grad: float32 [1024], P(('dp', 'mp'))
Inputs may be any that keep to these rules, and one draw needn't show every extreme that they name: Each row of lengths gives the frames of the items packed one after another into one group of 512 frames; frames after the row's total are padding.
All inputs are finite; a program needn't handle non-finite values.
Results may differ from a plain program's by a relative error of at most 0.023.
Values may be sent and summed in bfloat16 or wider, within the bound.
No kernel may reach another device: no remote copies, remote signals or barrier semaphores. Data moves between devices by JAX's collectives and lax.ppermute only.
A program may use at most 192 MiB of HBM per device.

v0:
```python
import math

import jax
import jax.numpy as jnp
from jax import lax
from jax.sharding import PartitionSpec as P

HD = 64


eps = 1e-05


def normalize(stream, gain_vec):
    return stream * lax.rsqrt(jnp.mean(stream * stream, axis=-1, keepdims=True) + eps) * gain_vec


def activate(values):
    return jax.nn.gelu(values, approximate=True)


def gather_rows(normed):
    return lax.all_gather(normed, "mp", axis=0, tiled=True)


def gather_grads(grad_rows):
    return lax.all_gather(grad_rows, "mp", axis=0, tiled=True)


def sum_rows(left_rows, project):
    share = left_rows.shape[0] // lax.axis_size("mp")

    def term_rows(first_row, row_count):
        return project(left_rows)

    return lax.psum_scatter(
        term_rows(jnp.int32(0), share * lax.axis_size("mp")).astype(jnp.bfloat16),
        "mp",
        scatter_dimension=0,
        tiled=True,
    ).astype(jnp.float32)


def sum_grads(left_rows, project):
    share = left_rows.shape[0] // lax.axis_size("mp")

    def term_rows(first_row, row_count):
        return project(left_rows)

    return lax.psum_scatter(
        term_rows(jnp.int32(0), share * lax.axis_size("mp")).astype(jnp.bfloat16),
        "mp",
        scatter_dimension=0,
        tiled=True,
    ).astype(jnp.float32)


def sum_matrices(matrices):
    return (
        lax.psum_scatter(matrices[0], "dp", scatter_dimension=1, tiled=True),
        lax.psum_scatter(matrices[1], "dp", scatter_dimension=1, tiled=True),
        lax.psum_scatter(matrices[2], "dp", scatter_dimension=0, tiled=True),
        lax.psum_scatter(matrices[3], "dp", scatter_dimension=1, tiled=True),
    )


def segments(lengths, whole_rows):
    item_ends = jnp.cumsum(lengths[0], dtype=jnp.int32)
    positions = jnp.arange(whole_rows, dtype=jnp.int32)
    segment = jnp.sum(
        (positions[:, None] >= item_ends[None, :]).astype(jnp.int32), axis=1, dtype=jnp.int32
    )
    is_valid = positions < item_ends[-1]
    segment = jnp.where(is_valid, segment, positions + lengths.shape[1])
    return (segment, is_valid)


def frame_mask(segment, first_row, block_rows):
    positions = jnp.arange(segment.shape[0], dtype=jnp.int32)
    query_pos = first_row + jnp.arange(block_rows, dtype=jnp.int32)
    return (positions[None, :] <= query_pos[:, None]) & (segment[None, :] == segment[:, None])


def frame_forward(qkv_rows, segment):
    whole_rows = qkv_rows.shape[1]
    col_width = qkv_rows.shape[2]
    head_count = col_width // HD
    queries = qkv_rows[0].reshape(whole_rows, head_count, HD)
    key_rows = qkv_rows[1].reshape(whole_rows, head_count, HD)
    value_rows = qkv_rows[2].reshape(whole_rows, head_count, HD)
    block_rows = min(512, whole_rows)
    score_scale = 1.0 / math.sqrt(HD)

    def one_block(first_row):
        raw_scores = (
            jnp.einsum("qhe,khe->hqk", queries, key_rows, preferred_element_type=jnp.float32)
            * score_scale
        )
        allowed = frame_mask(segment, first_row, block_rows)
        scores = jnp.where(allowed[None], raw_scores, -1e30)
        top_score = jnp.max(scores, axis=-1, keepdims=True)
        exp_scores = jnp.exp(scores - top_score)
        exp_total = jnp.sum(exp_scores, axis=-1, keepdims=True)
        attn_probs = (exp_scores / exp_total).astype(jnp.bfloat16)
        mixed_block = jnp.einsum(
            "hqk,khe->qhe", attn_probs, value_rows, preferred_element_type=jnp.float32
        )
        log_total = top_score[:, :, 0] + jnp.log(exp_total[:, :, 0])
        return (mixed_block.astype(jnp.bfloat16).reshape(block_rows, col_width), log_total)

    firsts = jnp.arange(whole_rows // block_rows, dtype=jnp.int32) * block_rows
    mixed_blocks, log_totals = lax.map(one_block, firsts)
    return (mixed_blocks.reshape(whole_rows, col_width), log_totals)


def frame_backward(qkv_rows, log_totals, grad_mixed, segment):
    whole_rows = qkv_rows.shape[1]
    col_width = qkv_rows.shape[2]
    head_count = col_width // HD
    queries = qkv_rows[0].reshape(whole_rows, head_count, HD)
    key_rows = qkv_rows[1].reshape(whole_rows, head_count, HD)
    value_rows = qkv_rows[2].reshape(whole_rows, head_count, HD)
    grad_heads = grad_mixed.reshape(whole_rows, head_count, HD)
    block_rows = min(512, whole_rows)
    score_scale = 1.0 / math.sqrt(HD)

    def one_step(totals, inputs):
        key_grad, value_grad = totals
        first_row, log_total = inputs
        raw_scores = (
            jnp.einsum("qhe,khe->hqk", queries, key_rows, preferred_element_type=jnp.float32)
            * score_scale
        )
        allowed = frame_mask(segment, first_row, block_rows)
        scores = jnp.where(allowed[None], raw_scores, -1e30)
        attn_probs = jnp.exp(scores - log_total[:, :, None])
        value_grad = value_grad + jnp.einsum(
            "hqk,qhe->khe",
            attn_probs.astype(jnp.bfloat16),
            grad_heads,
            preferred_element_type=jnp.float32,
        )
        grad_probs = jnp.einsum(
            "qhe,khe->hqk", grad_heads, value_rows, preferred_element_type=jnp.float32
        )
        row_delta = jnp.sum(attn_probs * grad_probs, axis=-1, keepdims=True)
        grad_scores = (attn_probs * (grad_probs - row_delta)).astype(jnp.bfloat16)
        query_grad = (
            jnp.einsum("hqk,khe->qhe", grad_scores, key_rows, preferred_element_type=jnp.float32)
            * score_scale
        )
        key_grad = (
            key_grad
            + jnp.einsum("hqk,qhe->khe", grad_scores, queries, preferred_element_type=jnp.float32)
            * score_scale
        )
        return ((key_grad, value_grad), query_grad)

    firsts = jnp.arange(whole_rows // block_rows, dtype=jnp.int32) * block_rows
    zeros = jnp.zeros((whole_rows, head_count, HD), jnp.float32)
    (key_grad, value_grad), query_grads = lax.scan(one_step, (zeros, zeros), (firsts, log_totals))
    return jnp.stack(
        [
            query_grads.reshape(whole_rows, col_width),
            key_grad.reshape(whole_rows, col_width),
            value_grad.reshape(whole_rows, col_width),
        ],
        axis=1,
    ).astype(jnp.bfloat16)


def token_forward(qkv_rows):
    all_rows = qkv_rows.shape[1]
    col_width = qkv_rows.shape[2]
    head_count = col_width // HD
    frame_count = all_rows // 3
    queries = qkv_rows[0].reshape(frame_count, 3, head_count, HD)
    key_rows = qkv_rows[1].reshape(frame_count, 3, head_count, HD)
    value_rows = qkv_rows[2].reshape(frame_count, 3, head_count, HD)
    score_scale = 1.0 / math.sqrt(HD)
    raw_scores = (
        jnp.einsum("fphe,fqhe->fhpq", queries, key_rows, preferred_element_type=jnp.float32)
        * score_scale
    )
    places = jnp.arange(3, dtype=jnp.int32)
    allowed = places[None, :] <= places[:, None]
    scores = jnp.where(allowed, raw_scores, -1e30)
    attn_probs = jax.nn.softmax(scores, axis=-1)
    mixed_rows = jnp.einsum(
        "fhpq,fqhe->fphe",
        attn_probs.astype(jnp.bfloat16),
        value_rows,
        preferred_element_type=jnp.float32,
    )
    return (mixed_rows.astype(jnp.bfloat16).reshape(all_rows, col_width), attn_probs)


def token_backward(qkv_rows, attn_probs, grad_mixed):
    all_rows = qkv_rows.shape[1]
    col_width = qkv_rows.shape[2]
    head_count = col_width // HD
    frame_count = all_rows // 3
    queries = qkv_rows[0].reshape(frame_count, 3, head_count, HD)
    key_rows = qkv_rows[1].reshape(frame_count, 3, head_count, HD)
    value_rows = qkv_rows[2].reshape(frame_count, 3, head_count, HD)
    grad_heads = grad_mixed.reshape(frame_count, 3, head_count, HD)
    score_scale = 1.0 / math.sqrt(HD)
    value_grad = jnp.einsum(
        "fhpq,fphe->fqhe",
        attn_probs.astype(jnp.bfloat16),
        grad_heads,
        preferred_element_type=jnp.float32,
    )
    grad_probs = jnp.einsum(
        "fphe,fqhe->fhpq", grad_heads, value_rows, preferred_element_type=jnp.float32
    )
    row_delta = jnp.sum(attn_probs * grad_probs, axis=-1, keepdims=True)
    grad_scores = (attn_probs * (grad_probs - row_delta)).astype(jnp.bfloat16)
    query_grad = (
        jnp.einsum("fhpq,fqhe->fphe", grad_scores, key_rows, preferred_element_type=jnp.float32)
        * score_scale
    )
    key_grad = (
        jnp.einsum("fhpq,fphe->fqhe", grad_scores, queries, preferred_element_type=jnp.float32)
        * score_scale
    )
    return jnp.stack(
        [
            query_grad.reshape(all_rows, col_width),
            key_grad.reshape(all_rows, col_width),
            value_grad.reshape(all_rows, col_width),
        ],
        axis=1,
    ).astype(jnp.bfloat16)


def block_forward(stream, params, attend):
    gain_a, w_qkv, w_out, gain_b, w_up, b_up, w_down, b_down = params
    normed_a = normalize(stream, gain_a.astype(jnp.float32)).astype(jnp.bfloat16)
    gathered_a = gather_rows(normed_a)
    qkv_rows = jnp.einsum(
        "rd,tde->tre", gathered_a, w_qkv, preferred_element_type=jnp.float32
    ).astype(jnp.bfloat16)
    mixed_rows, kept_state = attend(qkv_rows)
    branch_a = sum_rows(
        mixed_rows, lambda row_piece: jnp.dot(row_piece, w_out, preferred_element_type=jnp.float32)
    )
    middle = stream + branch_a
    normed_b = normalize(middle, gain_b.astype(jnp.float32)).astype(jnp.bfloat16)
    gathered_b = gather_rows(normed_b)
    hidden_pre = jnp.dot(gathered_b, w_up, preferred_element_type=jnp.float32) + b_up.astype(
        jnp.float32
    )
    hidden = activate(hidden_pre).astype(jnp.bfloat16)
    branch_b = sum_rows(
        hidden, lambda row_piece: jnp.dot(row_piece, w_down, preferred_element_type=jnp.float32)
    )
    result = middle + branch_b + b_down.astype(jnp.float32)
    saved = (
        stream,
        gathered_a,
        qkv_rows,
        mixed_rows,
        kept_state,
        middle,
        gathered_b,
        hidden_pre,
        hidden,
    )
    return (result, saved)


def block_backward(grad_out, saved, params, attend_back):
    gain_a, w_qkv, w_out, gain_b, w_up, b_up, w_down, b_down = params
    stream, gathered_a, qkv_rows, mixed_rows, kept_state, middle, gathered_b, hidden_pre, hidden = (
        saved
    )
    bias_down_grad = jnp.sum(grad_out, axis=0)
    gathered_down = gather_grads(grad_out.astype(jnp.bfloat16))
    grad_hidden = jnp.einsum("rd,fd->rf", gathered_down, w_down, preferred_element_type=jnp.float32)
    grad_pre = jax.vjp(activate, hidden_pre)[1](grad_hidden)[0].astype(jnp.bfloat16)
    down_grad = jnp.einsum("rf,rd->fd", hidden, gathered_down, preferred_element_type=jnp.float32)
    up_grad = jnp.einsum("rd,rf->df", gathered_b, grad_pre, preferred_element_type=jnp.float32)
    bias_up_grad = jnp.sum(grad_pre.astype(jnp.float32), axis=0)
    grad_normed_b = sum_grads(
        grad_pre,
        lambda row_piece: jnp.einsum(
            "rf,df->rd", row_piece, w_up, preferred_element_type=jnp.float32
        ),
    )
    second_norm = jax.vjp(normalize, middle, gain_b.astype(jnp.float32))[1](grad_normed_b)
    grad_middle = grad_out + second_norm[0]
    gathered_mid = gather_grads(grad_middle.astype(jnp.bfloat16))
    grad_mixed = jnp.einsum(
        "rd,ed->re", gathered_mid, w_out, preferred_element_type=jnp.float32
    ).astype(jnp.bfloat16)
    out_grad = jnp.einsum("re,rd->ed", mixed_rows, gathered_mid, preferred_element_type=jnp.float32)
    grad_qkv = attend_back(qkv_rows, kept_state, grad_mixed)
    qkv_grad = jnp.einsum("rd,rte->tde", gathered_a, grad_qkv, preferred_element_type=jnp.float32)
    grad_normed_a = sum_grads(
        grad_qkv,
        lambda row_piece: jnp.einsum(
            "rte,tde->rd", row_piece, w_qkv, preferred_element_type=jnp.float32
        ),
    )
    first_norm = jax.vjp(normalize, stream, gain_a.astype(jnp.float32))[1](grad_normed_a)
    grad_stream = grad_middle + first_norm[0]
    return (
        grad_stream,
        (qkv_grad, out_grad, up_grad, down_grad),
        (first_norm[1], second_norm[1], bias_up_grad, bias_down_grad),
    )


def shards(
    frames,
    codes_embed,
    lengths,
    cotangent,
    frame_gain_a,
    frame_qkv,
    frame_wout,
    frame_gain_b,
    frame_wup,
    frame_bup,
    frame_wdown,
    frame_bdown,
    token_gain_a,
    token_qkv,
    token_wout,
    token_gain_b,
    token_wup,
    token_bup,
    token_wdown,
    token_bdown,
):
    frame_params = (
        frame_gain_a,
        frame_qkv,
        frame_wout,
        frame_gain_b,
        frame_wup,
        frame_bup,
        frame_wdown,
        frame_bdown,
    )
    token_params = (
        token_gain_a,
        token_qkv,
        token_wout,
        token_gain_b,
        token_wup,
        token_bup,
        token_wdown,
        token_bdown,
    )
    parts = lax.axis_size("mp")
    my_index = lax.axis_index("mp")
    local_frames = frames.shape[0]
    segment, is_valid = segments(lengths, local_frames * parts)
    mine_valid = lax.dynamic_slice_in_dim(is_valid, my_index * local_frames, local_frames, 0)
    row_valid = jnp.repeat(mine_valid, 3)[:, None]

    def frame_attend(qkv_rows):
        return frame_forward(qkv_rows, segment)

    def frame_attend_back(qkv_rows, kept_state, grad_mixed):
        return frame_backward(qkv_rows, kept_state, grad_mixed, segment)

    start_rows = frames.astype(jnp.float32)
    frame_out, frame_saved = block_forward(start_rows, frame_params, frame_attend)
    token_in = jnp.repeat(frame_out, 3, axis=0) + codes_embed.astype(jnp.float32)
    token_out, token_saved = block_forward(token_in, token_params, token_forward)
    output = jnp.where(row_valid, token_out, 0.0).astype(jnp.bfloat16)
    grad_tokens = jnp.where(row_valid, cotangent.astype(jnp.float32), 0.0)
    grad_token_in, token_mats, token_vecs = block_backward(
        grad_tokens, token_saved, token_params, token_backward
    )
    token_sums = sum_matrices(token_mats)
    frame_state = block_forward(start_rows, frame_params, frame_attend)[1]
    grad_frame_out = jnp.sum(grad_token_in.reshape(local_frames, 3, grad_token_in.shape[1]), axis=1)
    frames_grad, frame_mats, frame_vecs = block_backward(
        grad_frame_out, frame_state, frame_params, frame_attend_back
    )
    frame_sums = sum_matrices(frame_mats)

    def widen(bias_grad):
        padded = jnp.zeros((bias_grad.shape[0] * parts,), jnp.float32)
        return lax.dynamic_update_slice_in_dim(padded, bias_grad, my_index * bias_grad.shape[0], 0)

    vectors = (
        lax.psum_scatter(frame_vecs[0], ("dp", "mp"), scatter_dimension=0, tiled=True),
        lax.psum_scatter(frame_vecs[1], ("dp", "mp"), scatter_dimension=0, tiled=True),
        lax.psum_scatter(widen(frame_vecs[2]), ("dp", "mp"), scatter_dimension=0, tiled=True),
        lax.psum_scatter(frame_vecs[3], ("dp", "mp"), scatter_dimension=0, tiled=True),
        lax.psum_scatter(token_vecs[0], ("dp", "mp"), scatter_dimension=0, tiled=True),
        lax.psum_scatter(token_vecs[1], ("dp", "mp"), scatter_dimension=0, tiled=True),
        lax.psum_scatter(widen(token_vecs[2]), ("dp", "mp"), scatter_dimension=0, tiled=True),
        lax.psum_scatter(token_vecs[3], ("dp", "mp"), scatter_dimension=0, tiled=True),
    )
    return (
        output,
        frames_grad,
        vectors[0],
        frame_sums[0],
        frame_sums[1],
        vectors[1],
        frame_sums[2],
        vectors[2],
        frame_sums[3],
        vectors[3],
        vectors[4],
        token_sums[0],
        token_sums[1],
        vectors[5],
        token_sums[2],
        vectors[6],
        token_sums[3],
        vectors[7],
    )


def solution(mesh):
    placed = (
        P(("dp", "mp"), None),
        P(("dp", "mp"), None),
        P("dp", None),
        P(("dp", "mp"), None),
        P(),
        P(None, None, "mp"),
        P("mp", None),
        P(),
        P(None, "mp"),
        P("mp"),
        P("mp", None),
        P(),
        P(),
        P(None, None, "mp"),
        P("mp", None),
        P(),
        P(None, "mp"),
        P("mp"),
        P("mp", None),
        P(),
    )
    return jax.shard_map(
        shards,
        mesh=mesh,
        in_specs=placed,
        out_specs=(
            P(("dp", "mp"), None),
            P(("dp", "mp"), None),
            P(("dp", "mp")),
            P(None, "dp", "mp"),
            P("mp", "dp"),
            P(("dp", "mp")),
            P("dp", "mp"),
            P(("dp", "mp")),
            P("mp", "dp"),
            P(("dp", "mp")),
            P(("dp", "mp")),
            P(None, "dp", "mp"),
            P("mp", "dp"),
            P(("dp", "mp")),
            P("dp", "mp"),
            P(("dp", "mp")),
            P("mp", "dp"),
            P(("dp", "mp")),
        ),
        check_vma=False,
    )
```

profile of v0, /device:TPU:8, one launch (start us, length us, event | category | flops | bytes accessed | tf_op | source)
XLA Modules:
  0.0 1316.6 jit_solution(8523894774684310933)
XLA Ops:
  13.9 26.8 %all-gather.9.cloned.1.call-done = bf16[512,1024]{1,0:T(8,128)(2,1)} async-done(((bf16[128,1024]{1,0:T(8,128)(2,1)}), bf16[512,1024]{1,0:T(8,128)(2,1)}) %all-gather.9.cloned.1.call-update) | async-done | bytes 1048592 | tf_op jit(solution)/shard_map/all_gather | solution.py:23
  49.7 24.7 %reduce-scatter.17.cloned.1.call-done = bf16[128,1024]{1,0:T(8,128)(2,1)} async-done(((bf16[512,1024]{1,0:T(8,128)(2,1)}), bf16[128,1024]{1,0:T(8,128)(2,1)}) %reduce-scatter.17.cloned.1.call-update) | async-done | bytes 262160 | tf_op jit(solution)/shard_map/reduce_scatter | solution.py:36
  77.8 28.7 %all-gather.11.cloned.1.call-done = bf16[512,1024]{1,0:T(8,128)(2,1)} async-done(((bf16[128,1024]{1,0:T(8,128)(2,1)}), bf16[512,1024]{1,0:T(8,128)(2,1)}) %all-gather.11.cloned.1.call-update) | async-done | bytes 1048592 | tf_op jit(solution)/shard_map/all_gather | solution.py:23
  113.8 24.7 %reduce-scatter.19.cloned.1.call-done = bf16[128,1024]{1,0:T(8,128)(2,1)} async-done(((bf16[512,1024]{1,0:T(8,128)(2,1)}), bf16[128,1024]{1,0:T(8,128)(2,1)}) %reduce-scatter.19.cloned.1.call-update) | async-done | bytes 262160 | tf_op jit(solution)/shard_map/reduce_scatter | solution.py:36
  149.4 62.0 %all-gather.13.cloned.1.call-done = bf16[1536,1024]{1,0:T(8,128)(2,1)} async-done(((bf16[384,1024]{1,0:T(8,128)(2,1)}), bf16[1536,1024]{1,0:T(8,128)(2,1)}) %all-gather.13.cloned.1.call-update) | async-done | bytes 3145744 | tf_op jit(solution)/shard_map/all_gather | solution.py:23
  226.5 11.9 fusion.105
  253.4 60.3 %reduce-scatter.21.cloned.1.call-done = bf16[384,1024]{1,0:T(8,128)(2,1)} async-done(((bf16[1536,1024]{1,0:T(8,128)(2,1)}), bf16[384,1024]{1,0:T(8,128)(2,1)}) %reduce-scatter.21.cloned.1.call-update) | async-done | bytes 786448 | tf_op jit(solution)/shard_map/reduce_scatter | solution.py:36
  320.6 58.4 %all-gather.15.cloned.1.call-done = bf16[1536,1024]{1,0:T(8,128)(2,1)} async-done(((bf16[384,1024]{1,0:T(8,128)(2,1)}), bf16[1536,1024]{1,0:T(8,128)(2,1)}) %all-gather.15.cloned.1.call-update) | async-done | bytes 3145744 | tf_op jit(solution)/shard_map/all_gather | solution.py:23
  387.6 55.2 %all-gather.17.cloned.1.call-done = bf16[1536,1024]{1,0:T(8,128)(2,1)} async-done(((bf16[384,1024]{1,0:T(8,128)(2,1)}), bf16[1536,1024]{1,0:T(8,128)(2,1)}) %all-gather.17.cloned.1.call-update) | async-done | bytes 3145744 | tf_op jit(solution)/shard_map/all_gather | solution.py:27
  460.4 60.7 %reduce-scatter.25.cloned.1.call-done = bf16[384,1024]{1,0:T(8,128)(2,1)} async-done(((bf16[1536,1024]{1,0:T(8,128)(2,1)}), bf16[384,1024]{1,0:T(8,128)(2,1)}) %reduce-scatter.25.cloned.1.call-update) | async-done | bytes 786448 | tf_op jit(solution)/shard_map/reduce_scatter | solution.py:50
  525.3 61.8 %all-gather.19.cloned.1.call-done = bf16[1536,1024]{1,0:T(8,128)(2,1)} async-done(((bf16[384,1024]{1,0:T(8,128)(2,1)}), bf16[1536,1024]{1,0:T(8,128)(2,1)}) %all-gather.19.cloned.1.call-update) | async-done | bytes 3145744 | tf_op jit(solution)/shard_map/all_gather | solution.py:27
  601.0 11.7 multiply_reduce_fusion.1
  661.8 51.5 %reduce-scatter.27.cloned.1.call-done = bf16[384,1024]{1,0:T(8,128)(2,1)} async-done(((bf16[1536,1024]{1,0:T(8,128)(2,1)}), bf16[384,1024]{1,0:T(8,128)(2,1)}) %reduce-scatter.27.cloned.1.call-update) | async-done | bytes 786448 | tf_op jit(solution)/shard_map/reduce_scatter | solution.py:50
  715.5 60.3 %reduce-scatter.23.cloned.1.call-done = bf16[384,1024]{1,0:T(8,128)(2,1)} async-done(((bf16[1536,1024]{1,0:T(8,128)(2,1)}), bf16[384,1024]{1,0:T(8,128)(2,1)}) %reduce-scatter.23.cloned.1.call-update) | async-done | bytes 786448 | tf_op jit(solution)/shard_map/reduce_scatter | solution.py:36
  787.2 28.5 %all-gather.21.cloned.1.call-done = bf16[512,1024]{1,0:T(8,128)(2,1)} async-done(((bf16[128,1024]{1,0:T(8,128)(2,1)}), bf16[512,1024]{1,0:T(8,128)(2,1)}) %all-gather.21.cloned.1.call-update) | async-done | bytes 1048592 | tf_op jit(solution)/shard_map/all_gather | solution.py:27
  824.3 24.7 %reduce-scatter.29.cloned.1.call-done = bf16[128,1024]{1,0:T(8,128)(2,1)} async-done(((bf16[512,1024]{1,0:T(8,128)(2,1)}), bf16[128,1024]{1,0:T(8,128)(2,1)}) %reduce-scatter.29.cloned.1.call-update) | async-done | bytes 262160 | tf_op jit(solution)/shard_map/reduce_scatter | solution.py:50
  859.7 21.1 %all-gather.23.cloned.1.call-done = bf16[512,1024]{1,0:T(8,128)(2,1)} async-done(((bf16[128,1024]{1,0:T(8,128)(2,1)}), bf16[512,1024]{1,0:T(8,128)(2,1)}) %all-gather.23.cloned.1.call-update) | async-done | bytes 1048592 | tf_op jit(solution)/shard_map/all_gather | solution.py:27
  958.7 42.1 %all-reduce.8 = (f32[1024]{0:T(1024)S(1)}, f32[1024]{0:T(1024)S(1)}, f32[4096]{0:T(1024)S(1)}, f32[1024]{0:T(1024)S(1)}, f32[1024]{0:T(1024)S(1)}, /*index=5*/f3...) all-reduce(f32[1024]{0:T(1024)S(1)} %get-tuple-element.165, ...), channel_id=10, replica_groups=mesh['dp'=8,'mp'=4] {'dp','mp'}, use_global_device_ids=true, to_apply=%region_26.27.clone | all-reduce | flops 14336 | bytes 114688
  1010.2 53.4 %reduce-scatter.47.cloned.1.call-done = f32[1024,128]{1,0:T(8,128)} async-done(((f32[1024,1024]{1,0:T(8,128)}), f32[1024,128]{1,0:T(8,128)}) %reduce-scatter.47.cloned.1.call-update) | async-done | bytes 524304 | tf_op jit(solution)/shard_map/reduce_scatter | solution.py:63
  1063.6 55.5 %reduce-scatter.45.cloned.1.call-done = f32[128,1024]{1,0:T(8,128)} async-done(((f32[1024,1024]{1,0:T(8,128)}), f32[128,1024]{1,0:T(8,128)}) %reduce-scatter.45.cloned.1.call-update) | async-done | bytes 524304 | tf_op jit(solution)/shard_map/reduce_scatter | solution.py:62
  1119.2 39.8 %reduce-scatter.43.cloned.1.call-done = f32[256,128]{1,0:T(8,128)} async-done(((f32[256,1024]{1,0:T(8,128)}), f32[256,128]{1,0:T(8,128)}) %reduce-scatter.43.cloned.1.call-update) | async-done | bytes 131088 | tf_op jit(solution)/shard_map/reduce_scatter | solution.py:61
  1159.0 39.8 %reduce-scatter.35.cloned.1.call-done = f32[256,128]{1,0:T(8,128)} async-done(((f32[256,1024]{1,0:T(8,128)}), f32[256,128]{1,0:T(8,128)}) %reduce-scatter.35.cloned.1.call-update) | async-done | bytes 131088 | tf_op jit(solution)/shard_map/reduce_scatter | solution.py:61
  1198.7 55.3 %reduce-scatter.39.cloned.1.call-done = f32[1024,128]{1,0:T(8,128)} async-done(((f32[1024,1024]{1,0:T(8,128)}), f32[1024,128]{1,0:T(8,128)}) %reduce-scatter.39.cloned.1.call-update) | async-done | bytes 524304 | tf_op jit(solution)/shard_map/reduce_scatter | solution.py:63
  1254.0 55.6 %reduce-scatter.37.cloned.1.call-done = f32[128,1024]{1,0:T(8,128)} async-done(((f32[1024,1024]{1,0:T(8,128)}), f32[128,1024]{1,0:T(8,128)}) %reduce-scatter.37.cloned.1.call-update) | async-done | bytes 524304 | tf_op jit(solution)/shard_map/reduce_scatter | solution.py:62
  (292 shorter events, 287.1 us)
Async XLA Ops:
  7.2 33.5 %all-gather.9.cloned.1.call-start = ((), (), s32[]{:S(2)}) async-start(), calls=%async_computation.16 | async-start | bytes 1310720 | tf_op jit(solution)/shard_map/all_gather | solution.py:23
  11.5 62.8 %reduce-scatter.17.cloned.1.call-start = ((), (), s32[]{:S(2)}) async-start(), calls=%async_computation.17 | async-start | bytes 1310720 | tf_op jit(solution)/shard_map/reduce_scatter | solution.py:36
  49.6 57.0 %all-gather.11.cloned.1.call-start = ((), (), s32[]{:S(2)}) async-start(), calls=%async_computation.18 | async-start | bytes 1310720 | tf_op jit(solution)/shard_map/all_gather | solution.py:23
  77.8 60.7 %reduce-scatter.19.cloned.1.call-start = ((), (), s32[]{:S(2)}) async-start(), calls=%async_computation.19 | async-start | bytes 1310720 | tf_op jit(solution)/shard_map/reduce_scatter | solution.py:36
  113.7 97.7 %all-gather.13.cloned.1.call-start = ((), (), s32[]{:S(2)}) async-start(), calls=%async_computation.20 | async-start | bytes 3932160 | tf_op jit(solution)/shard_map/all_gather | solution.py:23
  149.3 164.3 %reduce-scatter.21.cloned.1.call-start = ((), (), s32[]{:S(2)}) async-start(), calls=%async_computation.21 | async-start | bytes 3932160 | tf_op jit(solution)/shard_map/reduce_scatter | solution.py:36
  252.7 126.2 %all-gather.15.cloned.1.call-start = ((), (), s32[]{:S(2)}) async-start(), calls=%async_computation.22 | async-start | bytes 3932160 | tf_op jit(solution)/shard_map/all_gather | solution.py:23
  317.2 125.6 %all-gather.17.cloned.1.call-start = ((), (), s32[]{:S(2)}) async-start(), calls=%async_computation.24 | async-start | bytes 3932160 | tf_op jit(solution)/shard_map/all_gather | solution.py:27
  320.5 200.6 %reduce-scatter.25.cloned.1.call-start = ((), (), s32[]{:S(2)}) async-start(), calls=%async_computation.25 | async-start | bytes 3932160 | tf_op jit(solution)/shard_map/reduce_scatter | solution.py:50
  460.2 126.9 %all-gather.19.cloned.1.call-start = ((), (), s32[]{:S(2)}) async-start(), calls=%async_computation.26 | async-start | bytes 3932160 | tf_op jit(solution)/shard_map/all_gather | solution.py:27
  525.2 188.1 %reduce-scatter.27.cloned.1.call-start = ((), (), s32[]{:S(2)}) async-start(), calls=%async_computation.27 | async-start | bytes 3932160 | tf_op jit(solution)/shard_map/reduce_scatter | solution.py:50
  652.4 123.4 %reduce-scatter.23.cloned.1.call-start = ((), (), s32[]{:S(2)}) async-start(), calls=%async_computation.23 | async-start | bytes 3932160 | tf_op jit(solution)/shard_map/reduce_scatter | solution.py:36
  661.2 154.6 %all-gather.21.cloned.1.call-start = ((), (), s32[]{:S(2)}) async-start(), calls=%async_computation.28 | async-start | bytes 1310720 | tf_op jit(solution)/shard_map/all_gather | solution.py:27
  787.2 61.8 %reduce-scatter.29.cloned.1.call-start = ((), (), s32[]{:S(2)}) async-start(), calls=%async_computation.29 | async-start | bytes 1310720 | tf_op jit(solution)/shard_map/reduce_scatter | solution.py:50
  824.2 56.6 %all-gather.23.cloned.1.call-start = ((), (), s32[]{:S(2)}) async-start(), calls=%async_computation.30 | async-start | bytes 1310720 | tf_op jit(solution)/shard_map/all_gather | solution.py:27
  852.1 95.6 %reduce-scatter.41.cloned.1.call-start = ((), (), s32[]{:S(2)}) async-start(), calls=%async_computation.36 | async-start | bytes 3538944 | tf_op jit(solution)/shard_map/reduce_scatter | solution.py:60
  859.0 98.5 %reduce-scatter.31.cloned.1.call-start = ((), (), s32[]{:S(2)}) async-start(), calls=%async_computation.31 | async-start | bytes 1310720 | tf_op jit(solution)/shard_map/reduce_scatter | solution.py:50
  906.3 102.1 %reduce-scatter.33.cloned.1.call-start = ((), (), s32[]{:S(2)}) async-start(), calls=%async_computation.32 | async-start | bytes 3538944 | tf_op jit(solution)/shard_map/reduce_scatter | solution.py:60
  910.5 153.2 %reduce-scatter.47.cloned.1.call-start = ((), (), s32[]{:S(2)}) async-start(), calls=%async_computation.39 | async-start | bytes 4718592 | tf_op jit(solution)/shard_map/reduce_scatter | solution.py:63
  920.9 198.3 %reduce-scatter.45.cloned.1.call-start = ((), (), s32[]{:S(2)}) async-start(), calls=%async_computation.38 | async-start | bytes 4718592 | tf_op jit(solution)/shard_map/reduce_scatter | solution.py:62
  929.8 229.2 %reduce-scatter.43.cloned.1.call-start = ((), (), s32[]{:S(2)}) async-start(), calls=%async_computation.37 | async-start | bytes 1179648 | tf_op jit(solution)/shard_map/reduce_scatter | solution.py:61
  934.0 264.7 %reduce-scatter.35.cloned.1.call-start = ((), (), s32[]{:S(2)}) async-start(), calls=%async_computation.33 | async-start | bytes 1179648 | tf_op jit(solution)/shard_map/reduce_scatter | solution.py:61
  936.9 317.1 %reduce-scatter.39.cloned.1.call-start = ((), (), s32[]{:S(2)}) async-start(), calls=%async_computation.35 | async-start | bytes 4718592 | tf_op jit(solution)/shard_map/reduce_scatter | solution.py:63
  942.4 367.1 %reduce-scatter.37.cloned.1.call-start = ((), (), s32[]{:S(2)}) async-start(), calls=%async_computation.34 | async-start | bytes 4718592 | tf_op jit(solution)/shard_map/reduce_scatter | solution.py:62
  (60 other events, 981.3 us)
Sparse Core Ops, SparseCore 0:
  11.6 29.0 all-gather.8
  49.7 24.5 reduce-scatter.16
  77.9 28.6 all-gather.10
  113.8 24.6 reduce-scatter.18
  149.5 61.8 all-gather.12
  252.9 60.7 reduce-scatter.20
  317.3 61.6 all-gather.14
  380.6 62.1 all-gather.16
  460.3 60.7 reduce-scatter.24
  525.4 61.6 all-gather.18
  652.5 60.7 reduce-scatter.26
  715.5 60.2 reduce-scatter.22
  787.3 28.3 all-gather.20
  824.3 24.5 reduce-scatter.28
  852.2 28.6 all-gather.22
  884.5 45.7 reduce-scatter.40
  932.4 25.0 reduce-scatter.30
  961.1 47.1 reduce-scatter.32
  1012.2 51.3 reduce-scatter.46
  1067.8 51.3 reduce-scatter.44
  1122.9 35.9 reduce-scatter.42
  1162.7 35.9 reduce-scatter.34
  1202.7 51.2 reduce-scatter.38
  1258.2 51.3 reduce-scatter.36
where the time goes:
time: 1330 us; the launch traced here: 1320 us
  waiting for transfers between devices  957 us (72%)
  matrix products  176 us (13%)
  local copies, waits for them, and re-layouts  78.2 us (6%)
  other arithmetic  45.3 us (3%)
  blocking collectives  42.1 us (3%)
  between operations  15.3 us (1%)
    all_gather x4, waiting for transfers between devices, gather_rows(): return lax.all_gather(normed, 'mp', axis=0, tiled=True)  176 us
    reduce_scatter x4, waiting for transfers between devices, sum_rows(): lax.psum_scatter(term_rows(jnp.int32(0), share * lax.axis_size('mp')).ast...  170 us
    all_gather x4, waiting for transfers between devices, gather_grads(): return lax.all_gather(grad_rows, 'mp', axis=0, tiled=True)  167 us
    reduce_scatter x4, waiting for transfers between devices, sum_grads(): lax.psum_scatter(term_rows(jnp.int32(0), share * lax.axis_size('mp')).ast...  145 us
    reduce_scatter x2, waiting for transfers between devices, sum_matrices(): lax.psum_scatter(matrices[2], 'dp', scatter_dimension=0, tiled=True)  111 us
    reduce_scatter x2, waiting for transfers between devices, sum_matrices(): lax.psum_scatter(matrices[3], 'dp', scatter_dimension=1, tiled=True)  109 us
    reduce_scatter x2, waiting for transfers between devices, sum_matrices(): lax.psum_scatter(matrices[1], 'dp', scatter_dimension=1, tiled=True)  79.6 us
    unnamed x1, blocking collectives  42.1 us
  transfers between devices with their start and end apart: 24, of which 23 were waited for; matrix products, arithmetic and copies ran while one was open for 8% of the time, Pallas kernels for 0%

commit v1 on v0

v1 whole, which is shorter than its diff:
```python
import math

import jax
import jax.numpy as jnp
from jax import lax
from jax.sharding import PartitionSpec as P

HD = 64
eps = 1e-05
BF = jnp.bfloat16
F32 = jnp.float32


def normalize(stream, gain_vec):
    return stream * lax.rsqrt(jnp.mean(stream * stream, axis=-1, keepdims=True) + eps) * gain_vec


def activate(values):
    return jax.nn.gelu(values, approximate=True)


def dot_nt(a, b):
    return lax.dot_general(a, b, (((1,), (1,)), ((), ())), preferred_element_type=F32)


def dot_nn(a, b):
    return lax.dot_general(a, b, (((1,), (0,)), ((), ())), preferred_element_type=F32)


def dot_tn(a, b):
    return lax.dot_general(a, b, (((0,), (0,)), ((), ())), preferred_element_type=F32)


def gather_rows(rows):
    return lax.all_gather(rows, "mp", axis=0, tiled=True)


def scatter_rows(partial):
    return lax.psum_scatter(
        partial.astype(BF), "mp", scatter_dimension=0, tiled=True
    ).astype(F32)


def swap_dp(value, bit):
    size = lax.axis_size("dp")
    return lax.ppermute(value, "dp", [(i, i ^ bit) for i in range(size)])


def swap_mp(value, mask):
    size = lax.axis_size("mp")
    return lax.ppermute(value, "mp", [(i, i ^ mask) for i in range(size)])


def plane_bits():
    size = lax.axis_size("dp")
    bits = []
    bit = 2
    while bit < size:
        bits.append(bit)
        bit *= 2
    return bits


def gather_shards(piece):
    z = lax.axis_index("mp")
    near = swap_mp(piece, 1)
    far = swap_mp(piece, 2)
    inner = lax.ppermute(piece, "mp", [(1, 2), (2, 1)])
    outer = lax.ppermute(far, "mp", [(2, 3), (1, 0)])
    middle = (z == 1) | (z == 2)
    last = jnp.where(middle, inner, outer)
    return jnp.concatenate([near, far, last], axis=1)


def gather_plane(block, order):
    masks = [0]
    parts = [block]
    whole = block
    for bit in order:
        got = swap_dp(whole, bit)
        k = block.shape[1]
        parts = parts + [got[:, i * k : (i + 1) * k] for i in range(len(masks))]
        masks = masks + [m ^ bit for m in masks]
        if bit == order[-1]:
            ranked = sorted(range(len(masks)), key=lambda i: masks[i])
            whole = jnp.concatenate([parts[i] for i in ranked], axis=1)
        else:
            whole = jnp.concatenate(parts, axis=1)
    return whole


def own_piece(shard_rows):
    dp = lax.axis_size("dp")
    k = shard_rows.shape[1] // dp
    return lax.dynamic_slice_in_dim(shard_rows, lax.axis_index("dp") * k, k, 1)


def gather_weight(shard_rows, order):
    mine = gather_plane(gather_shards(own_piece(shard_rows)), order)
    other = swap_dp(mine, 1)
    return jnp.concatenate([shard_rows, mine, other], axis=1)


def by_xor(slots):
    me = lax.axis_index("dp")
    for bit in [1] + plane_bits():
        on = (me & bit) != 0
        slots = [jnp.where(on, slots[i ^ bit], slots[i]) for i in range(len(slots))]
    return slots


def gather_bias(bias):
    dp = lax.axis_size("dp")
    n = bias.shape[0]
    k = n // dp
    row = bias.reshape(1, 1, n)
    rest = gather_shards(row).reshape(3, dp, k)
    slots = by_xor([rest[:, i] for i in range(dp)])
    rest = jnp.stack(slots[0::2] + slots[1::2])
    return jnp.concatenate([bias, rest.reshape(3 * n)])


def d_blocks(rows):
    dp = lax.axis_size("dp")
    block = rows.shape[1] // dp
    view = by_xor([rows[:, i * block : (i + 1) * block] for i in range(dp)])
    return view[0::2], view[1::2]


def swap_masks(value, bit, segs):
    own, per, count = segs
    pieces = [value[:own]] if own else []
    shift = bit // 2
    for core in range(2):
        base = own + core * per * count
        for m in range(count):
            at = base + (m ^ shift) * per
            pieces.append(value[at : at + per])
    return jnp.concatenate(pieces, axis=0)


def scatter_plane(make, order, segs):
    bits = list(order)
    count = 1 << len(bits)
    masks = list(range(count))
    first = bits[0] // 2
    keep_masks = [m for m in masks if not m & first]
    send_masks = [m for m in masks if m & first]
    if len(bits) > 1:
        nxt = bits[1] // 2
        keep_masks = sorted(keep_masks, key=lambda m: (bool(m & nxt), m))
    send_masks = [m ^ first for m in keep_masks]
    send_masks = [m | first for m in send_masks]
    block_send = make(send_masks)
    block_keep = make(keep_masks)
    held = keep_masks
    got = swap_dp(block_send, bits[0])
    if segs is not None:
        got = swap_masks(got, bits[0], segs)
    total = block_keep.astype(F32) + got.astype(F32)
    for i, bit in enumerate(bits[1:], start=1):
        b = bit // 2
        width = total.shape[1] // len(held)
        low = [j for j, m in enumerate(held) if not m & b]
        high = [j for j, m in enumerate(held) if m & b]
        high = [next(j for j in high if held[j] == held[q] | b) for q in low]
        pick = lambda js: jnp.concatenate([total[:, j * width : (j + 1) * width] for j in js], axis=1)
        got = swap_dp(pick(high).astype(BF), bit)
        if segs is not None:
            got = swap_masks(got, bit, segs)
        total = pick(low) + got.astype(F32)
        held = [held[j] for j in low]
    return total


def scatter_shards(total, n):
    dp = lax.axis_size("dp")
    per = n // dp
    block = total.shape[1]
    rest = total[n:].reshape(2, dp // 2, 3, per, block).astype(BF)
    got = sum(
        swap_mp(rest[:, :, r - 1], r).astype(F32) for r in (1, 2, 3)
    )
    slots = by_xor([got[i & 1, i >> 1] for i in range(dp)])
    return total[:n] + jnp.concatenate(slots, axis=0)


def segments(lengths, whole_rows):
    count = lengths.shape[1]
    order = jnp.arange(count, dtype=jnp.int32)
    item_ends = jnp.sum(
        jnp.where(order[None, :] <= order[:, None], lengths[0][None, :], 0), axis=1, dtype=jnp.int32
    )
    positions = jnp.arange(whole_rows, dtype=jnp.int32)
    segment = jnp.sum(
        (positions[:, None] >= item_ends[None, :]).astype(jnp.int32), axis=1, dtype=jnp.int32
    )
    is_valid = positions < jnp.sum(lengths[0], dtype=jnp.int32)
    segment = jnp.where(is_valid, segment, positions + count)
    return (segment, is_valid)


def frame_allowed(segment):
    positions = jnp.arange(segment.shape[0], dtype=jnp.int32)
    return (positions[None, :] <= positions[:, None]) & (segment[None, :] == segment[:, None])


def split_heads(rows):
    return rows.reshape(rows.shape[0], rows.shape[1] // HD, HD)


def frame_forward(qkv_rows, segment):
    queries, key_rows, value_rows = (split_heads(qkv_rows[t]) for t in range(3))
    raw_scores = jnp.einsum("qhe,khe->hqk", queries, key_rows, preferred_element_type=F32) * (
        1.0 / math.sqrt(HD)
    )
    scores = jnp.where(frame_allowed(segment)[None], raw_scores, -1e30)
    top_score = jnp.max(scores, axis=-1, keepdims=True)
    exp_scores = jnp.exp(scores - top_score)
    exp_total = jnp.sum(exp_scores, axis=-1, keepdims=True)
    attn_probs = (exp_scores / exp_total).astype(BF)
    mixed = jnp.einsum("hqk,khe->qhe", attn_probs, value_rows, preferred_element_type=F32)
    log_total = top_score[:, :, 0] + jnp.log(exp_total[:, :, 0])
    return (mixed.astype(BF).reshape(qkv_rows.shape[1], -1), log_total)


def frame_backward(qkv_rows, log_total, grad_mixed, segment):
    queries, key_rows, value_rows = (split_heads(qkv_rows[t]) for t in range(3))
    grad_heads = split_heads(grad_mixed)
    scale = 1.0 / math.sqrt(HD)
    raw_scores = jnp.einsum("qhe,khe->hqk", queries, key_rows, preferred_element_type=F32) * scale
    scores = jnp.where(frame_allowed(segment)[None], raw_scores, -1e30)
    attn_probs = jnp.exp(scores - log_total[:, :, None])
    value_grad = jnp.einsum(
        "hqk,qhe->khe", attn_probs.astype(BF), grad_heads, preferred_element_type=F32
    )
    grad_probs = jnp.einsum("qhe,khe->hqk", grad_heads, value_rows, preferred_element_type=F32)
    row_delta = jnp.sum(attn_probs * grad_probs, axis=-1, keepdims=True)
    grad_scores = (attn_probs * (grad_probs - row_delta)).astype(BF)
    query_grad = jnp.einsum("hqk,khe->qhe", grad_scores, key_rows, preferred_element_type=F32) * scale
    key_grad = jnp.einsum("hqk,qhe->khe", grad_scores, queries, preferred_element_type=F32) * scale
    rows = qkv_rows.shape[1]
    return [g.reshape(rows, -1).astype(BF) for g in (query_grad, key_grad, value_grad)]


def frame_block_forward(stream, params, segment):
    gain_a, w_qkv, w_out, gain_b, w_up, b_up, w_down, b_down = params
    normed_a = normalize(stream, gain_a.astype(F32)).astype(BF)
    gathered_a = gather_rows(normed_a)
    qkv_rows = jnp.einsum(
        "rd,tde->tre", gathered_a, w_qkv, preferred_element_type=F32
    ).astype(BF)
    mixed_rows, log_total = frame_forward(qkv_rows, segment)
    middle = stream + scatter_rows(dot_nn(mixed_rows, w_out))
    normed_b = normalize(middle, gain_b.astype(F32)).astype(BF)
    gathered_b = gather_rows(normed_b)
    hidden_pre = dot_nn(gathered_b, w_up) + b_up.astype(F32)
    hidden = activate(hidden_pre).astype(BF)
    result = middle + scatter_rows(dot_nn(hidden, w_down)) + b_down.astype(F32)
    saved = (stream, gathered_a, qkv_rows, mixed_rows, log_total, middle, gathered_b, hidden_pre, hidden)
    return (result, saved)


def frame_scatter(left, right, order):
    same, cross = d_blocks(right)
    units = left.shape[1]
    give = dot_tn(left, jnp.concatenate(cross, axis=1)).astype(BF)
    hold = dot_tn(left, jnp.concatenate(same, axis=1))
    total = hold + swap_dp(give, 1).astype(F32)
    width = right.shape[1] // lax.axis_size("dp")

    def make(masks):
        return jnp.concatenate([total[:, m * width : (m + 1) * width] for m in masks], axis=1).astype(BF)

    return scatter_plane(make, order, None)


def frame_block_backward(grad_out, saved, params, segment):
    gain_a, w_qkv, w_out, gain_b, w_up, b_up, w_down, b_down = params
    stream, gathered_a, qkv_rows, mixed_rows, log_total, middle, gathered_b, hidden_pre, hidden = saved
    up_order = plane_bits()
    down_order = up_order[::-1]
    bias_down_grad = jnp.sum(grad_out, axis=0)
    gathered_down = gather_rows(grad_out.astype(BF))
    grad_hidden = dot_nt(gathered_down, w_down)
    grad_pre = jax.vjp(activate, hidden_pre)[1](grad_hidden)[0].astype(BF)
    bias_up_grad = jnp.sum(grad_pre.astype(F32), axis=0)
    grad_normed_b = scatter_rows(dot_nt(grad_pre, w_up))
    down_grad = frame_scatter(hidden, gathered_down, down_order)
    up_grad = frame_scatter(grad_pre, gathered_b, up_order)
    second_norm = jax.vjp(normalize, middle, gain_b.astype(F32))[1](grad_normed_b)
    grad_middle = grad_out + second_norm[0]
    gathered_mid = gather_rows(grad_middle.astype(BF))
    grad_mixed = dot_nt(gathered_mid, w_out).astype(BF)
    out_grad = frame_scatter(mixed_rows, gathered_mid, down_order)
    grad_qkv = frame_backward(qkv_rows, log_total, grad_mixed, segment)
    grad_all = jnp.concatenate(grad_qkv, axis=1)
    w_all = jnp.concatenate([w_qkv[0], w_qkv[1], w_qkv[2]], axis=1)
    grad_normed_a = scatter_rows(dot_nt(grad_all, w_all))
    qkv_grad = frame_scatter(grad_all, gathered_a, up_order)
    first_norm = jax.vjp(normalize, stream, gain_a.astype(F32))[1](grad_normed_a)
    grad_stream = grad_middle + first_norm[0]
    return (
        grad_stream,
        (qkv_grad, out_grad, up_grad, down_grad),
        (first_norm[1], second_norm[1], bias_up_grad, bias_down_grad),
    )


def head_table(features, own):
    at = jnp.arange(features, dtype=jnp.int32)
    shards = lax.axis_size("mp")
    own_heads = own // HD
    rest = (features - own) // 2
    piece = rest // (features // HD - own_heads)
    head = jnp.where(at < own, at // HD, own_heads + ((at - own) % rest) // piece)
    return (head[:, None] == jnp.arange(128, dtype=jnp.int32)[None, :]).astype(F32)


def token_pairs():
    return [(p, q) for p in range(3) for q in range(p + 1)]


def token_forward(q, k, v, table):
    q32, k32, v32 = (a.astype(F32) for a in (q, k, v))
    scale = 1.0 / math.sqrt(HD)
    pairs = token_pairs()
    prods = jnp.concatenate([q32[p] * k32[s] for p, s in pairs], axis=0)
    scores = jnp.dot(prods, table, precision=lax.Precision.HIGHEST) * scale
    frames = q.shape[1]
    score = {pair: scores[i * frames : (i + 1) * frames] for i, pair in enumerate(pairs)}
    probs = {}
    for p in range(3):
        row = [score[(p, s)] for s in range(p + 1)]
        top = row[0]
        for r in row[1:]:
            top = jnp.maximum(top, r)
        ex = [jnp.exp(r - top) for r in row]
        tot = sum(ex[1:], ex[0])
        for s in range(p + 1):
            probs[(p, s)] = ex[s] / tot
    low = jnp.concatenate([probs[pair] for pair in pairs], axis=0).astype(BF)
    wide = dot_nt(low, table.astype(BF))
    wide = {pair: wide[i * frames : (i + 1) * frames] for i, pair in enumerate(pairs)}
    mixed = jnp.stack(
        [sum(wide[(p, s)] * v32[s] for s in range(p + 1)) for p in range(3)]
    ).astype(BF)
    return mixed, (probs, low)


def token_backward(q, k, v, kept, grad_mixed, table):
    probs, low = kept
    q32, k32, v32, g32 = (a.astype(F32) for a in (q, k, v, grad_mixed))
    scale = 1.0 / math.sqrt(HD)
    pairs = token_pairs()
    frames = q.shape[1]
    cut = lambda a: {pair: a[i * frames : (i + 1) * frames] for i, pair in enumerate(pairs)}
    prods = jnp.concatenate([g32[p] * v32[s] for p, s in pairs], axis=0)
    gp = cut(jnp.dot(prods, table, precision=lax.Precision.HIGHEST))
    gs = []
    for p in range(3):
        delta = sum(probs[(p, s)] * gp[(p, s)] for s in range(p + 1))
        for s in range(p + 1):
            gs.append((probs[(p, s)] * (gp[(p, s)] - delta)).astype(BF))
    both = dot_nt(jnp.concatenate(gs + [low], axis=0), table.astype(BF))
    gw = cut(both[: 6 * frames])
    pw = cut(both[6 * frames :])
    gq = [sum(gw[(p, s)] * k32[s] for s in range(p + 1)) * scale for p in range(3)]
    gk = [sum(gw[(p, s)] * q32[p] for p in range(s, 3)) * scale for s in range(3)]
    gv = [sum(pw[(p, s)] * g32[p] for p in range(s, 3)) for s in range(3)]
    return [jnp.concatenate(a, axis=0).astype(BF) for a in (gq, gk, gv)]


def token_scatter(left, right, order, n):
    same, cross = d_blocks(right)
    from_right = swap_dp(jnp.concatenate(cross, axis=1), 1)
    from_left = swap_dp(left, 1)
    half = 3 * n // 2
    from_left = jnp.concatenate(
        [from_left[:, :n], from_left[:, n + half :], from_left[:, n : n + half]], axis=1
    )
    lefts = jnp.concatenate([left, from_left], axis=0)
    width = right.shape[1] // lax.axis_size("dp")

    def make(masks):
        mine = jnp.concatenate([same[m] for m in masks], axis=1)
        theirs = jnp.concatenate([from_right[:, m * width : (m + 1) * width] for m in masks], axis=1)
        return dot_tn(lefts, jnp.concatenate([mine, theirs], axis=0)).astype(BF)

    dp = lax.axis_size("dp")
    total = scatter_plane(make, order, (n, 3 * (n // dp), dp // 2))
    return scatter_shards(total, n)


def token_block(frame_out, embed, cotangent, row_valid, params, weights):
    gain_a, gain_b, b_down = (params[i].astype(F32) for i in (0, 3, 7))
    n_attn = params[2].shape[0]
    n_ff = params[6].shape[0]
    w_q, w_k, w_v, w_o, w_u, w_d, b_u = weights
    frames, d = frame_out.shape
    rows = 3 * frames
    table = head_table(w_o.shape[0], n_attn)

    stream = (frame_out[None] + embed.astype(F32)).reshape(rows, d)
    normed_a = normalize(stream, gain_a).astype(BF)
    q, k, v = (dot_nt(normed_a, w).astype(BF).reshape(3, frames, -1) for w in (w_q, w_k, w_v))
    mixed, kept = token_forward(q, k, v, table)
    mixed = mixed.reshape(rows, -1)
    middle = stream + dot_nn(mixed, w_o)
    normed_b = normalize(middle, gain_b).astype(BF)
    hidden_pre = dot_nt(normed_b, w_u) + b_u.astype(F32)
    hidden = activate(hidden_pre).astype(BF)
    token_out = middle + dot_nn(hidden, w_d) + b_down
    output = jnp.where(row_valid, token_out.reshape(3, frames, d), 0.0).astype(BF)

    up_order = plane_bits()
    down_order = up_order[::-1]
    grad_out = jnp.where(row_valid, cotangent.astype(F32), 0.0).reshape(rows, d)
    bias_down_grad = jnp.sum(grad_out, axis=0)
    g_low = grad_out.astype(BF)
    grad_hidden = dot_nt(g_low, w_d)
    grad_pre = jax.vjp(activate, hidden_pre)[1](grad_hidden)[0].astype(BF)
    bias_up_grad = jnp.sum(grad_pre.astype(F32), axis=0)
    down_grad = token_scatter(hidden, g_low, down_order, n_ff)
    up_grad = token_scatter(grad_pre, normed_b, up_order, n_ff)
    grad_normed_b = dot_nn(grad_pre, w_u)
    second_norm = jax.vjp(normalize, middle, gain_b)[1](grad_normed_b)
    grad_middle = grad_out + second_norm[0]
    m_low = grad_middle.astype(BF)
    grad_mixed = dot_nt(m_low, w_o).astype(BF)
    gq, gk, gv = token_backward(q, k, v, kept, grad_mixed.reshape(3, frames, -1), table)
    out_grad = token_scatter(mixed, m_low, down_order, n_attn)
    q_grad = token_scatter(gq, normed_a, up_order, n_attn)
    k_grad = token_scatter(gk, normed_a, up_order, n_attn)
    v_grad = token_scatter(gv, normed_a, down_order, n_attn)
    grad_normed_a = dot_nn(gq, w_q) + dot_nn(gk, w_k) + dot_nn(gv, w_v)
    first_norm = jax.vjp(normalize, stream, gain_a)[1](grad_normed_a)
    grad_stream = grad_middle + first_norm[0]
    return (
        output,
        jnp.sum(grad_stream.reshape(3, frames, d), axis=0),
        (jnp.concatenate([q_grad, k_grad, v_grad], axis=0), out_grad, up_grad, down_grad),
        (first_norm[1], second_norm[1], bias_up_grad, bias_down_grad),
    )


def place_bias(grad, n):
    dp = lax.axis_size("dp")
    z = lax.axis_index("mp")
    k = n // dp
    rest = grad[n:].reshape(2, dp // 2, 3, k)
    slots = by_xor([rest[i & 1, i >> 1] for i in range(dp)])
    shards = [grad[:n]] + [jnp.concatenate([s[r] for s in slots]) for r in range(3)]
    for bit in (1, 2):
        on = (z & bit) != 0
        shards = [jnp.where(on, shards[i ^ bit], shards[i]) for i in range(4)]
    return jnp.stack(shards)


def shards(
    frames,
    codes_embed,
    lengths,
    cotangent,
    *params,
):
    frame_params = params[:8]
    token_params = params[8:]
    parts = lax.axis_size("mp")
    z = lax.axis_index("mp")
    local_frames, d = frames.shape
    segment, is_valid = segments(lengths, local_frames * parts)
    mine_valid = lax.dynamic_slice_in_dim(is_valid, z * local_frames, local_frames, 0)
    row_valid = mine_valid[None, :, None]

    def by_place(rows):
        return jnp.transpose(rows.reshape(local_frames, 3, d), (1, 0, 2))

    up_order = plane_bits()
    down_order = up_order[::-1]
    qkv_t = jnp.transpose(token_params[1], (0, 2, 1))
    qk = gather_weight(qkv_t[:2], up_order)
    vo = gather_weight(jnp.stack([qkv_t[2], token_params[2]]), down_order)
    up = gather_weight(token_params[4].T[None], up_order)
    down = gather_weight(token_params[6][None], down_order)
    b_u = gather_bias(token_params[5])
    weights = (qk[0], qk[1], vo[0], vo[1], up[0], down[0], b_u)

    frame_out, frame_saved = frame_block_forward(frames.astype(F32), frame_params, segment)
    output, grad_frame_out, token_mats, token_vecs = token_block(
        frame_out, by_place(codes_embed), by_place(cotangent), row_valid, token_params, weights
    )
    output = jnp.transpose(output, (1, 0, 2)).reshape(3 * local_frames, d)
    frames_grad, frame_mats, frame_vecs = frame_block_backward(
        grad_frame_out, frame_saved, frame_params, segment
    )

    n_ff = frame_params[4].shape[1]
    devices = lax.axis_size("dp") * parts
    wide = jnp.zeros((parts, n_ff), F32)
    frame_up = lax.dynamic_update_slice_in_dim(wide, frame_vecs[2][None], z, 0)
    token_up = place_bias(token_vecs[2], n_ff)
    packed = jnp.concatenate(
        [
            v.reshape(devices, -1)
            for v in (
                frame_vecs[0],
                frame_vecs[1],
                frame_up,
                frame_vecs[3],
                token_vecs[0],
                token_vecs[1],
                token_up,
                token_vecs[3],
            )
        ],
        axis=1,
    )
    summed = lax.psum_scatter(packed, ("dp", "mp"), scatter_dimension=0, tiled=False)
    vectors = []
    at = 0
    for width in (d, d, n_ff * parts, d) * 2:
        size = width // devices
        vectors.append(summed[at : at + size])
        at += size

    def finish(mats):
        qkv, out, up_, down_ = mats
        width = qkv.shape[1]
        return (jnp.transpose(qkv.reshape(3, -1, width), (0, 2, 1)), out, up_.T, down_)

    f = finish(frame_mats)
    t = finish(token_mats)
    return (
        output,
        frames_grad,
        vectors[0],
        f[0],
        f[1],
        vectors[1],
        f[2],
        vectors[2],
        f[3],
        vectors[3],
        vectors[4],
        t[0],
        t[1],
        vectors[5],
        t[2],
        vectors[6],
        t[3],
        vectors[7],
    )


def solution(mesh):
    rows = P(("dp", "mp"), None)
    block = (
        P(),
        P(None, None, "mp"),
        P("mp", None),
        P(),
        P(None, "mp"),
        P("mp"),
        P("mp", None),
        P(),
    )
    vec = P(("dp", "mp"))
    block_out = (
        vec,
        P(None, "dp", "mp"),
        P("mp", "dp"),
        vec,
        P("dp", "mp"),
        vec,
        P("mp", "dp"),
        vec,
    )
    return jax.shard_map(
        shards,
        mesh=mesh,
        in_specs=(rows, rows, P("dp", None), rows) + block + block,
        out_specs=(rows, rows) + block_out + block_out,
        check_vma=False,
    )
```

time: 1330 us -> 727 us (0.55)
  waiting for transfers between devices: 957 us -> 137 us
  starting transfers between devices: 1.96 us -> 107 us
  local copies, waits for them, and re-layouts: 78.2 us -> 166 us
  other arithmetic: 45.3 us -> 85.6 us
  matrix products: 176 us -> 157 us
    reduce_scatter x16 -> x4, waiting for transfers between devices: 615 us -> 4.99 us  [scatter_rows(): lax.psum_scatter(partial.astype(BF), 'mp', scatter_dimension=0, tiled=True)]
    all_gather x8 -> x4, waiting for transfers between devices: 342 us -> 1.02 us  [gather_rows(): return lax.all_gather(rows, 'mp', axis=0, tiled=True)]
    ppermute x0 -> x84, waiting for transfers between devices: none -> 131 us  [the longest x46 102 us: swap_dp(): return lax.ppermute(value, 'dp', [(i, i ^ bit) for i in range(size)])]
    ppermute x0 -> x84, starting transfers between devices: none -> 106 us  [the longest x28 38.6 us: swap_mp(): return lax.ppermute(value, 'mp', [(i, i ^ mask) for i in range(size)])]
    unnamed x132 -> x527, local copies, waits for them, and re-layouts: 23.1 us -> 87.2 us
    concatenate x0 -> x28, local copies, waits for them, and re-layouts: none -> 32 us  [the longest x4 13.4 us: gather_weight(): return jnp.concatenate([shard_rows, mine, other], axis=1)]
    another operation x12 -> x0, local copies, waits for them, and re-layouts: 24.9 us -> none  [the longest x4 10.8 us: token_backward(): jnp.stack([query_grad.reshape(all_rows, col_width), key_grad.reshape(all_...]
    slice x3 -> x38, local copies, waits for them, and re-layouts: 2.01 us -> 22.3 us  [the longest x10 5.69 us: scatter_plane(): total[:, j * width:(j + 1) * width]]
  transfers between devices with their start and end apart: 24 -> 92, of which waited for: 23 -> 29; matrix products, arithmetic and copies ran while one was open for 8% -> 44% of each run, Pallas kernels for 0% -> 0%
where the time goes in v1:
time: 727 us; the launch traced here: 713 us
  local copies, waits for them, and re-layouts  166 us (23%)
  matrix products  157 us (22%)
  waiting for transfers between devices  137 us (19%)
  starting transfers between devices  107 us (15%)
  other arithmetic  85.6 us (12%)
  blocking collectives  41.7 us (6%)
  between operations  18.8 us (3%)
    ppermute x46, waiting for transfers between devices, swap_dp(): return lax.ppermute(value, 'dp', [(i, i ^ bit) for i in range(size)])  102 us
    unnamed x527, local copies, waits for them, and re-layouts  87.2 us
    dot_general x20, matrix products, dot_tn(): lax.dot_general(a, b, (((0,), (0,)), ((), ())), preferred_element_type=F32)  60.7 us
    dot_general x12, matrix products, dot_nt(): lax.dot_general(a, b, (((1,), (1,)), ((), ())), preferred_element_type=F32)  50.8 us
    unnamed x1, blocking collectives  41.7 us
    ppermute x28, starting transfers between devices, swap_mp(): return lax.ppermute(value, 'mp', [(i, i ^ mask) for i in range(size)])  38.6 us
    ppermute x46, starting transfers between devices, swap_dp(): return lax.ppermute(value, 'dp', [(i, i ^ bit) for i in range(size)])  36.7 us
    dot_general x9, matrix products, dot_nn(): lax.dot_general(a, b, (((1,), (0,)), ((), ())), preferred_element_type=F32)  32.8 us
  transfers between devices with their start and end apart: 92, of which 29 were waited for; matrix products, arithmetic and copies ran while one was open for 44% of the time, Pallas kernels for 0%

profile of v1, /device:TPU:8, one launch (start us, length us, event | category | flops | bytes accessed | tf_op | source)
XLA Modules:
  0.0 713.4 jit_solution(4553227582056572172)
XLA Ops:
  28.0 3.9 copy.232
  55.2 4.4 collective-permute-start.24
  103.8 5.0 collective-permute-done.26
  108.8 4.7 collective-permute-start.28
  151.7 9.8 %collective-permute-done.5 = bf16[2,192,1024]{2,1,0:T(8,128)(2,1)} collective-permute-done((bf16[2,192,1024]{2,1,0:T(8,128)(2,1)}, bf16[2,192,1024]{2,1,0:T(8,128)(2,1)}, u32[]{:S(2)}, u32[]{:S(2)}) %collective-permute-start.5) | collective-permute-done | bytes 786464 | tf_op jit(solution)/shard_map/ppermute | solution.py:46
  176.9 16.6 %collective-permute-done.19 = bf16[1,768,1024]{2,1,0:T(8,128)(2,1)} collective-permute-done((bf16[1,768,1024]{2,1,0:T(8,128)(2,1)}, bf16[1,768,1024]{2,1,0:T(8,128)(2,1)}, u32[]{:S(2)}, u32[]{:S(2)}) %collective-permute-start.19) | collective-permute-done | bytes 1572896 | tf_op jit(solution)/shard_map/ppermute | solution.py:46
  205.8 4.3 multiply_convert_fusion.2
  228.3 4.0 constant_dynamic-update-slice_fusion.54
  232.3 5.0 reduce-scatter.7.cloned.1.call-done
  254.6 7.4 %multiply_convert_fusion = (bf16[384,4096]{1,0:T(8,128)(2,1)}, f32[384,4096]{1,0:T(8,128)}) fusion(f32[4096]{0:T(1024)S(1)} %copy-done.173, bf16[384,1024]{1,0:T(8,128)(2,1)S(1)} %multiply_convert_fusion.4, bf16[1,4096,1024]{2,1,0:T(8,128)(2,1)S(1)} %bitcast.494), kind=kOutput, calls=%fused_computation.20 | convolution fusion | flops 3236954112 | bytes 18628608 | tf_op jit(solution)/shard_map/dot_general | solution.py:23
  262.0 23.1 %convert_reduce_fusion = (f32[4096]{0:T(1024)}, bf16[384,4096]{1,0:T(8,128)(2,1)}) fusion(f32[384,4096]{1,0:T(8,128)} %get-tuple-element.571, bf16[384,1024]{1,0:T(8,128)(2,1)S(1)} %bitcast.489, bf16[1,4096,1024]{2,1,0:T(8,128)(2,1)} %constant_dynamic-update-slice_fusion.54), kind=kOutput, calls=%fused_computation.19 | convolution fusion | flops 3255824384 | bytes 18628608 | tf_op jit(solution)/shard_map/dot_general | solution.py:23
  285.1 5.8 multiply_reduce_fusion.1
  308.8 8.0 %add_add_fusion.3 = bf16[384,1024]{1,0:T(8,128)(2,1)S(1)} fusion(f32[384,1024]{1,0:T(8,128)S(1)} %get-tuple-element.569, bf16[384,4096]{1,0:T(8,128)(2,1)} %get-tuple-element.570, bf16[1,4096,1024]{2,1,0:T(8,128)(2,1)} %constant_dynamic-update-slice_fusion.54, f32[1024]{0:T(1024)S(1)} %copy-done.183), kind=kOutput, calls=%fused_computation.113 | convolution fusion | flops 3222405120 | bytes 13897728 | tf_op jit(solution)/shard_map/dot_general | solution.py:27
  377.6 8.2 %collective-permute-done.46 = bf16[1024,256]{1,0:T(8,128)(2,1)S(1)} collective-permute-done((bf16[1024,256]{1,0:T(8,128)(2,1)S(1)}, bf16[1024,256]{1,0:T(8,128)(2,1)S(1)}, u32[]{:S(2)}, u32[]{:S(2)}) %collective-permute-start.46) | collective-permute-done | bytes 524320 | tf_op jit(solution)/shard_map/ppermute | solution.py:46
  393.0 5.0 convert_reduce_fusion.1
  462.0 6.6 collective-permute-done.39
  481.2 18.2 %convolution_convert_fusion.2 = bf16[4096,256]{1,0:T(8,128)(2,1)} fusion(bf16[384,1536]{1,0:T(8,128)(2,1)S(1)} %get-tuple-element.341, bf16[384,1536]{1,0:T(8,128)(2,1)S(1)} %get-tuple-element.340, bf16[384,1024]{1,0:T(8,128)(2,1)S(1)} %slice.2076, bf16[384,4096]{1,0:T(8,128)(2,1)} %get-tuple-element.577, bf16[384,128]{1,0:T(8,128)(2,1)S(1)} %copy-done.153, ...), kind=kOutput, calls=%fused_computation.26 | convolution fusion | flops 1638400000 | bytes 8781824 | tf_op jit(solution)/shard_map/dot_general | solution.py:31
  506.6 18.0 %convolution_convert_fusion = bf16[4096,256]{1,0:T(8,128)(2,1)} fusion(bf16[384,1536]{1,0:T(8,128)(2,1)S(1)} %get-tuple-element.339, bf16[384,1536]{1,0:T(8,128)(2,1)S(1)} %get-tuple-element.338, bf16[384,1024]{1,0:T(8,128)(2,1)S(1)} %slice.2120, bf16[384,4096]{1,0:T(8,128)(2,1)} %get-tuple-element.570, bf16[384,256]{1,0:T(8,128)(2,1)S(1)} %copy-done.129, ...), kind=kOutput, calls=%fused_computation.22 | convolution fusion | flops 1638006784 | bytes 8781824 | tf_op jit(solution)/shard_map/dot_general | solution.py:31
  559.9 13.7 %collective-permute-done.79 = bf16[4096,256]{1,0:T(8,128)(2,1)} collective-permute-done((bf16[4096,256]{1,0:T(8,128)(2,1)}, bf16[4096,256]{1,0:T(8,128)(2,1)}, u32[]{:S(2)}, u32[]{:S(2)}) %collective-permute-start.79) | collective-permute-done | bytes 2097184 | tf_op jit(solution)/shard_map/ppermute | solution.py:46
  580.0 16.3 %collective-permute-done.36 = bf16[256,256]{1,0:T(8,128)(2,1)S(1)} collective-permute-done((bf16[256,256]{1,0:T(8,128)(2,1)S(1)}, bf16[256,256]{1,0:T(8,128)(2,1)S(1)}, u32[]{:S(2)}, u32[]{:S(2)}) %collective-permute-start.36) | collective-permute-done | bytes 131104 | tf_op jit(solution)/shard_map/ppermute | solution.py:46
  606.7 4.3 collective-permute-start.75
  611.0 17.3 %collective-permute-done.80 = bf16[4096,128]{1,0:T(8,128)(2,1)S(1)} collective-permute-done((bf16[4096,128]{1,0:T(8,128)(2,1)S(1)}, bf16[4096,128]{1,0:T(8,128)(2,1)S(1)}, u32[]{:S(2)}, u32[]{:S(2)}) %collective-permute-start.80) | collective-permute-done | bytes 1048608 | tf_op jit(solution)/shard_map/ppermute | solution.py:46
  640.3 7.9 %collective-permute-done.83 = bf16[2,4,128,128]{3,2,1,0:T(8,128)(2,1)S(1)} collective-permute-done((bf16[2,4,128,128]{3,2,1,0:T(8,128)(2,1)}, bf16[2,4,128,128]{3,2,1,0:T(8,128)(2,1)S(1)}, u32[]{:S(2)}, u32[]{:S(2)}) %collective-permute-start.83) | collective-permute-done | bytes 262176 | tf_op jit(solution)/shard_map/ppermute | solution.py:51
  661.1 41.7 %all-reduce = f32[32,448]{1,0:T(8,128)S(1)} all-reduce(f32[32,448]{1,0:T(8,128)S(1)} %concatenate.415), channel_id=6, replica_groups=mesh['dp'=8,'mp'=4] {'dp','mp'}, use_global_device_ids=true, to_apply=%region_27.28.clone | all-reduce | flops 14336 | bytes 114688
  (1060 shorter events, 435.3 us)
Async XLA Ops:
  7.2 123.9 %all-gather.5.cloned.1.call-start = ((), (), s32[]{:S(2)}) async-start(), calls=%async_computation.4 | async-start | bytes 1310720 | tf_op jit(solution)/shard_map/all_gather | solution.py:35
  14.5 56.1 %collective-permute-start = (bf16[2,32,1024]{2,1,0:T(8,128)(2,1)}, bf16[2,32,1024]{2,1,0:T(8,128)(2,1)S(1)}, u32[]{:S(2)}, u32[]{:S(2)}) collective-permute-start(bf16[2,32,1024]{2,1,0:T(8,128)(2,1)} %constant_dynamic-slice_fusion), channel_id=1, source_target_pairs={{0,1},{1,0},{2,3},{3,2},{4,5},{5,4},{6,7},{7,6},{8,9},{9,8},{10,11... | collective-permute-start | bytes 393224 | tf_op jit(solution)/shard_map/ppermute | solution.py:51
  14.5 59.3 %collective-permute-start.1 = (bf16[2,32,1024]{2,1,0:T(8,128)(2,1)}, bf16[2,32,1024]{2,1,0:T(8,128)(2,1)S(1)}, u32[]{:S(2)}, u32[]{:S(2)}) collective-permute-start(bf16[2,32,1024]{2,1,0:T(8,128)(2,1)} %constant_dynamic-slice_fusion), channel_id=1, source_target_pairs={{0,2},{1,3},{2,0},{3,1},{4,6},{5,7},{6,4},{7,5},{8,10},{9,11},{10,... | collective-permute-start | bytes 393224 | tf_op jit(solution)/shard_map/ppermute | solution.py:51
  17.6 63.9 %collective-permute-start.2 = (bf16[2,32,1024]{2,1,0:T(8,128)(2,1)}, bf16[2,32,1024]{2,1,0:T(8,128)(2,1)}, u32[]{:S(2)}, u32[]{:S(2)}) collective-permute-start(bf16[2,32,1024]{2,1,0:T(8,128)(2,1)} %constant_dynamic-slice_fusion), channel_id=1, source_target_pairs={{1,2},{2,1},{5,6},{6,5},{9,10},{10,9},{13,14},{14,13},{17,18},{18,... | collective-permute-start | bytes 393224 | tf_op jit(solution)/shard_map/ppermute | solution.py:68
  25.2 147.8 %reduce-scatter.5.cloned.1.call-start = ((), (), s32[]{:S(2)}) async-start(), calls=%async_computation.5 | async-start | bytes 1310720 | tf_op jit(solution)/shard_map/reduce_scatter | solution.py:39
  140.0 65.7 %all-gather.7.cloned.1.call-start = ((), (), s32[]{:S(2)}) async-start(), calls=%async_computation.6 | async-start | bytes 1310720 | tf_op jit(solution)/shard_map/all_gather | solution.py:35
  145.8 47.7 %collective-permute-start.19 = (bf16[1,768,1024]{2,1,0:T(8,128)(2,1)}, bf16[1,768,1024]{2,1,0:T(8,128)(2,1)}, u32[]{:S(2)}, u32[]{:S(2)}) collective-permute-start(bf16[1,768,1024]{2,1,0:T(8,128)(2,1)} %pad_maximum_fusion), channel_id=1, source_target_pairs={{0,16},{4,20},{8,24},{12,28},{16,0},{20,4},{24,8},{28,12},{1,17},{... | collective-permute-start | bytes 4718600 | tf_op jit(solution)/shard_map/ppermute | solution.py:46
  147.7 49.5 %collective-permute-start.30 = (bf16[1,768,1024]{2,1,0:T(8,128)(2,1)}, bf16[1,768,1024]{2,1,0:T(8,128)(2,1)}, u32[]{:S(2)}, u32[]{:S(2)}) collective-permute-start(bf16[1,768,1024]{2,1,0:T(8,128)(2,1)} %pad_maximum_fusion.1), channel_id=1, source_target_pairs={{0,8},{4,12},{8,0},{12,4},{16,24},{20,28},{24,16},{28,20},{1,9},{5... | collective-permute-start | bytes 4718600 | tf_op jit(solution)/shard_map/ppermute | solution.py:46
  164.1 52.3 %collective-permute-start.6 = (bf16[2,384,1024]{2,1,0:T(8,128)(2,1)}, bf16[2,384,1024]{2,1,0:T(8,128)(2,1)}, u32[]{:S(2)}, u32[]{:S(2)}) collective-permute-start(bf16[2,384,1024]{2,1,0:T(8,128)(2,1)} %get-tuple-element.420), channel_id=1, source_target_pairs={{0,4},{4,0},{8,12},{12,8},{16,20},{20,16},{24,28},{28,24},{1,5},{5... | collective-permute-start | bytes 4718600 | tf_op jit(solution)/shard_map/ppermute | solution.py:46
  168.8 50.4 %collective-permute-start.13 = (bf16[2,384,1024]{2,1,0:T(8,128)(2,1)}, bf16[2,384,1024]{2,1,0:T(8,128)(2,1)}, u32[]{:S(2)}, u32[]{:S(2)}) collective-permute-start(bf16[2,384,1024]{2,1,0:T(8,128)(2,1)} %get-tuple-element.418), channel_id=1, source_target_pairs={{0,4},{4,0},{8,12},{12,8},{16,20},{20,16},{24,28},{28,24},{1,5},{5... | collective-permute-start | bytes 4718600 | tf_op jit(solution)/shard_map/ppermute | solution.py:46
  176.9 60.4 %reduce-scatter.7.cloned.1.call-start = ((), (), s32[]{:S(2)}) async-start(), calls=%async_computation.7 | async-start | bytes 1310720 | tf_op jit(solution)/shard_map/reduce_scatter | solution.py:39
  213.3 179.7 %all-gather.9.cloned.1.call-start = ((), (), s32[]{:S(2)}) async-start(), calls=%async_computation.8 | async-start | bytes 1310720 | tf_op jit(solution)/shard_map/all_gather | solution.py:35
  307.4 54.6 %collective-permute-start.63 = (bf16[384,1024]{1,0:T(8,128)(2,1)}, bf16[384,1024]{1,0:T(8,128)(2,1)}, u32[]{:S(2)}, u32[]{:S(2)}) collective-permute-start(bf16[384,1024]{1,0:T(8,128)(2,1)} %bitcast.19), channel_id=1, source_target_pairs={{0,4},{4,0},{8,12},{12,8},{16,20},{20,16},{24,28},{28,24},{1,5},{5... | collective-permute-start | bytes 2359304 | tf_op jit(solution)/shard_map/ppermute | solution.py:46
  307.4 170.3 %collective-permute-start.70 = (bf16[384,4096]{1,0:T(8,128)(2,1)}, bf16[384,4096]{1,0:T(8,128)(2,1)}, u32[]{:S(2)}, u32[]{:S(2)}) collective-permute-start(bf16[384,4096]{1,0:T(8,128)(2,1)} %get-tuple-element.577), channel_id=1, source_target_pairs={{0,4},{4,0},{8,12},{12,8},{16,20},{20,16},{24,28},{28,24},{1,5},{5... | collective-permute-start | bytes 9437192 | tf_op jit(solution)/shard_map/ppermute | solution.py:46
  332.8 166.9 %reduce-scatter.9.cloned.1.call-start = ((), (), s32[]{:S(2)}) async-start(), calls=%async_computation.9 | async-start | bytes 1310720 | tf_op jit(solution)/shard_map/reduce_scatter | solution.py:39
  352.8 150.0 %collective-permute-start.77 = (bf16[384,4096]{1,0:T(8,128)(2,1)}, bf16[384,4096]{1,0:T(8,128)(2,1)}, u32[]{:S(2)}, u32[]{:S(2)}) collective-permute-start(bf16[384,4096]{1,0:T(8,128)(2,1)} %get-tuple-element.570), channel_id=1, source_target_pairs={{0,4},{4,0},{8,12},{12,8},{16,20},{20,16},{24,28},{28,24},{1,5},{5... | collective-permute-start | bytes 9437192 | tf_op jit(solution)/shard_map/ppermute | solution.py:46
  401.4 129.3 %all-gather.11.cloned.1.call-start = ((), (), s32[]{:S(2)}) async-start(), calls=%async_computation.10 | async-start | bytes 1310720 | tf_op jit(solution)/shard_map/all_gather | solution.py:35
  471.7 53.7 %collective-permute-start.40 = (bf16[1024,128]{0,1:T(8,128)(2,1)}, bf16[1024,128]{0,1:T(8,128)(2,1)}, u32[]{:S(2)}, u32[]{:S(2)}) collective-permute-start(bf16[1024,128]{0,1:T(8,128)(2,1)} %slice.2825), channel_id=1, source_target_pairs={{0,16},{4,20},{8,24},{12,28},{16,0},{20,4},{24,8},{28,12},{1,17},{... | collective-permute-start | bytes 786440 | tf_op jit(solution)/shard_map/ppermute | solution.py:46
  475.9 51.3 %collective-permute-start.43 = (bf16[1024,128]{1,0:T(8,128)(2,1)}, bf16[1024,128]{1,0:T(8,128)(2,1)}, u32[]{:S(2)}, u32[]{:S(2)}) collective-permute-start(bf16[1024,128]{1,0:T(8,128)(2,1)} %slice.2824), channel_id=1, source_target_pairs={{0,8},{4,12},{8,0},{12,4},{16,24},{20,28},{24,16},{28,20},{1,9},{5... | collective-permute-start | bytes 786440 | tf_op jit(solution)/shard_map/ppermute | solution.py:46
  499.3 46.6 %collective-permute-start.72 = (bf16[4096,256]{1,0:T(8,128)(2,1)}, bf16[4096,256]{1,0:T(8,128)(2,1)}, u32[]{:S(2)}, u32[]{:S(2)}) collective-permute-start(bf16[4096,256]{1,0:T(8,128)(2,1)} %convolution_convert_fusion.2), channel_id=1, source_target_pairs={{0,8},{4,12},{8,0},{12,4},{16,24},{20,28},{24,16},{28,20},{1,9},{5... | collective-permute-start | bytes 6291464 | tf_op jit(solution)/shard_map/ppermute | solution.py:46
  502.8 155.0 %reduce-scatter.11.cloned.1.call-start = ((), (), s32[]{:S(2)}) async-start(), calls=%async_computation.11 | async-start | bytes 1310720 | tf_op jit(solution)/shard_map/reduce_scatter | solution.py:39
  524.7 48.9 %collective-permute-start.79 = (bf16[4096,256]{1,0:T(8,128)(2,1)}, bf16[4096,256]{1,0:T(8,128)(2,1)}, u32[]{:S(2)}, u32[]{:S(2)}) collective-permute-start(bf16[4096,256]{1,0:T(8,128)(2,1)} %convolution_convert_fusion), channel_id=1, source_target_pairs={{0,16},{4,20},{8,24},{12,28},{16,0},{20,4},{24,8},{28,12},{1,17},{... | collective-permute-start | bytes 6291464 | tf_op jit(solution)/shard_map/ppermute | solution.py:46
  544.1 59.1 %collective-permute-start.32 = (bf16[768,512]{0,1:T(8,128)(2,1)S(1)}, bf16[768,512]{0,1:T(8,128)(2,1)S(1)}, u32[]{:S(2)}, u32[]{:S(2)}) collective-permute-start(bf16[768,512]{0,1:T(8,128)(2,1)S(1)} %convolution_convert_fusion.9), channel_id=1, source_target_pairs={{0,4},{4,0},{8,12},{12,8},{16,20},{20,16},{24,28},{28,24},{1,5},{5... | collective-permute-start | bytes 2359304 | tf_op jit(solution)/shard_map/ppermute | solution.py:46
  558.9 47.2 %collective-permute-start.73 = (bf16[4096,128]{1,0:T(8,128)(2,1)S(1)}, bf16[4096,128]{1,0:T(8,128)(2,1)S(1)}, u32[]{:S(2)}, u32[]{:S(2)}) collective-permute-start(bf16[4096,128]{1,0:T(8,128)(2,1)S(1)} %slice.2817), channel_id=1, source_target_pairs={{0,16},{4,20},{8,24},{12,28},{16,0},{20,4},{24,8},{28,12},{1,17},{... | collective-permute-start | bytes 3145736 | tf_op jit(solution)/shard_map/ppermute | solution.py:46
  (278 other events, 2950.2 us)
Sparse Core Ops, SparseCore 0:
  25.3 29.3 all-gather.4
  140.2 24.3 reduce-scatter.4
  177.0 27.4 all-gather.6
  213.4 23.7 reduce-scatter.6
  332.9 28.6 all-gather.8
  401.5 40.6 reduce-scatter.8
  502.9 27.7 all-gather.10
  542.3 24.6 reduce-scatter.10

commit v2 on v1

v2 whole, which is shorter than its diff:
```python
import functools
import math

import jax
import jax.numpy as jnp
from jax import lax
from jax.experimental import pallas as pl
from jax.experimental.pallas import tpu as pltpu
from jax.sharding import PartitionSpec as P

HD = 64
eps = 1e-05
BF = jnp.bfloat16
F32 = jnp.float32


def normalize(stream, gain_vec):
    return stream * lax.rsqrt(jnp.mean(stream * stream, axis=-1, keepdims=True) + eps) * gain_vec


def activate(values):
    return jax.nn.gelu(values, approximate=True)


def dot_nt(a, b):
    return lax.dot_general(a, b, (((1,), (1,)), ((), ())), preferred_element_type=F32)


def dot_nn(a, b):
    return lax.dot_general(a, b, (((1,), (0,)), ((), ())), preferred_element_type=F32)


def dot_tn(a, b):
    return lax.dot_general(a, b, (((0,), (0,)), ((), ())), preferred_element_type=F32)


def gather_rows(rows):
    return lax.all_gather(rows, "mp", axis=0, tiled=True)


def scatter_rows(partial):
    return lax.psum_scatter(
        partial.astype(BF), "mp", scatter_dimension=0, tiled=True
    ).astype(F32)


INNER = 8


def swap_dp(value, bit):
    size = lax.axis_size("dp")
    return lax.ppermute(value, "dp", [(i, i ^ bit) for i in range(size)])


def swap_mp(value, mask):
    size = lax.axis_size("mp")
    return lax.ppermute(value, "mp", [(i, i ^ mask) for i in range(size)])


def my_place():
    return lax.axis_index("dp") % INNER


BITS = [2, 4]
SIDES = [BITS, BITS[::-1]]


def after(value, *marks):
    return lax.optimization_barrier((value,) + tuple(marks))[0]


def all_after(values, *marks):
    return lax.optimization_barrier(tuple(values) + tuple(marks))[: len(values)]


class Gather:
    def __init__(self, piece):
        self.k = piece.shape[1]
        self.piece = piece

    def shards(self, *marks):
        piece = after(self.piece, *marks) if marks else self.piece
        near = swap_mp(piece, 1)
        far = swap_mp(piece, 2)
        inner = lax.ppermute(piece, "mp", [(1, 2), (2, 1)])
        outer = lax.ppermute(far, "mp", [(2, 3), (1, 0)])
        self.held = (near, far, inner, outer)

    def plane_first(self, *marks):
        near, far, inner, outer = all_after(self.held, *marks)
        z = lax.axis_index("mp")
        last = jnp.where((z == 1) | (z == 2), inner, outer)
        half = near.shape[2] // 2
        self.held = []
        for h, side in enumerate(SIDES):
            lanes = slice(h * half, (h + 1) * half)
            whole = jnp.concatenate([near[..., lanes], far[..., lanes], last[..., lanes]], axis=1)
            self.held.append((whole, swap_dp(whole, side[0])))

    def marks(self):
        return [got for _, got in self.held]

    def plane_last(self, *marks):
        held = []
        for (whole, got), side in zip(self.held, SIDES):
            whole, got = all_after((whole, got), *marks)
            low = jnp.concatenate([whole, got], axis=1)
            held.append((low, swap_dp(low, side[1])))
        self.held = held

    def cores(self, *marks):
        held = []
        for low, high in self.held:
            low, high = all_after((low, high), *marks)
            held += [low, high, swap_dp(low, 1), swap_dp(high, 1)]
        self.held = held

    def runs(self):
        out = []
        k = self.k
        for h, side in enumerate(SIDES):
            first, last = side[0] // 2, side[1] // 2
            for core in range(2):
                for high in range(2):
                    for i in range(2):
                        mask = i * first + high * last
                        for r in range(3):
                            out.append(
                                (core, h, 4 * h + 2 * core + high, (3 * i + r) * k, (4 * r + mask) * k, k)
                            )
        return out


def own_rows(shard_rows):
    k = shard_rows.shape[0] // INNER
    return lax.dynamic_slice_in_dim(shard_rows, my_place() * k, k, 0)


def own_cols(shard_cols):
    k = shard_cols.shape[-1] // INNER
    piece = lax.dynamic_slice_in_dim(shard_cols, my_place() * k, k, shard_cols.ndim - 1)
    return jnp.swapaxes(piece, -1, -2)


def by_xor(slots):
    me = my_place()
    for bit in [1] + BITS:
        on = (me & bit) != 0
        slots = [jnp.where(on, slots[i ^ bit], slots[i]) for i in range(len(slots))]
    return slots


def by_xor_mp(slots):
    z = lax.axis_index("mp")
    for bit in (1, 2):
        on = (z & bit) != 0
        slots = [jnp.where(on, slots[i ^ bit], slots[i]) for i in range(len(slots))]
    return slots


def gather_bias(bias):
    n = bias.shape[0]
    row = bias.reshape(1, n)
    rest = jnp.concatenate([swap_mp(row, r) for r in (1, 2, 3)], axis=0).reshape(3, INNER, n // INNER)
    slots = by_xor([rest[:, i] for i in range(INNER)])
    cores = [jnp.stack(slots[c::2], axis=1).reshape(-1) for c in range(2)]
    return jnp.concatenate([bias] + cores)


def place_bias(grad, n):
    rest = grad[n:].reshape(2, 3, INNER // 2, n // INNER)
    slots = by_xor([rest[i & 1, :, i >> 1] for i in range(INNER)])
    return [grad[:n]] + [jnp.concatenate([s[r] for s in slots]) for r in range(3)]


def d_order(rows):
    outer = lax.axis_size("dp") // INNER
    if outer == 1:
        return rows
    view = rows.reshape(rows.shape[0], outer, INNER, -1)
    return jnp.transpose(view, (0, 2, 1, 3)).reshape(rows.shape)


def outer_sum(value, axis):
    size = lax.axis_size("dp")
    if size == INNER:
        return value
    groups = [[o * INNER + i for o in range(size // INNER)] for i in range(INNER)]
    return lax.psum_scatter(
        value, "dp", scatter_dimension=axis, axis_index_groups=groups, tiled=True
    )


def rsq(x):
    return lax.rsqrt(jnp.mean(x * x, axis=-1, keepdims=True) + eps)


def norm_back(grad, x, gain):
    r = rsq(x)
    xr = x * r
    gg = grad * gain
    return r * (gg - xr * jnp.mean(gg * xr, axis=-1, keepdims=True)), grad * xr


def split_dot(x, table):
    hi = x.astype(BF)
    lo = (x - hi.astype(F32)).astype(BF)
    return dot_nn(hi, table) + dot_nn(lo, table)


PAIRS = [(p, s) for p in range(3) for s in range(p + 1)]


def weight_copies(runs, bufs, own_rows, dst, sem, first):
    lead = (slice(None),) * (len(dst.shape) - 2)
    rest = (dst.shape[-2] - own_rows) // 2
    half = dst.shape[-1] // 2
    copies = []
    for i, (core, h, buf, row, at, rows) in enumerate(runs):
        copies.append(
            pltpu.make_async_copy(
                bufs[buf].at[lead + (pl.ds(row, rows),)],
                dst.at[lead + (pl.ds(own_rows + core * rest + at, rows), pl.ds(h * half, half))],
                sem.at[first + i],
            )
        )
    return copies


def attn_weight_copies(runs, own_qkv, own_out, bufs, w, sem):
    n = own_out.shape[0]
    copies = [
        pltpu.make_async_copy(own_qkv, w.at[pl.ds(0, 3), pl.ds(0, n)], sem.at[0]),
        pltpu.make_async_copy(own_out, w.at[3, pl.ds(0, n)], sem.at[1]),
    ]
    return copies + weight_copies(runs, bufs, n, w, sem, 2)


def place_pick(p, frames):
    col = lax.broadcasted_iota(jnp.int32, (frames, 3 * frames), 1)
    row = lax.broadcasted_iota(jnp.int32, (frames, 3 * frames), 0)
    return (col == 3 * row + p).astype(BF)


def place_put(p, frames):
    row = lax.broadcasted_iota(jnp.int32, (3 * frames, frames), 0)
    col = lax.broadcasted_iota(jnp.int32, (3 * frames, frames), 1)
    return (row == 3 * col + p).astype(BF)


def token_attn_kernel(runs, fo, emb, cot, valid, ga, gb, table, own_qkv, own_out, *rest):
    bufs, (s_o, g_o, na_o, q_o, k_o, v_o, mix_o, mid_o, nb_o, pr_o, w, sem) = rest[:8], rest[8:]
    copies = attn_weight_copies(runs, own_qkv, own_out, bufs, w, sem)
    for c in copies:
        c.start()
    frames = fo.shape[0]
    places = [pl.ds(p * frames, frames) for p in range(3)]
    for p in range(3):
        pick = place_pick(p, frames)
        g = dot_nn(pick, cot[...])
        g_o[places[p]] = jnp.where(valid[...] > 0.0, g, 0.0).astype(BF)
        s = fo[...] + dot_nn(pick, emb[...])
        s_o[places[p]] = s
        na_o[places[p]] = (s * rsq(s) * ga[...]).astype(BF)
    for c in copies:
        c.wait()
    for t, out in enumerate((q_o, k_o, v_o)):
        out[...] = dot_nt(na_o[...], w[t]).astype(BF)
    scale = 1.0 / math.sqrt(HD)
    for p in range(3):
        scores = [
            split_dot(q_o[places[p]].astype(F32) * k_o[places[s]].astype(F32), table[...]) * scale
            for s in range(p + 1)
        ]
        top = scores[0]
        for x in scores[1:]:
            top = jnp.maximum(top, x)
        ex = [jnp.exp(x - top) for x in scores]
        total = ex[0]
        for x in ex[1:]:
            total = total + x
        mixed = None
        for s in range(p + 1):
            prob = ex[s] / total
            pr_o[PAIRS.index((p, s))] = prob
            term = dot_nt(prob.astype(BF), table[...]) * v_o[places[s]].astype(F32)
            mixed = term if mixed is None else mixed + term
        mix_o[places[p]] = mixed.astype(BF)
    for p in places:
        mid = s_o[p] + dot_nn(mix_o[p], w[3])
        mid_o[p] = mid
        nb_o[p] = (mid * rsq(mid) * gb[...]).astype(BF)


def token_back_kernel(runs, g, gnb, mid, s_in, ga, gb, q, k, v, mix, pr, table, own_qkv, own_out, *rest):
    bufs, (ml_o, left_o, gf_o, da_o, db_o, w, gm, gx, sem) = rest[:8], rest[8:]
    copies = attn_weight_copies(runs, own_qkv, own_out, bufs, w, sem)
    for c in copies:
        c.start()
    frames, feats = gf_o.shape[0], q.shape[1]
    places = [pl.ds(p * frames, frames) for p in range(3)]
    lanes = [pl.ds(t * feats, feats) for t in range(4)]
    total = None
    for p in places:
        dx, dg = norm_back(gnb[p], mid[p], gb[...])
        grad = g[p].astype(F32) + dx
        gm[p] = grad
        ml_o[p] = grad.astype(BF)
        row = jnp.sum(dg, axis=0, keepdims=True)
        total = row if total is None else total + row
    db_o[...] = total
    left_o[:, lanes[3]] = mix[...]
    for c in copies:
        c.wait()
    gx[...] = dot_nt(ml_o[...], w[3]).astype(BF)
    scale = 1.0 / math.sqrt(HD)
    kg, vg = {}, {}
    for p in range(3):
        gp = [
            split_dot(gx[places[p]].astype(F32) * v[places[s]].astype(F32), table[...])
            for s in range(p + 1)
        ]
        probs = [pr[PAIRS.index((p, s))] for s in range(p + 1)]
        delta = probs[0] * gp[0]
        for s in range(1, p + 1):
            delta = delta + probs[s] * gp[s]
        query = None
        for s in range(p + 1):
            wide = dot_nt((probs[s] * (gp[s] - delta)).astype(BF), table[...])
            term = wide * k[places[s]].astype(F32)
            query = term if query is None else query + term
            key = wide * q[places[p]].astype(F32) * scale
            value = dot_nt(probs[s].astype(BF), table[...]) * gx[places[p]].astype(F32)
            if p == s:
                kg[s], vg[s] = key, value
            else:
                kg[s], vg[s] = kg[s] + key, vg[s] + value
        left_o[places[p], lanes[0]] = (query * scale).astype(BF)
    for s in range(3):
        left_o[places[s], lanes[1]] = kg[s].astype(BF)
        left_o[places[s], lanes[2]] = vg[s].astype(BF)
    gna = dot_nn(left_o[:, lanes[0]], w[0]) + dot_nn(left_o[:, lanes[1]], w[1]) + dot_nn(left_o[:, lanes[2]], w[2])
    total = out = None
    for i, p in enumerate(places):
        dx, dg = norm_back(gna[i * frames : (i + 1) * frames], s_in[p], ga[...])
        grad = gm[p] + dx
        row = jnp.sum(dg, axis=0, keepdims=True)
        total = row if total is None else total + row
        out = grad if out is None else out + grad
    da_o[...] = total
    gf_o[...] = out


GELU_S = math.sqrt(2.0 / math.pi)


def gelu_both(u):
    u2 = u * u
    t = jnp.tanh(GELU_S * (u + 0.044715 * (u2 * u)))
    h = 0.5 * (1.0 + t)
    return u * h, h + 0.5 * u * (1.0 - t * t) * (GELU_S * (1.0 + 3.0 * 0.044715 * u2))


def token_ff_kernel(runs, step, nb, g, mid, valid, bias, bdown, own_up, own_down, *rest):
    bufs, (out_o, gnb_o, left_o, gb_o, wuo, wdo, w, acc, sem) = rest[:8], rest[8:]
    n, frames = own_down.shape[0], valid.shape[0]
    own = [
        pltpu.make_async_copy(own_up, wuo, sem.at[0]),
        pltpu.make_async_copy(own_down, wdo, sem.at[1]),
    ]
    copies = weight_copies(runs, bufs, 0, w, sem, 2)
    for c in own + copies:
        c.start()
    acc[...] = jnp.zeros_like(acc)
    gnb_o[...] = jnp.zeros_like(gnb_o)

    def middle(at, size, pre, back):
        cols = pl.ds(at, size)
        h, dh = gelu_both(pre + bias[:, cols])
        h = h.astype(BF)
        gp = (dh * back).astype(BF)
        left_o[:, cols] = h
        left_o[:, pl.ds(pl.multiple_of(4 * n + at, 128), size)] = gp
        gb_o[:, cols] = jnp.sum(gp.astype(F32), axis=0, keepdims=True)
        return h, gp

    for c in own:
        c.wait()
    own_step = n // 2

    def own_block(j, carry):
        at = pl.multiple_of(j * own_step, own_step)
        cols = pl.ds(at, own_step)
        pre = dot_nn(nb[...], wuo[:, cols])
        back = dot_nt(g[...], wdo[cols, :])
        h, gp = middle(at, own_step, pre, back)
        acc[...] += dot_nn(h, wdo[cols, :])
        gnb_o[...] += dot_nt(gp, wuo[:, cols])
        return carry

    lax.fori_loop(0, n // own_step, own_block, 0)
    for c in copies:
        c.wait()

    def block(j, carry):
        rows = pl.ds(pl.multiple_of(j * step, step), step)
        pre = dot_nt(nb[...], w[0, rows, :])
        back = dot_nt(g[...], w[1, rows, :])
        h, gp = middle(pl.multiple_of(n + j * step, 128), step, pre, back)
        acc[...] += dot_nn(h, w[1, rows, :])
        gnb_o[...] += dot_nn(gp, w[0, rows, :])
        return carry

    lax.fori_loop(0, w.shape[1] // step, block, 0)
    out = None
    for p in range(3):
        rows = pl.ds(p * frames, frames)
        val = jnp.where(valid[...] > 0.0, acc[rows] + mid[rows] + bdown[...], 0.0).astype(BF)
        term = dot_nn(place_put(p, frames), val)
        out = term if out is None else out + term
    out_o[...] = out.astype(BF)


def stage_masks(side):
    first, last = side[0] // 2, side[1] // 2
    return [0, last], [first, first | last]


def right_rows(me, core):
    order = []
    for h, side in enumerate(SIDES):
        keep, give = stage_masks(side)
        for m in keep + give:
            order.append(((me ^ (2 * m + core)), h))
    return order


def lay_right(dst, at, right, me, core, block):
    half = block // 2
    for i, (place, h) in enumerate(right_rows(me, core)):
        dst[pl.ds(at + i * half, half), :] = right[
            pl.ds(pl.multiple_of(place * block + h * half, half), half), :
        ]


def pair_grad_kernel(new, swap, me_ref, lm, lt, rm, rt, *rest):
    outs, (tmp, am, at) = rest[:4], rest[4:]
    j = pl.program_id(0)
    me = me_ref[0]
    block = rm.shape[2] // INNER

    @pl.when(new(j))
    def _():
        for src, dst in ((rm, am), (rt, at)):
            tmp[...] = jnp.transpose(src[0])
            lay_right(dst, 0, tmp, me, 0, block)

    other = lt[...]
    if swap is not None:
        a, b = swap
        other = jnp.concatenate([other[:, :a], other[:, a + b :], other[:, a : a + b]], axis=1)
    total = dot_nn(am[...], lm[...]) + dot_nn(at[...], other)
    size = total.shape[0] // 4
    for i, out in enumerate(outs):
        out[...] = total[i * size : (i + 1) * size].astype(BF)


def frame_grad_kernel(new, me_ref, left, right, *rest):
    outs, (tmp, am) = rest[:5], rest[5:]
    j = pl.program_id(0)
    me = me_ref[0]
    d = right.shape[2]
    block = d // INNER

    @pl.when(new(j))
    def _():
        tmp[...] = jnp.transpose(right[0])
        lay_right(am, 0, tmp, me, 0, block)
        lay_right(am, d // 2, tmp, me, 1, block)

    total = dot_nn(am[...], left[...])
    size = d // 8
    for i in range(4):
        outs[i][...] = total[i * size : (i + 1) * size].astype(BF)
    outs[4][...] = total[d // 2 :].astype(BF)


def lane_swap(x, bit, k, own):
    parts = [x[:, :own]] if own else []
    lanes = 4 * k
    for at in range(own, x.shape[1], lanes):
        group = x[:, at : at + lanes]
        if k % 128 == 0:
            parts += [group[:, (m ^ bit) * k : (m ^ bit) * k + k] for m in range(4)]
        elif bit == 2:
            parts.append(pltpu.roll(group, lanes // 2, 1))
        else:
            lane = lax.broadcasted_iota(jnp.int32, group.shape, 1)
            parts.append(
                jnp.where((lane & k) == 0, pltpu.roll(group, lanes - k, 1), pltpu.roll(group, k, 1))
            )
    return jnp.concatenate(parts, axis=1) if len(parts) > 1 else parts[0]


def add_kernel(k, own_of, *refs):
    ins, outs = refs[:4], refs[4:]
    j = pl.program_id(0)
    for h, side in enumerate(SIDES):
        keep, got, low, high = ins[2 * h], ins[2 * h + 1], outs[2 * h], outs[2 * h + 1]
        half = keep.shape[0] // 2

        def put(value):
            total = keep[...].astype(F32) + value
            low[...] = total[:half]
            high[...] = total[half:].astype(BF)

        def plain():
            put(got[...].astype(F32))

        def moved(own=0):
            put(lane_swap(got[...].astype(F32), side[0] // 2, k, own))

        if k is None:
            plain()
        elif isinstance(own_of, int):
            moved(own_of)
        else:
            pl.when(own_of(j))(plain)
            pl.when(jnp.logical_not(own_of(j)))(moved)


def split_kernel(k, own, *refs):
    ins, (own_o, *sent) = refs[:4], refs[4:]
    for h, side in enumerate(SIDES):
        keep, got = ins[2 * h], ins[2 * h + 1]
        half = keep.shape[0]
        rows = pl.ds(h * half, half)
        total = keep[...] + lane_swap(got[...].astype(F32), side[1] // 2, k, own)
        own_o[rows, :] = total[:, :own]
        for core in range(2):
            for r in range(3):
                at = own + (3 * core + r) * 4 * k
                sent[r][rows, pl.ds(core * 4 * k, 4 * k)] = total[:, at : at + 4 * k].astype(BF)


def ff_final_kernel(me_ref, own, g1, g2, g3, down, up):
    me = me_ref[0]
    n = own.shape[1] // 2
    k = n // INNER
    for m in range(2):
        for i in range(INNER):
            slot = me ^ i
            at = pl.multiple_of(m * n + (slot & 1) * (n // 2) + (slot >> 1) * k, k)
            lanes = pl.ds(at, k)
            total = own[:, m * n + i * k : m * n + (i + 1) * k]
            for g in (g1, g2, g3):
                total = total + g[:, lanes].astype(F32)
            if m == 0:
                down[i * k : (i + 1) * k, :] = jnp.transpose(total)
            else:
                up[:, i * k : (i + 1) * k] = total


def attn_final_kernel(me_ref, own, g1, g2, g3, qkv, out):
    me = me_ref[0]
    n = own.shape[1] // 4
    k = n // INNER
    row = lax.broadcasted_iota(jnp.int32, (n, n), 0)
    col = lax.broadcasted_iota(jnp.int32, (n, n), 1)
    half = n // 2
    inside = row & (half - 1)
    place = (2 * (inside // k) + (row // half)) ^ me
    perm = (col == place * k + (row & (k - 1))).astype(BF)
    for t in range(4):
        lanes = slice(t * n, (t + 1) * n)
        total = own[:, lanes]
        for g in (g1, g2, g3):
            total = total + dot_nn(g[:, lanes], perm)
        if t < 3:
            qkv[t] = total
        else:
            out[...] = jnp.transpose(total)


def frame_core_kernel(*refs):
    keeps, got, outs = refs[:4], refs[4], refs[5:]
    size = outs[0].shape[0]
    for i in range(4):
        outs[i][...] = (
            keeps[i][...].astype(F32) + got[i * size : (i + 1) * size, :].astype(F32)
        ).astype(BF)


def frame_final_kernel(kind, ka, ga, kb, gb, *outs):
    half = ka.shape[0]

    def put(at, size):
        return jnp.concatenate(
            [
                ka[:, at : at + size] + ga[:, at : at + size].astype(F32),
                kb[:, at : at + size] + gb[:, at : at + size].astype(F32),
            ],
            axis=0,
        )

    units = ka.shape[1]
    if kind == "ff":
        n = units // 2
        step = n // 8
        for i in range(8):
            outs[0][i * step : (i + 1) * step, :] = jnp.transpose(put(i * step, step))
        outs[1][...] = put(n, n)
    else:
        n = units // 4
        for t in range(3):
            outs[0][t] = put(t * n, n)
        outs[1][...] = jnp.transpose(put(3 * n, n))


VMEM_LIMIT = 60 * 1024 * 1024


def arr(shape, dtype):
    return jax.ShapeDtypeStruct(shape, dtype)


def cost(flops, ins, outs):
    size = sum(a.size * a.dtype.itemsize for a in ins) + sum(
        math.prod(o.shape) * o.dtype.itemsize for o in outs
    )
    return pl.CostEstimate(flops=flops, bytes_accessed=size, transcendentals=0)


def call(kernel, outs, ins, scratch, any_from, flops, smem=0):
    def space(i):
        return pltpu.SMEM if i < smem else pltpu.VMEM if i < any_from else pl.ANY

    return pl.pallas_call(
        kernel,
        out_shape=outs,
        in_specs=[pl.BlockSpec(memory_space=space(i)) for i in range(len(ins))],
        out_specs=[pl.BlockSpec(memory_space=pltpu.VMEM)] * len(outs),
        scratch_shapes=scratch,
        compiler_params=pltpu.CompilerParams(vmem_limit_bytes=VMEM_LIMIT),
        cost_estimate=cost(flops, ins, outs),
    )(*ins)


def token_attn(fo, emb, cot, valid, ga, gb, table, own_qkv, own_out, gather, bufs):
    frames, d = fo.shape
    rows, feats = 3 * frames, table.shape[0]
    runs = gather.runs()
    outs = (
        [arr((rows, d), F32), arr((rows, d), BF), arr((rows, d), BF)]
        + [arr((rows, feats), BF)] * 4
        + [arr((rows, d), F32), arr((rows, d), BF), arr((len(PAIRS), frames, table.shape[1]), F32)]
    )
    return call(
        functools.partial(token_attn_kernel, runs),
        outs,
        [fo, emb, cot, valid, ga, gb, table, own_qkv, own_out, *bufs],
        [pltpu.VMEM((4, feats, d), BF), pltpu.SemaphoreType.DMA((2 + len(runs),))],
        7,
        8 * rows * feats * d,
    )


def token_back(g, gnb, mid, s, ga, gb, q, k, v, mix, pr, table, own_qkv, own_out, gather, bufs):
    rows, d = s.shape
    frames, feats = rows // 3, table.shape[0]
    runs = gather.runs()
    outs = [
        arr((rows, d), BF),
        arr((rows, 4 * feats), BF),
        arr((frames, d), F32),
        arr((1, d), F32),
        arr((1, d), F32),
    ]
    return call(
        functools.partial(token_back_kernel, runs),
        outs,
        [g, gnb, mid, s, ga, gb, q, k, v, mix, pr, table, own_qkv, own_out, *bufs],
        [
            pltpu.VMEM((4, feats, d), BF),
            pltpu.VMEM((rows, d), F32),
            pltpu.VMEM((rows, feats), BF),
            pltpu.SemaphoreType.DMA((2 + len(runs),)),
        ],
        12,
        8 * rows * feats * d,
    )


def token_ff(nb, g, mid, valid, bias, bdown, own_up, own_down, gather, bufs):
    rows, d = nb.shape
    n = own_down.shape[0]
    runs = gather.runs()
    outs = [
        arr((rows, d), BF),
        arr((rows, d), F32),
        arr((rows, 8 * n), BF),
        arr((1, 4 * n), F32),
    ]
    return call(
        functools.partial(token_ff_kernel, runs, 384),
        outs,
        [nb, g, mid, valid, bias, bdown, own_up, own_down, *bufs],
        [
            pltpu.VMEM((d, n), BF),
            pltpu.VMEM((n, d), BF),
            pltpu.VMEM((2, 3 * n, d), BF),
            pltpu.VMEM((rows, d), F32),
            pltpu.SemaphoreType.DMA((2 + len(runs),)),
        ],
        6,
        32 * rows * n * d,
    )


def smem_spec():
    return pl.BlockSpec(memory_space=pltpu.SMEM)


def pair_grad(me, left, left_other, rights, rights_other, step, pick, partner, new, swap):
    rows, units = left.shape
    d = rights.shape[2]
    outs = [arr((d // 8, units), BF)] * 4
    return pl.pallas_call(
        functools.partial(pair_grad_kernel, new, swap),
        grid=(units // step,),
        in_specs=[
            smem_spec(),
            pl.BlockSpec((rows, step), lambda j: (0, j)),
            pl.BlockSpec((rows, step), lambda j: (0, partner(j))),
            pl.BlockSpec((1, rows, d), lambda j: (pick(j), 0, 0)),
            pl.BlockSpec((1, rows, d), lambda j: (pick(j), 0, 0)),
        ],
        out_specs=[pl.BlockSpec((d // 8, step), lambda j: (0, j))] * 4,
        out_shape=outs,
        scratch_shapes=[pltpu.VMEM((d, rows), BF)] + [pltpu.VMEM((d // 2, rows), BF)] * 2,
        compiler_params=pltpu.CompilerParams(vmem_limit_bytes=VMEM_LIMIT),
        cost_estimate=cost(2 * rows * units * d, [left, left_other, rights, rights_other], outs),
    )(me, left, left_other, rights, rights_other)


def ff_pair_grad(me, left, other, rights, rights_other, n):
    step = n // 2

    def partner(j):
        b = j % 8
        return j - b + jnp.where(b < 2, b, jnp.where(b < 5, b + 3, b - 3))

    return pair_grad(
        me, left, other, rights, rights_other, step,
        lambda j: j // 8, partner, lambda j: j % 8 == 0, None,
    )


def attn_pair_grad(me, left, other, rights, rights_other, n):
    return pair_grad(
        me, left, other, rights, rights_other, 4 * n,
        lambda j: j // 3, lambda j: j, lambda j: (j == 0) | (j == 3), (n, 3 * n // 2),
    )


def frame_grad(me, left, rights, split):
    rows, units = left.shape
    d = rights.shape[2]
    step = units // 4 if split * 4 % units else units // 4
    at = split // step
    outs = [arr((d // 8, units), BF)] * 4 + [arr((d // 2, units), BF)]
    return pl.pallas_call(
        functools.partial(frame_grad_kernel, lambda j: (j == 0) | (j == at)),
        grid=(4,),
        in_specs=[
            smem_spec(),
            pl.BlockSpec((rows, step), lambda j: (0, j)),
            pl.BlockSpec((1, rows, d), lambda j: (jnp.where(j < at, 0, 1), 0, 0)),
        ],
        out_specs=[pl.BlockSpec((d // 8, step), lambda j: (0, j))] * 4
        + [pl.BlockSpec((d // 2, step), lambda j: (0, j))],
        out_shape=outs,
        scratch_shapes=[pltpu.VMEM((d, rows), BF)] * 2,
        compiler_params=pltpu.CompilerParams(vmem_limit_bytes=VMEM_LIMIT),
        cost_estimate=cost(2 * rows * units * d, [left, rights], outs),
    )(me, left, rights)


def add_halves(keep_a, got_a, keep_b, got_b, step, k, own_of):
    rows, units = keep_a.shape
    outs = [arr((rows // 2, units), F32), arr((rows // 2, units), BF)] * 2
    ins = [keep_a, got_a, keep_b, got_b]
    return pl.pallas_call(
        functools.partial(add_kernel, k, own_of),
        grid=(units // step,),
        in_specs=[pl.BlockSpec((rows, step), lambda j: (0, j))] * 4,
        out_specs=[pl.BlockSpec((rows // 2, step), lambda j: (0, j))] * 4,
        out_shape=outs,
        compiler_params=pltpu.CompilerParams(vmem_limit_bytes=VMEM_LIMIT),
        cost_estimate=cost(0, ins, outs),
    )(*ins)


def split_shards(keep_a, got_a, keep_b, got_b, n, k):
    rows, units = keep_a.shape
    count = units // (4 * n)
    outs = [arr((2 * rows, count * n), F32)] + [arr((2 * rows, count * n), BF)] * 3
    ins = [keep_a, got_a, keep_b, got_b]
    return pl.pallas_call(
        functools.partial(split_kernel, k, n),
        grid=(count,),
        in_specs=[pl.BlockSpec((rows, 4 * n), lambda j: (0, j))] * 4,
        out_specs=[pl.BlockSpec((2 * rows, n), lambda j: (0, j))] * 4,
        out_shape=outs,
        compiler_params=pltpu.CompilerParams(vmem_limit_bytes=VMEM_LIMIT),
        cost_estimate=cost(0, ins, outs),
    )(*ins)


class TokenGrads:
    def __init__(self, quarters, n, k, step, own_of):
        self.n, self.k, self.step, self.own_of = n, k, step, own_of
        keep_a, give_a, keep_b, give_b = quarters
        self.hold = keep_a
        self.held = (keep_a, swap_dp(give_a, SIDES[0][0]), keep_b, swap_dp(give_b, SIDES[1][0]))

    def middle(self, *marks):
        keep_a, give_a, keep_b, give_b = add_halves(
            *all_after(self.held, *marks), self.step, self.k, self.own_of
        )
        self.hold = keep_a
        self.held = (keep_a, swap_dp(give_a, SIDES[0][1]), keep_b, swap_dp(give_b, SIDES[1][1]))

    def shards(self, *marks):
        own, *sent = split_shards(*all_after(self.held, *marks), self.n, self.k)
        self.own = own
        self.held = tuple(swap_mp(sent[r - 1], r) for r in (1, 2, 3))
        return own

    def last(self, kernel, outs, me, *marks):
        ins = [me, self.own, *all_after(self.held, *marks)]
        return call(kernel, outs, ins, [], len(ins), 0, smem=1)


class FrameGrads:
    def __init__(self, parts):
        self.hold = parts[0]
        self.held = tuple(parts[:4]) + (swap_dp(parts[4], 1),)

    def first(self, *marks):
        ins = all_after(self.held, *marks)
        rows, units = ins[0].shape
        step = units // 4
        outs = [arr((rows, units), BF)] * 4
        keep_a, give_a, keep_b, give_b = pl.pallas_call(
            frame_core_kernel,
            grid=(4,),
            in_specs=[pl.BlockSpec((rows, step), lambda j: (0, j))] * 4
            + [pl.BlockSpec((4 * rows, step), lambda j: (0, j))],
            out_specs=[pl.BlockSpec((rows, step), lambda j: (0, j))] * 4,
            out_shape=outs,
            compiler_params=pltpu.CompilerParams(vmem_limit_bytes=VMEM_LIMIT),
            cost_estimate=cost(0, ins, outs),
        )(*ins)
        self.hold = keep_a
        self.held = (keep_a, swap_dp(give_a, SIDES[0][0]), keep_b, swap_dp(give_b, SIDES[1][0]))

    def middle(self, *marks):
        ins = all_after(self.held, *marks)
        keep_a, give_a, keep_b, give_b = add_halves(*ins, ins[0].shape[1] // 2, None, None)
        self.hold = keep_a
        self.held = (keep_a, swap_dp(give_a, SIDES[0][1]), keep_b, swap_dp(give_b, SIDES[1][1]))

    def last(self, kind, outs, *marks):
        ins = all_after(self.held, *marks)
        return call(functools.partial(frame_final_kernel, kind), outs, list(ins), [], 4, 0)


def segments(lengths, whole_rows):
    count = lengths.shape[1]
    order = jnp.arange(count, dtype=jnp.int32)
    item_ends = jnp.sum(
        jnp.where(order[None, :] <= order[:, None], lengths[0][None, :], 0), axis=1, dtype=jnp.int32
    )
    positions = jnp.arange(whole_rows, dtype=jnp.int32)
    segment = jnp.sum(
        (positions[:, None] >= item_ends[None, :]).astype(jnp.int32), axis=1, dtype=jnp.int32
    )
    is_valid = positions < jnp.sum(lengths[0], dtype=jnp.int32)
    segment = jnp.where(is_valid, segment, positions + count)
    return (segment, is_valid)


def frame_allowed(segment):
    positions = jnp.arange(segment.shape[0], dtype=jnp.int32)
    return (positions[None, :] <= positions[:, None]) & (segment[None, :] == segment[:, None])


def split_heads(rows):
    return rows.reshape(rows.shape[0], rows.shape[1] // HD, HD)


def frame_forward(qkv_rows, segment):
    queries, key_rows, value_rows = (split_heads(qkv_rows[t]) for t in range(3))
    raw_scores = jnp.einsum("qhe,khe->hqk", queries, key_rows, preferred_element_type=F32) * (
        1.0 / math.sqrt(HD)
    )
    scores = jnp.where(frame_allowed(segment)[None], raw_scores, -1e30)
    top_score = jnp.max(scores, axis=-1, keepdims=True)
    exp_scores = jnp.exp(scores - top_score)
    exp_total = jnp.sum(exp_scores, axis=-1, keepdims=True)
    attn_probs = (exp_scores / exp_total).astype(BF)
    mixed = jnp.einsum("hqk,khe->qhe", attn_probs, value_rows, preferred_element_type=F32)
    log_total = top_score[:, :, 0] + jnp.log(exp_total[:, :, 0])
    return (mixed.astype(BF).reshape(qkv_rows.shape[1], -1), log_total)


def frame_backward(qkv_rows, log_total, grad_mixed, segment):
    queries, key_rows, value_rows = (split_heads(qkv_rows[t]) for t in range(3))
    grad_heads = split_heads(grad_mixed)
    scale = 1.0 / math.sqrt(HD)
    raw_scores = jnp.einsum("qhe,khe->hqk", queries, key_rows, preferred_element_type=F32) * scale
    scores = jnp.where(frame_allowed(segment)[None], raw_scores, -1e30)
    attn_probs = jnp.exp(scores - log_total[:, :, None])
    value_grad = jnp.einsum(
        "hqk,qhe->khe", attn_probs.astype(BF), grad_heads, preferred_element_type=F32
    )
    grad_probs = jnp.einsum("qhe,khe->hqk", grad_heads, value_rows, preferred_element_type=F32)
    row_delta = jnp.sum(attn_probs * grad_probs, axis=-1, keepdims=True)
    grad_scores = (attn_probs * (grad_probs - row_delta)).astype(BF)
    query_grad = jnp.einsum("hqk,khe->qhe", grad_scores, key_rows, preferred_element_type=F32) * scale
    key_grad = jnp.einsum("hqk,qhe->khe", grad_scores, queries, preferred_element_type=F32) * scale
    rows = qkv_rows.shape[1]
    return [g.reshape(rows, -1).astype(BF) for g in (query_grad, key_grad, value_grad)]


def head_table(features, own):
    at = jnp.arange(features, dtype=jnp.int32)
    own_heads = own // HD
    rest = (features - own) // 2
    piece = rest // (features // HD - own_heads)
    head = jnp.where(at < own, at // HD, own_heads + ((at - own) % rest) // piece)
    return (head[:, None] == jnp.arange(128, dtype=jnp.int32)[None, :]).astype(BF)


def shards(frames, codes_embed, lengths, cotangent, *params):
    gain_a, w_qkv, w_out, gain_b, w_up, b_up, w_down, b_down = params[:8]
    t_gain_a, t_qkv, t_out, t_gain_b, t_up, t_bup, t_down, t_bdown = params[8:]
    dp, parts = lax.axis_size("dp"), lax.axis_size("mp")
    z = lax.axis_index("mp")
    me = my_place().astype(jnp.int32).reshape(1)
    local, d = frames.shape
    n_attn, n_ff = w_out.shape[0], w_down.shape[0]
    block = d // INNER
    segment, is_valid = segments(lengths, local * parts)
    valid = lax.dynamic_slice_in_dim(is_valid, z * local, local, 0).astype(F32)[:, None]

    stream = frames.astype(F32)
    gain_a32, gain_b32 = gain_a.astype(F32), gain_b.astype(F32)
    normed_a = normalize(stream, gain_a32).astype(BF)
    gathered_a = gather_rows(normed_a)

    attn_w = Gather(jnp.concatenate([own_cols(t_qkv), own_rows(t_out)[None]], axis=0))
    ff_w = Gather(jnp.stack([own_cols(t_up), own_rows(t_down)]))
    attn_w.shards()
    gathered_a = after(gathered_a, *attn_w.held)

    qkv_rows = jnp.einsum("rd,tde->tre", gathered_a, w_qkv, preferred_element_type=F32).astype(BF)
    mixed_rows, log_total = frame_forward(qkv_rows, segment)
    part_a = dot_nn(mixed_rows, w_out).astype(BF)
    branch_a = scatter_rows(part_a)

    ff_w.shards(part_a)
    attn_w.plane_first(part_a)
    middle = stream + after(branch_a, *ff_w.held, *attn_w.marks())

    normed_b = normalize(middle, gain_b32).astype(BF)
    gathered_b = gather_rows(normed_b)

    attn_w.plane_last(normed_b)
    ff_w.plane_first(normed_b)
    gathered_b = after(gathered_b, *attn_w.marks(), *ff_w.marks())

    hidden_pre = dot_nn(gathered_b, w_up) + b_up.astype(F32)
    hidden = activate(hidden_pre).astype(BF)
    part_b = dot_nn(hidden, w_down).astype(BF)
    branch_b = scatter_rows(part_b)

    attn_w.cores(part_b)
    ff_w.plane_last(part_b)
    frame_out = middle + after(branch_b, *attn_w.held, *ff_w.marks()) + b_down.astype(F32)

    t_bias = gather_bias(t_bup).astype(F32)[None]
    own_qkv = jnp.transpose(t_qkv, (0, 2, 1))
    table = head_table(n_attn * parts, n_attn)
    tga, tgb = t_gain_a.astype(F32)[None], t_gain_b.astype(F32)[None]

    attn_bufs = attn_w.held
    t_stream, g_low, t_na, q, k, v, mixed, t_middle, t_nb, probs = token_attn(
        frame_out, codes_embed, cotangent, valid, tga, tgb, table, own_qkv, t_out, attn_w, attn_bufs
    )
    ff_w.cores()
    output, t_gnb, t_left, t_gbup = token_ff(
        t_nb, g_low, t_middle, valid, t_bias, t_bdown.astype(F32)[None], t_up, t_down, ff_w, ff_w.held
    )
    rights = jnp.stack([d_order(g_low), d_order(t_nb)])
    rights_other = swap_dp(rights, 1)
    left_other = swap_dp(t_left, 1)
    m_low, a_left, grad_frame, t_da, t_db = token_back(
        g_low, t_gnb, t_middle, t_stream, tga, tgb, q, k, v, mixed, probs, table, own_qkv, t_out, attn_w, attn_bufs
    )
    t_dbd = jnp.sum(g_low.astype(F32), axis=0)

    grad_low = grad_frame.astype(BF)
    gathered_down = gather_rows(grad_low)

    ff_s = TokenGrads(
        ff_pair_grad(me, after(t_left, grad_low), left_other, rights, rights_other, n_ff),
        n_ff, n_ff // INNER, n_ff, lambda j: j % 4 == 0,
    )
    a_left = after(a_left, grad_low)
    a_rights = jnp.stack([d_order(t_na), d_order(m_low)])
    a_rights_other = swap_dp(a_rights, 1)
    a_other = swap_dp(a_left, 1)

    gathered_down = after(gathered_down, ff_s.hold)
    grad_hidden = dot_nt(gathered_down, w_down)
    grad_pre = jax.vjp(activate, hidden_pre)[1](grad_hidden)[0].astype(BF)
    part_c = dot_nt(grad_pre, w_up).astype(BF)
    grad_nb = scatter_rows(part_c)

    attn_s = TokenGrads(
        attn_pair_grad(me, after(a_left, part_c), a_other, a_rights, a_rights_other, n_attn),
        n_attn, n_attn // INNER, 4 * n_attn, n_attn,
    )
    f_left = jnp.concatenate([hidden, grad_pre], axis=1)
    f_ff = FrameGrads(
        frame_grad(me, after(f_left, part_c), jnp.stack([d_order(gathered_down), d_order(gathered_b)]), n_ff)
    )

    grad_nb = after(grad_nb, attn_s.hold, f_ff.hold)
    second = jax.vjp(normalize, middle, gain_b32)[1](grad_nb)
    grad_middle = grad_frame + second[0]
    mid_low = grad_middle.astype(BF)
    gathered_mid = gather_rows(mid_low)

    ff_s.middle(mid_low)
    f_ff.first(mid_low)

    grad_mixed = dot_nt(after(gathered_mid, ff_s.hold, f_ff.hold), w_out).astype(BF)
    grad_qkv = jnp.concatenate(frame_backward(qkv_rows, log_total, grad_mixed, segment), axis=1)
    w_all = jnp.concatenate([w_qkv[0], w_qkv[1], w_qkv[2]], axis=1)
    part_d32 = dot_nt(grad_qkv, w_all)
    part_d = part_d32.astype(BF)
    grad_na = scatter_rows(part_d)
    f_da = jnp.sum(part_d32 * gathered_a.astype(F32), axis=0) / gain_a32

    ff_s.shards(part_d)
    attn_s.middle(part_d)
    f_ff.middle(part_d)
    f_attn = FrameGrads(
        frame_grad(
            me,
            after(jnp.concatenate([grad_qkv, mixed_rows], axis=1), part_d),
            jnp.stack([d_order(gathered_a), d_order(gathered_mid)]),
            3 * n_attn,
        )
    )

    wide = lax.dynamic_update_slice_in_dim(
        jnp.zeros((parts, n_ff), F32), jnp.sum(grad_pre.astype(F32), axis=0)[None], z, 0
    )
    t_wide = jnp.stack(by_xor_mp(place_bias(t_gbup[0], n_ff)))

    def by_owner(full):
        return jnp.transpose(full.reshape(dp, parts, -1), (1, 0, 2)).reshape(parts, -1)

    vec = jnp.concatenate(
        [
            jnp.stack([f_da, second[1], jnp.sum(grad_frame, axis=0), t_da[0], t_db[0], t_dbd]),
            by_owner(wide),
            by_owner(t_wide),
        ],
        axis=0,
    )
    vec = d_order(vec)
    vec = jnp.concatenate(by_xor([vec[:, i * block : (i + 1) * block] for i in range(INNER)]), axis=1)
    for bit in (4, 2, 1):
        half = vec.shape[1] // 2
        vec = vec[:, :half] + swap_dp(vec[:, half:], bit)
    vec = outer_sum(vec, 1)
    width = vec.shape[1]
    quarter = width // parts
    rows = by_xor_mp(
        [
            jnp.concatenate(
                [vec[:6, i * quarter : (i + 1) * quarter].reshape(-1), vec[6 + i], vec[6 + parts + i]]
            )
            for i in range(parts)
        ]
    )
    mine = rows[0] + sum(swap_mp(rows[r], r) for r in (1, 2, 3))
    vectors = [mine[i * quarter : (i + 1) * quarter] for i in range(6)]
    f_bup, t_bup_grad = mine[6 * quarter : 6 * quarter + width], mine[6 * quarter + width :]

    ff_outs = [arr((n_ff, block), F32), arr((block, n_ff), F32)]
    attn_outs = [arr((3, block, n_attn), F32), arr((n_attn, block), F32)]
    attn_s.shards()
    f_attn.first()
    grad_na = after(grad_na, attn_s.hold, f_ff.hold, f_attn.hold)
    first = jax.vjp(normalize, stream, gain_a32)[1](grad_na)
    frames_grad = grad_middle + first[0]
    f_attn.middle()
    t_down_grad, t_up_grad = ff_s.last(ff_final_kernel, ff_outs, me)
    f_down_grad, f_up_grad = f_ff.last("ff", ff_outs)
    t_qkv_grad, t_out_grad = attn_s.last(attn_final_kernel, attn_outs, me)
    f_qkv_grad, f_out_grad = f_attn.last("attn", attn_outs)

    def owned(qkv_grad, out_grad, up_grad, down_grad):
        return (
            outer_sum(qkv_grad, 1),
            outer_sum(out_grad, 1),
            outer_sum(up_grad, 0),
            outer_sum(down_grad, 1),
        )

    f = owned(f_qkv_grad, f_out_grad, f_up_grad, f_down_grad)
    t = owned(t_qkv_grad, t_out_grad, t_up_grad, t_down_grad)
    return (
        output,
        frames_grad,
        vectors[0],
        f[0],
        f[1],
        vectors[1],
        f[2],
        f_bup,
        f[3],
        vectors[2],
        vectors[3],
        t[0],
        t[1],
        vectors[4],
        t[2],
        t_bup_grad,
        t[3],
        vectors[5],
    )


def solution(mesh):
    rows = P(("dp", "mp"), None)
    block = (
        P(),
        P(None, None, "mp"),
        P("mp", None),
        P(),
        P(None, "mp"),
        P("mp"),
        P("mp", None),
        P(),
    )
    vec = P(("dp", "mp"))
    block_out = (
        vec,
        P(None, "dp", "mp"),
        P("mp", "dp"),
        vec,
        P("dp", "mp"),
        vec,
        P("mp", "dp"),
        vec,
    )
    return jax.shard_map(
        shards,
        mesh=mesh,
        in_specs=(rows, rows, P("dp", None), rows) + block + block,
        out_specs=(rows, rows) + block_out + block_out,
        check_vma=False,
    )
```

time: 727 us -> 539 us (0.74)
  Pallas kernels: 0 us -> 143 us
  local copies, waits for them, and re-layouts: 166 us -> 33.9 us
  matrix products: 157 us -> 28.9 us
  waiting for transfers between devices: 137 us -> 196 us
  other arithmetic: 85.6 us -> 37.8 us
  blocking collectives: 41.7 us -> 0 us
  starting transfers between devices: 107 us -> 74 us
    pallas_call x0 -> x19, Pallas kernels: none -> 143 us  [the longest x7 67.2 us: call(): pl.pallas_call(kernel, out_shape=outs, in_specs=[pl.BlockSpec(memory_spac...]
    ppermute x28 -> x16, waiting for transfers between devices: 25.6 us -> 106 us  [swap_mp(): return lax.ppermute(value, 'mp', [(i, i ^ mask) for i in range(size)])]
    unnamed x527 -> x136, local copies, waits for them, and re-layouts: 87.2 us -> 13.7 us
    dot_general x23 -> x1, matrix products: 66.8 us -> 2.75 us  [shards(): jnp.einsum('rd,tde->tre', gathered_a, w_qkv, preferred_element_type=F32)]
    unnamed x1 -> x0, blocking collectives: 41.7 us -> none
    dot_general x12 -> x4, matrix products: 50.8 us -> 11.1 us  [dot_nt(): lax.dot_general(a, b, (((1,), (1,)), ((), ())), preferred_element_type=F32)]
    concatenate x27 -> x8, local copies, waits for them, and re-layouts: 30.7 us -> 5.31 us  [the longest x4 5.09 us: plane_last(): low = jnp.concatenate([whole, got], axis=1)]
    ppermute x46 -> x41, waiting for transfers between devices: 102 us -> 77.1 us  [swap_dp(): return lax.ppermute(value, 'dp', [(i, i ^ bit) for i in range(size)])]
  transfers between devices with their start and end apart: 92 -> 69, of which waited for: 29 -> 26; matrix products, arithmetic and copies ran while one was open for 44% -> 13% of each run, Pallas kernels for 0% -> 21%
where the time goes in v2:
time: 539 us; the launch traced here: 529 us
  waiting for transfers between devices  196 us (36%)
  Pallas kernels  143 us (27%)
  starting transfers between devices  74 us (14%)
  other arithmetic  37.8 us (7%)
  local copies, waits for them, and re-layouts  33.9 us (6%)
  matrix products  28.9 us (5%)
  between operations  15.8 us (3%)
    ppermute x16, waiting for transfers between devices, swap_mp(): return lax.ppermute(value, 'mp', [(i, i ^ mask) for i in range(size)])  106 us
    ppermute x41, waiting for transfers between devices, swap_dp(): return lax.ppermute(value, 'dp', [(i, i ^ bit) for i in range(size)])  77.1 us
    pallas_call x7, Pallas kernels, call(): pl.pallas_call(kernel, out_shape=outs, in_specs=[pl.BlockSpec(memory_spac...  67.2 us
    ppermute x41, starting transfers between devices, swap_dp(): return lax.ppermute(value, 'dp', [(i, i ^ bit) for i in range(size)])  30.5 us
    pallas_call x2, Pallas kernels, pair_grad(): pl.pallas_call(functools.partial(pair_grad_kernel, new, swap), grid=(unit...  29 us
    ppermute x16, starting transfers between devices, swap_mp(): return lax.ppermute(value, 'mp', [(i, i ^ mask) for i in range(size)])  28.5 us
    pallas_call x4, Pallas kernels, add_halves(): pl.pallas_call(functools.partial(add_kernel, k, own_of), grid=(units // s...  17.4 us
    unnamed x136, local copies, waits for them, and re-layouts  13.7 us
  transfers between devices with their start and end apart: 69, of which 26 were waited for; matrix products, arithmetic and copies ran while one was open for 13% of the time, Pallas kernels for 21%

profile of v2, /device:TPU:8, one launch (start us, length us, event | category | flops | bytes accessed | tf_op | source)
XLA Modules:
  0.0 529.3 jit_solution(16615680283758714183)
XLA Ops:
  21.8 18.4 %collective-permute-done.1 = bf16[4,32,1024]{2,1,0:T(8,128)(2,1)S(1)} collective-permute-done((bf16[4,32,1024]{2,1,0:T(8,128)(2,1)S(1)}, bf16[4,32,1024]{2,1,0:T(8,128)(2,1)S(1)}, u32[]{:S(2)}, u32[]{:S(2)}) %collective-permute-start.1) | collective-permute-done | bytes 262176 | tf_op jit(solution)/shard_map/ppermute | solution.py:57
  45.1 6.6 %collective-permute-done.2 = bf16[4,32,1024]{2,1,0:T(8,128)(2,1)S(1)} collective-permute-done((bf16[4,32,1024]{2,1,0:T(8,128)(2,1)S(1)}, bf16[4,32,1024]{2,1,0:T(8,128)(2,1)S(1)}, u32[]{:S(2)}, u32[]{:S(2)}) %collective-permute-start.2) | collective-permute-done | bytes 262176 | tf_op jit(solution)/shard_map/ppermute | solution.py:85
  70.1 38.1 %collective-permute-done.5 = bf16[2,128,1024]{2,1,0:T(8,128)(2,1)} collective-permute-done((bf16[2,128,1024]{2,1,0:T(8,128)(2,1)}, bf16[2,128,1024]{2,1,0:T(8,128)(2,1)}, u32[]{:S(2)}, u32[]{:S(2)}) %collective-permute-start.5) | collective-permute-done | bytes 524320 | tf_op jit(solution)/shard_map/ppermute | solution.py:57
  108.3 5.3 collective-permute-start.7
  135.9 10.7 %collective-permute-done.10.rest_1_ = bf16[4,192,512]{2,1,0:T(8,128)(2,1)S(1)} collective-permute-done((bf16[4,192,512]{2,1,0:T(8,128)(2,1)S(1)}, bf16[4,192,512]{2,1,0:T(8,128)(2,1)S(1)}, u32[]{:S(2)}, u32[]{:S(2)}) %collective-permute-start.10) | collective-permute-done | bytes 786464 | tf_op jit(solution)/shard_map/ppermute | solution.py:52
  150.2 9.0 %collective-permute-done.12 = bf16[2,384,512]{2,1,0:T(8,128)(2,1)S(1)} collective-permute-done((bf16[2,384,512]{2,1,0:T(8,128)(2,1)S(1)}, bf16[2,384,512]{2,1,0:T(8,128)(2,1)S(1)}, u32[]{:S(2)}, u32[]{:S(2)}) %collective-permute-start.12) | collective-permute-done | bytes 786464 | tf_op jit(solution)/shard_map/ppermute | solution.py:52
  160.2 4.4 multiply_convert_fusion.1
  192.2 7.0 %collective-permute-done.18.rest_1_ = bf16[2,768,512]{2,1,0:T(8,128)(2,1)} collective-permute-done((bf16[2,768,512]{2,1,0:T(8,128)(2,1)}, bf16[2,768,512]{2,1,0:T(8,128)(2,1)}, u32[]{:S(2)}, u32[]{:S(2)}) %collective-permute-start.18) | collective-permute-done | bytes 1572896 | tf_op jit(solution)/shard_map/ppermute | solution.py:52
  210.3 12.3 %shard_map.331 = (f32[384,1024]{1,0:T(8,128)}, bf16[384,1024]{1,0:T(8,128)(2,1)}, bf16[384,1024]{1,0:T(8,128)(2,1)}, bf16[384,1024]{1,0:T(8,128)(2,1)}, bf16[384...) custom-call(f32[128,1024]{1,0:T(8,128)} %add_add_fusion.2.fo, ...), custom_call_target="tpu_custom_call" | custom-call | flops 3221225472 | bytes 19800576 | tf_op jit(solution)/shard_map/pallas_call | solution.py:638
  222.7 30.3 %shard_map.332 = (bf16[384,1024]{1,0:T(8,128)(2,1)}, f32[384,1024]{1,0:T(8,128)}, bf16[384,8192]{1,0:T(8,128)(2,1)}, f32[1,4096]{1,0:T(1,128)}) custom-call(bf16[384,1024]{1,0:T(8,128)(2,1)} %get-tuple-element.206.nb, bf16[384,1024]{1,0:T(8,128)(2,1)} %get-tuple-element.207.g, f32[384,1024]{1,0:T(8,128)} %get-tuple-element.208.mid, f32[128,1]{1,0:T(8,128)} %copy.71.valid, ...), custom_call_target="tpu_custom_call" | custom-call | flops 12884901888 | bytes 28611072 | tf_op jit(solution)/shard_map/pallas_call | solution.py:638
  256.0 14.5 %shard_map.333 = (bf16[384,1024]{1,0:T(8,128)(2,1)}, bf16[384,4096]{1,0:T(8,128)(2,1)}, f32[128,1024]{1,0:T(8,128)}, f32[1,1024]{1,0:T(1,128)}, f32[1,1024]{1,0:T(1,128)}) custom-call(bf16[384,1024]{1,0:T(8,128)(2,1)} %get-tuple-element.207.g, f32[384,1024]{1,0:T(8,128)} %get-tuple-element.214.gnb, f32[384,1024]{1,0:T(8,128)} %get-tuple-element.208.mid, ...), custom_call_target="tpu_custom_call" | custom-call | flops 3221225472 | bytes 22167552 | tf_op jit(solution)/shard_map/pallas_call | solution.py:638
  277.4 19.2 %shard_map.334 = (bf16[128,8192]{1,0:T(8,128)(2,1)}, bf16[128,8192]{1,0:T(8,128)(2,1)}, bf16[128,8192]{1,0:T(8,128)(2,1)}, bf16[128,8192]{1,0:T(8,128)(2,1)}) custom-call(s32[1]{0:T(128)} %bitcast.18.me_ref, bf16[384,8192]{1,0:T(8,128)(2,1)} %get-tuple-element.223.lm, bf16[384,8192]{1,0:T(8,128)(2,1)} %collective-permute-done.27.lt, ...), custom_call_target="tpu_custom_call" | custom-call | flops 6442450944 | bytes 24117248 | tf_op jit(solution)/shard_map/pallas_call | solution.py:728
  296.5 6.4 %all-gather.9.cloned.1.call-done = bf16[512,1024]{1,0:T(8,128)(2,1)} async-done(((bf16[128,1024]{1,0:T(8,128)(2,1)}), bf16[512,1024]{1,0:T(8,128)(2,1)}) %all-gather.9.cloned.1.call-update) | async-done | bytes 1048592 | tf_op jit(solution)/shard_map/all_gather | solution.py:38
  302.9 5.0 convert_reduce_fusion
  320.2 7.1 %shard_map.336 = (bf16[128,2048]{1,0:T(8,128)(2,1)}, bf16[128,2048]{1,0:T(8,128)(2,1)}, bf16[128,2048]{1,0:T(8,128)(2,1)}, bf16[128,2048]{1,0:T(8,128)(2,1)}, bf16[512,2048]{1,0:T(8,128)(2,1)}) custom-call(s32[1]{0:T(128)} %bitcast.18.me_ref, bf16[512,2048]{1,0:T(8,128)(2,1)} %pad_maximum_fusion.left, bf16[2,512,1024]{2,1,0:T(8,128)(2,1)} %pad_maximum_fusion.1.right), custom_call_target="tpu_custom_call" | custom-call | flops 2147483648 | bytes 8388608 | tf_op jit(solution)/shard_map/pallas_call | solution.py:772
  327.4 9.8 %shard_map.335 = (bf16[128,4096]{1,0:T(8,128)(2,1)}, bf16[128,4096]{1,0:T(8,128)(2,1)}, bf16[128,4096]{1,0:T(8,128)(2,1)}, bf16[128,4096]{1,0:T(8,128)(2,1)}) custom-call(s32[1]{0:T(128)} %bitcast.18.me_ref, bf16[384,4096]{1,0:T(8,128)(2,1)} %get-tuple-element.228.lm, bf16[384,4096]{1,0:T(8,128)(2,1)} %collective-permute-done.29.lt, ...), custom_call_target="tpu_custom_call" | custom-call | flops 3221225472 | bytes 13631488 | tf_op jit(solution)/shard_map/pallas_call | solution.py:728
  341.7 22.7 %collective-permute-done.31.refs_1_ = bf16[128,8192]{1,0:T(8,128)(2,1)} collective-permute-done((bf16[128,8192]{1,0:T(8,128)(2,1)}, bf16[128,8192]{1,0:T(8,128)(2,1)}, u32[]{:S(2)}, u32[]{:S(2)}) %collective-permute-start.31) | collective-permute-done | bytes 2097184 | tf_op jit(solution)/shard_map/ppermute | solution.py:52
  372.3 8.3 %shard_map.337 = (f32[64,8192]{1,0:T(8,128)}, bf16[64,8192]{1,0:T(8,128)(2,1)}, f32[64,8192]{1,0:T(8,128)}, bf16[64,8192]{1,0:T(8,128)(2,1)}) custom-call(bf16[128,8192]{1,0:T(8,128)(2,1)} %get-tuple-element.238.refs_0_, bf16[128,8192]{1,0:T(8,128)(2,1)} %collective-permute-done.31.refs_1_, bf16[128,8192]{1,0:T(8,128)(2,1)} %get-tuple-element.240.refs_2_, ...), custom_call_target="tpu_custom_call" | custom-call | bytes 14680064 | tf_op jit(solution)/shard_map/pallas_call | solution.py:793
  405.4 5.8 %shard_map.341 = (bf16[128,1024]{1,0:T(8,128)(2,1)}, bf16[128,1024]{1,0:T(8,128)(2,1)}, bf16[128,1024]{1,0:T(8,128)(2,1)}, bf16[128,1024]{1,0:T(8,128)(2,1)}, bf16[512,1024]{1,0:T(8,128)(2,1)}) custom-call(s32[1]{0:T(128)} %bitcast.18.me_ref, bf16[512,1024]{1,0:T(8,128)(2,1)} %pad_maximum_fusion.5.left, bf16[2,512,1024]{2,1,0:T(8,128)(2,1)} %pad_maximum_fusion.2.right), custom_call_target="tpu_custom_call" | custom-call | flops 1073741824 | bytes 5242880 | tf_op jit(solution)/shard_map/pallas_call | solution.py:772
  414.8 4.6 shard_map.339
  421.4 7.4 %collective-permute-done.56.refs_1_ = bf16[64,8192]{1,0:T(8,128)(2,1)} collective-permute-done((bf16[64,8192]{1,0:T(8,128)(2,1)}, bf16[64,8192]{1,0:T(8,128)(2,1)}, u32[]{:S(2)}, u32[]{:S(2)}) %collective-permute-start.56) | collective-permute-done | bytes 1048608 | tf_op jit(solution)/shard_map/ppermute | solution.py:52
  462.3 6.5 %collective-permute-done.58.g1 = bf16[128,2048]{1,0:T(8,128)(2,1)S(1)} collective-permute-done((bf16[128,2048]{1,0:T(8,128)(2,1)}, bf16[128,2048]{1,0:T(8,128)(2,1)S(1)}, u32[]{:S(2)}, u32[]{:S(2)}) %collective-permute-start.58) | collective-permute-done | bytes 524320 | tf_op jit(solution)/shard_map/ppermute | solution.py:57
  475.8 18.9 %collective-permute-done.59.g2 = bf16[128,2048]{1,0:T(8,128)(2,1)} collective-permute-done((bf16[128,2048]{1,0:T(8,128)(2,1)}, bf16[128,2048]{1,0:T(8,128)(2,1)}, u32[]{:S(2)}, u32[]{:S(2)}) %collective-permute-start.59) | collective-permute-done | bytes 524320 | tf_op jit(solution)/shard_map/ppermute | solution.py:57
  495.5 11.9 %collective-permute-done.60.g3 = bf16[128,2048]{1,0:T(8,128)(2,1)} collective-permute-done((bf16[128,2048]{1,0:T(8,128)(2,1)}, bf16[128,2048]{1,0:T(8,128)(2,1)}, u32[]{:S(2)}, u32[]{:S(2)}) %collective-permute-start.60) | collective-permute-done | bytes 524320 | tf_op jit(solution)/shard_map/ppermute | solution.py:57
  (406 shorter events, 223.2 us)
Async XLA Ops:
  7.2 44.5 %all-gather.5.cloned.1.call-start = ((), (), s32[]{:S(2)}) async-start(), calls=%async_computation.4 | async-start | bytes 1310720 | tf_op jit(solution)/shard_map/all_gather | solution.py:38
  11.0 105.8 %reduce-scatter.5.cloned.1.call-start = ((), (), s32[]{:S(2)}) async-start(), calls=%async_computation.5 | async-start | bytes 1310720 | tf_op jit(solution)/shard_map/reduce_scatter | solution.py:42
  60.5 99.7 %all-gather.7.cloned.1.call-start = ((), (), s32[]{:S(2)}) async-start(), calls=%async_computation.6 | async-start | bytes 1310720 | tf_op jit(solution)/shard_map/all_gather | solution.py:38
  63.5 60.4 %collective-permute-start.4 = (bf16[2,128,1024]{2,1,0:T(8,128)(2,1)}, bf16[2,128,1024]{2,1,0:T(8,128)(2,1)}, u32[]{:S(2)}, u32[]{:S(2)}) collective-permute-start(bf16[2,128,1024]{2,1,0:T(8,128)(2,1)} %pad_maximum_fusion.8), channel_id=1, source_target_pairs={{0,1},{1,0},{2,3},{3,2},{4,5},{5,4},{6,7},{7,6},{8,9},{9,8},{10,11... | collective-permute-start | bytes 1572872 | tf_op jit(solution)/shard_map/ppermute | solution.py:57
  65.2 43.1 %collective-permute-start.5 = (bf16[2,128,1024]{2,1,0:T(8,128)(2,1)}, bf16[2,128,1024]{2,1,0:T(8,128)(2,1)}, u32[]{:S(2)}, u32[]{:S(2)}) collective-permute-start(bf16[2,128,1024]{2,1,0:T(8,128)(2,1)} %pad_maximum_fusion.8), channel_id=1, source_target_pairs={{0,2},{1,3},{2,0},{3,1},{4,6},{5,7},{6,4},{7,5},{8,10},{9,11},{10,... | collective-permute-start | bytes 1572872 | tf_op jit(solution)/shard_map/ppermute | solution.py:57
  67.5 56.4 %collective-permute-start.6 = (bf16[2,128,1024]{2,1,0:T(8,128)(2,1)}, bf16[2,128,1024]{2,1,0:T(8,128)(2,1)}, u32[]{:S(2)}, u32[]{:S(2)}) collective-permute-start(bf16[2,128,1024]{2,1,0:T(8,128)(2,1)} %pad_maximum_fusion.8), channel_id=1, source_target_pairs={{1,2},{2,1},{5,6},{6,5},{9,10},{10,9},{13,14},{14,13},{17,18},{18,... | collective-permute-start | bytes 1572872 | tf_op jit(solution)/shard_map/ppermute | solution.py:85
  124.9 80.2 %reduce-scatter.7.cloned.1.call-start = ((), (), s32[]{:S(2)}) async-start(), calls=%async_computation.7 | async-start | bytes 1310720 | tf_op jit(solution)/shard_map/reduce_scatter | solution.py:42
  175.1 127.9 %all-gather.9.cloned.1.call-start = ((), (), s32[]{:S(2)}) async-start(), calls=%async_computation.8 | async-start | bytes 1310720 | tf_op jit(solution)/shard_map/all_gather | solution.py:38
  272.4 64.8 %reduce-scatter.9.cloned.1.call-start = ((), (), s32[]{:S(2)}) async-start(), calls=%async_computation.9 | async-start | bytes 1310720 | tf_op jit(solution)/shard_map/reduce_scatter | solution.py:42
  277.1 50.2 %collective-permute-start.29 = (bf16[384,4096]{1,0:T(8,128)(2,1)}, bf16[384,4096]{1,0:T(8,128)(2,1)}, u32[]{:S(2)}, u32[]{:S(2)}) collective-permute-start(bf16[384,4096]{1,0:T(8,128)(2,1)} %get-tuple-element.228.lm), channel_id=1, source_target_pairs={{0,4},{4,0},{8,12},{12,8},{16,20},{20,16},{24,28},{28,24},{1,5},{5... | collective-permute-start | bytes 9437192 | tf_op jit(solution)/shard_map/ppermute | solution.py:52
  311.3 69.3 %all-gather.11.cloned.1.call-start = ((), (), s32[]{:S(2)}) async-start(), calls=%async_computation.10 | async-start | bytes 1310720 | tf_op jit(solution)/shard_map/all_gather | solution.py:38
  315.7 48.7 %collective-permute-start.31 = (bf16[128,8192]{1,0:T(8,128)(2,1)}, bf16[128,8192]{1,0:T(8,128)(2,1)}, u32[]{:S(2)}, u32[]{:S(2)}) collective-permute-start(bf16[128,8192]{1,0:T(8,128)(2,1)} %get-tuple-element.235), channel_id=1, source_target_pairs={{0,8},{4,12},{8,0},{12,4},{16,24},{20,28},{24,16},{28,20},{1,9},{5... | collective-permute-start | bytes 6291464 | tf_op jit(solution)/shard_map/ppermute | solution.py:52
  317.2 48.8 %collective-permute-start.32 = (bf16[128,8192]{1,0:T(8,128)(2,1)}, bf16[128,8192]{1,0:T(8,128)(2,1)}, u32[]{:S(2)}, u32[]{:S(2)}) collective-permute-start(bf16[128,8192]{1,0:T(8,128)(2,1)} %get-tuple-element.237), channel_id=1, source_target_pairs={{0,16},{4,20},{8,24},{12,28},{16,0},{20,4},{24,8},{28,12},{1,17},{... | collective-permute-start | bytes 6291464 | tf_op jit(solution)/shard_map/ppermute | solution.py:52
  339.4 180.5 %reduce-scatter.11.cloned.1.call-start = ((), (), s32[]{:S(2)}) async-start(), calls=%async_computation.11 | async-start | bytes 1310720 | tf_op jit(solution)/shard_map/reduce_scatter | solution.py:42
  339.6 62.8 %collective-permute-start.34 = (bf16[128,4096]{1,0:T(8,128)(2,1)}, bf16[128,4096]{1,0:T(8,128)(2,1)}, u32[]{:S(2)}, u32[]{:S(2)}) collective-permute-start(bf16[128,4096]{1,0:T(8,128)(2,1)} %get-tuple-element.254), channel_id=1, source_target_pairs={{0,8},{4,12},{8,0},{12,4},{16,24},{20,28},{24,16},{28,20},{1,9},{5... | collective-permute-start | bytes 3145736 | tf_op jit(solution)/shard_map/ppermute | solution.py:52
  340.2 65.1 %collective-permute-start.35 = (bf16[128,4096]{1,0:T(8,128)(2,1)}, bf16[128,4096]{1,0:T(8,128)(2,1)}, u32[]{:S(2)}, u32[]{:S(2)}) collective-permute-start(bf16[128,4096]{1,0:T(8,128)(2,1)} %get-tuple-element.256), channel_id=1, source_target_pairs={{0,16},{4,20},{8,24},{12,28},{16,0},{20,4},{24,8},{28,12},{1,17},{... | collective-permute-start | bytes 3145736 | tf_op jit(solution)/shard_map/ppermute | solution.py:52
  370.3 41.0 %collective-permute-start.36 = (bf16[128,2048]{1,0:T(8,128)(2,1)}, bf16[128,2048]{1,0:T(8,128)(2,1)}, u32[]{:S(2)}, u32[]{:S(2)}) collective-permute-start(bf16[128,2048]{1,0:T(8,128)(2,1)} %get-tuple-element.262), channel_id=1, source_target_pairs={{0,8},{4,12},{8,0},{12,4},{16,24},{20,28},{24,16},{28,20},{1,9},{5... | collective-permute-start | bytes 1572872 | tf_op jit(solution)/shard_map/ppermute | solution.py:52
  370.8 40.4 %collective-permute-start.37 = (bf16[128,2048]{1,0:T(8,128)(2,1)}, bf16[128,2048]{1,0:T(8,128)(2,1)}, u32[]{:S(2)}, u32[]{:S(2)}) collective-permute-start(bf16[128,2048]{1,0:T(8,128)(2,1)} %get-tuple-element.264), channel_id=1, source_target_pairs={{0,16},{4,20},{8,24},{12,28},{16,0},{20,4},{24,8},{28,12},{1,17},{... | collective-permute-start | bytes 1572872 | tf_op jit(solution)/shard_map/ppermute | solution.py:52
  411.2 40.1 %collective-permute-start.38 = (bf16[512,1024]{1,0:T(8,128)(2,1)}, bf16[512,1024]{1,0:T(8,128)(2,1)}, u32[]{:S(2)}, u32[]{:S(2)}) collective-permute-start(bf16[512,1024]{1,0:T(8,128)(2,1)} %get-tuple-element.275), channel_id=1, source_target_pairs={{0,4},{4,0},{8,12},{12,8},{16,20},{20,16},{24,28},{28,24},{1,5},{5... | collective-permute-start | bytes 3145736 | tf_op jit(solution)/shard_map/ppermute | solution.py:52
  448.9 45.8 %collective-permute-start.59 = (bf16[128,2048]{1,0:T(8,128)(2,1)}, bf16[128,2048]{1,0:T(8,128)(2,1)}, u32[]{:S(2)}, u32[]{:S(2)}) collective-permute-start(bf16[128,2048]{1,0:T(8,128)(2,1)} %get-tuple-element.337), channel_id=1, source_target_pairs={{0,2},{1,3},{2,0},{3,1},{4,6},{5,7},{6,4},{7,5},{8,10},{9,11},{10,... | collective-permute-start | bytes 1572872 | tf_op jit(solution)/shard_map/ppermute | solution.py:57
  451.4 56.0 %collective-permute-start.60 = (bf16[128,2048]{1,0:T(8,128)(2,1)}, bf16[128,2048]{1,0:T(8,128)(2,1)}, u32[]{:S(2)}, u32[]{:S(2)}) collective-permute-start(bf16[128,2048]{1,0:T(8,128)(2,1)} %get-tuple-element.338), channel_id=1, source_target_pairs={{0,3},{1,2},{2,1},{3,0},{4,7},{5,6},{6,5},{7,4},{8,11},{9,10},{10,... | collective-permute-start | bytes 1572872 | tf_op jit(solution)/shard_map/ppermute | solution.py:57
  468.8 45.2 %collective-permute-start.53 = (bf16[128,1024]{1,0:T(8,128)(2,1)}, bf16[128,1024]{1,0:T(8,128)(2,1)S(1)}, u32[]{:S(2)}, u32[]{:S(2)}) collective-permute-start(bf16[128,1024]{1,0:T(8,128)(2,1)} %get-tuple-element.320), channel_id=1, source_target_pairs={{0,1},{1,0},{2,3},{3,2},{4,5},{5,4},{6,7},{7,6},{8,9},{9,8},{10,11... | collective-permute-start | bytes 786440 | tf_op jit(solution)/shard_map/ppermute | solution.py:57
  471.6 42.4 %collective-permute-start.54 = (bf16[128,1024]{1,0:T(8,128)(2,1)}, bf16[128,1024]{1,0:T(8,128)(2,1)S(1)}, u32[]{:S(2)}, u32[]{:S(2)}) collective-permute-start(bf16[128,1024]{1,0:T(8,128)(2,1)} %get-tuple-element.321), channel_id=1, source_target_pairs={{0,2},{1,3},{2,0},{3,1},{4,6},{5,7},{6,4},{7,5},{8,10},{9,11},{10,... | collective-permute-start | bytes 786440 | tf_op jit(solution)/shard_map/ppermute | solution.py:57
  471.8 42.2 %collective-permute-start.55 = (bf16[128,1024]{1,0:T(8,128)(2,1)}, bf16[128,1024]{1,0:T(8,128)(2,1)}, u32[]{:S(2)}, u32[]{:S(2)}) collective-permute-start(bf16[128,1024]{1,0:T(8,128)(2,1)} %get-tuple-element.322), channel_id=1, source_target_pairs={{0,3},{1,2},{2,1},{3,0},{4,7},{5,6},{6,5},{7,4},{8,11},{9,10},{10,... | collective-permute-start | bytes 786440 | tf_op jit(solution)/shard_map/ppermute | solution.py:57
  (106 other events, 1474.9 us)
Sparse Core Ops, SparseCore 0:
  11.1 37.9 all-gather.4
  60.6 49.2 reduce-scatter.4
  125.0 26.1 all-gather.6
  175.2 25.2 reduce-scatter.6
  272.5 30.4 all-gather.8
  311.4 24.5 reduce-scatter.8
  339.5 27.4 all-gather.10
  397.8 24.6 reduce-scatter.10

commit v3 on v2

v3 whole, which is shorter than its diff:
```python
import functools
import math

import jax
import jax.numpy as jnp
from jax import lax
from jax.experimental import pallas as pl
from jax.experimental.pallas import tpu as pltpu
from jax.sharding import PartitionSpec as P

HD = 64
eps = 1e-05
BF = jnp.bfloat16
F32 = jnp.float32


def normalize(stream, gain_vec):
    return stream * lax.rsqrt(jnp.mean(stream * stream, axis=-1, keepdims=True) + eps) * gain_vec


def activate(values):
    return jax.nn.gelu(values, approximate=True)


def dot_nt(a, b):
    return lax.dot_general(a, b, (((1,), (1,)), ((), ())), preferred_element_type=F32)


def dot_nn(a, b):
    return lax.dot_general(a, b, (((1,), (0,)), ((), ())), preferred_element_type=F32)


def dot_tn(a, b):
    return lax.dot_general(a, b, (((0,), (0,)), ((), ())), preferred_element_type=F32)


def gather_rows(rows):
    return lax.all_gather(rows, "mp", axis=0, tiled=True)


def scatter_rows(partial):
    return lax.psum_scatter(
        partial.astype(BF), "mp", scatter_dimension=0, tiled=True
    ).astype(F32)


INNER = 8


def swap_dp(value, bit):
    size = lax.axis_size("dp")
    return lax.ppermute(value, "dp", [(i, i ^ bit) for i in range(size)])


def swap_mp(value, mask):
    size = lax.axis_size("mp")
    return lax.ppermute(value, "mp", [(i, i ^ mask) for i in range(size)])


def my_place():
    return lax.axis_index("dp") % INNER


BITS = [2, 4]
SIDES = [BITS, BITS[::-1]]


def after(value, *marks):
    return lax.optimization_barrier((value,) + tuple(marks))[0]


def all_after(values, *marks):
    return lax.optimization_barrier(tuple(values) + tuple(marks))[: len(values)]


class Gather:
    def __init__(self, piece):
        self.k = piece.shape[1]
        self.piece = piece

    def shards(self, *marks, then=()):
        piece = after(self.piece, *marks) if marks else self.piece
        near = swap_mp(piece, 1)
        far = swap_mp(piece, 2)
        inner = lax.ppermute(piece, "mp", [(1, 2), (2, 1)])
        outer = lax.ppermute(after(far, *then), "mp", [(2, 3), (1, 0)])
        self.held = (near, far, inner, outer)

    def plane_first(self, *marks):
        near, far, inner, outer = all_after(self.held, *marks)
        z = lax.axis_index("mp")
        last = jnp.where((z == 1) | (z == 2), inner, outer)
        half = near.shape[2] // 2
        self.held = []
        for h, side in enumerate(SIDES):
            lanes = slice(h * half, (h + 1) * half)
            whole = jnp.concatenate([near[..., lanes], far[..., lanes], last[..., lanes]], axis=1)
            self.held.append((whole, swap_dp(whole, side[0])))

    def marks(self):
        return [got for _, got in self.held]

    def plane_last(self, *marks):
        held = []
        for (whole, got), side in zip(self.held, SIDES):
            whole, got = all_after((whole, got), *marks)
            low = jnp.concatenate([whole, got], axis=1)
            held.append((low, swap_dp(low, side[1])))
        self.held = held

    def cores(self, *marks):
        held = []
        for low, high in self.held:
            low, high = all_after((low, high), *marks)
            held += [low, high, swap_dp(low, 1), swap_dp(high, 1)]
        self.held = held


def buffer_rows(k):
    out = []
    for h, side in enumerate(SIDES):
        first, last = side[0] // 2, side[1] // 2
        for core in range(2):
            for high in range(2):
                for i in range(2):
                    place = 2 * (i * first + high * last) + core
                    for r in range(3):
                        out.append((h, 4 * h + 2 * core + high, (3 * i + r) * k, place, r + 1))
    return out


def own_rows(shard_rows):
    k = shard_rows.shape[0] // INNER
    return lax.dynamic_slice_in_dim(shard_rows, my_place() * k, k, 0)


def own_cols(shard_cols):
    k = shard_cols.shape[-1] // INNER
    piece = lax.dynamic_slice_in_dim(shard_cols, my_place() * k, k, shard_cols.ndim - 1)
    return jnp.swapaxes(piece, -1, -2)


def by_xor(slots):
    me = my_place()
    for bit in [1] + BITS:
        on = (me & bit) != 0
        slots = [jnp.where(on, slots[i ^ bit], slots[i]) for i in range(len(slots))]
    return slots


def by_xor_mp(slots):
    z = lax.axis_index("mp")
    for bit in (1, 2):
        on = (z & bit) != 0
        slots = [jnp.where(on, slots[i ^ bit], slots[i]) for i in range(len(slots))]
    return slots


def gather_all(value):
    return by_xor_mp([value] + [swap_mp(value, r) for r in (1, 2, 3)])


def gather_rows_p(rows):
    return jnp.concatenate(gather_all(rows), axis=0)


def scatter_rows_p(partial):
    low = partial.astype(BF)
    local = low.shape[0] // 4
    z = lax.axis_index("mp")
    cut = lambda at: lax.dynamic_slice_in_dim(low, at * local, local, 0)
    return cut(z), [swap_mp(cut(z ^ r), r) for r in (1, 2, 3)]


def scatter_plane(value):
    size = lax.axis_size("dp")
    groups = [
        [o + 2 * i + c for i in range(4)] for o in range(0, size, INNER) for c in range(2)
    ]
    return lax.psum_scatter(value, "dp", scatter_dimension=0, axis_index_groups=groups, tiled=True)


def plane_parts(value, *marks):
    if marks:
        value = after(value, *marks)
    block = value.shape[0] // 4
    at = my_place() // 2
    cut = lambda i: lax.dynamic_slice_in_dim(value, i * block, block, 0)
    return cut(at), [swap_dp(cut(at ^ m), 2 * m) for m in (1, 2, 3)]


def scatter_shards(value, n, *marks):
    z = lax.axis_index("mp")
    if marks:
        value = after(value, *marks)
    count = value.shape[1] // (4 * n)

    def cut(at):
        return jnp.concatenate(
            [lax.dynamic_slice_in_dim(value, (4 * i + at) * n, n, 1) for i in range(count)], axis=1
        )

    return cut(z), [swap_mp(cut(z ^ r), r) for r in (1, 2, 3)]


def shards_total(own, sent, *marks):
    sent = all_after(sent, *marks)
    return own.astype(F32) + sent[0].astype(F32) + sent[1].astype(F32) + sent[2].astype(F32)


def d_order(rows):
    outer = lax.axis_size("dp") // INNER
    if outer == 1:
        return rows
    view = rows.reshape(rows.shape[0], outer, INNER, -1)
    return jnp.transpose(view, (0, 2, 1, 3)).reshape(rows.shape)


def outer_sum(value, axis):
    size = lax.axis_size("dp")
    if size == INNER:
        return value
    groups = [[o * INNER + i for o in range(size // INNER)] for i in range(INNER)]
    return lax.psum_scatter(
        value, "dp", scatter_dimension=axis, axis_index_groups=groups, tiled=True
    )


def rsq(x):
    return lax.rsqrt(jnp.mean(x * x, axis=-1, keepdims=True) + eps)


def norm_back(grad, x, gain):
    r = rsq(x)
    xr = x * r
    gg = grad * gain
    return r * (gg - xr * jnp.mean(gg * xr, axis=-1, keepdims=True)), grad * xr


def split_dot(x, table):
    hi = x.astype(BF)
    lo = (x - hi.astype(F32)).astype(BF)
    return dot_nn(hi, table) + dot_nn(lo, table)


PAIRS = [(p, s) for p in range(3) for s in range(p + 1)]


def weight_copies(ids, k, bufs, dst, sem, first):
    half, n = dst.shape[2] // 2, dst.shape[1] // 4
    copies = []
    for i, (h, buf, row, place, hop) in enumerate(buffer_rows(k)):
        at = pl.multiple_of((ids[1] ^ hop) * n + (ids[0] ^ place) * k, k)
        copies.append(
            pltpu.make_async_copy(
                bufs[buf].at[:, pl.ds(row, k)],
                dst.at[:, pl.ds(at, k), pl.ds(h * half, half)],
                sem.at[first + i],
            )
        )
    return copies


COPIES = 48


def attn_weight_copies(ids, own_qkv, own_out, bufs, w, sem):
    n = own_out.shape[0]
    own = pl.ds(pl.multiple_of(ids[1] * n, n), n)
    copies = [
        pltpu.make_async_copy(own_qkv, w.at[pl.ds(0, 3), own], sem.at[0]),
        pltpu.make_async_copy(own_out, w.at[3, own], sem.at[1]),
    ]
    return copies + weight_copies(ids, n // INNER, bufs, w, sem, 2)


def place_pick(p, frames):
    col = lax.broadcasted_iota(jnp.int32, (frames, 3 * frames), 1)
    row = lax.broadcasted_iota(jnp.int32, (frames, 3 * frames), 0)
    return (col == 3 * row + p).astype(BF)


def place_put(p, frames):
    row = lax.broadcasted_iota(jnp.int32, (3 * frames, frames), 0)
    col = lax.broadcasted_iota(jnp.int32, (3 * frames, frames), 1)
    return (row == 3 * col + p).astype(BF)


def frame_out_copies(ids, own, bufs, w, sem):
    n, d = own.shape
    k, half = n // INNER, d // 2
    copies = [pltpu.make_async_copy(own, w.at[0], sem.at[0])]
    for h, buf, row, place, hop in buffer_rows(k):
        at = pl.multiple_of((ids[0] ^ place) * k, k)
        copies.append(
            pltpu.make_async_copy(
                bufs[buf].at[0, pl.ds(row, k)],
                w.at[hop, pl.ds(at, k), pl.ds(h * half, half)],
                sem.at[len(copies)],
            )
        )
    return copies


FRAME_OUT_COPIES = 1 + 48


def frame_out_kernel(ids, m0, m1, m2, m3, frames, gain, own, *rest):
    bufs, (mid_o, nb_o, w, sem) = rest[:8], rest[8:]
    copies = frame_out_copies(ids, own, bufs, w, sem)
    for c in copies:
        c.start()
    for c in copies:
        c.wait()
    mid = frames[...].astype(F32)
    for r, m in enumerate((m0, m1, m2, m3)):
        mid = mid + dot_nn(m[...], w[r])
    mid_o[...] = mid
    nb_o[...] = (mid * rsq(mid) * gain[...]).astype(BF)


def frame_mid_kernel(ids, gnb, mid, grad_out, gain, own, *rest):
    bufs, (gm_o, low_o, dg_o, gx_o, w, sem) = rest[:8], rest[8:]
    copies = frame_out_copies(ids, own, bufs, w, sem)
    for c in copies:
        c.start()
    dx, dg = norm_back(gnb[...], mid[...], gain[...])
    grad = grad_out[...] + dx
    gm_o[...] = grad
    low_o[...] = grad.astype(BF)
    dg_o[...] = jnp.sum(dg, axis=0, keepdims=True)
    for c in copies:
        c.wait()
    for r in range(4):
        gx_o[r] = dot_nt(low_o[...], w[r]).astype(BF)


def token_attn_kernel(ids, fo, emb, cot, valid, ga, gb, table, own_qkv, own_out, *rest):
    bufs, (s_o, g_o, na_o, q_o, k_o, v_o, mix_o, mid_o, nb_o, pr_o, w, sem) = rest[:8], rest[8:]
    copies = attn_weight_copies(ids, own_qkv, own_out, bufs, w, sem)
    for c in copies:
        c.start()
    frames = fo.shape[0]
    places = [pl.ds(p * frames, frames) for p in range(3)]
    for p in range(3):
        pick = place_pick(p, frames)
        g = dot_nn(pick, cot[...])
        g_o[places[p]] = jnp.where(valid[...] > 0.0, g, 0.0).astype(BF)
        s = fo[...] + dot_nn(pick, emb[...])
        s_o[places[p]] = s
        na_o[places[p]] = (s * rsq(s) * ga[...]).astype(BF)
    for c in copies:
        c.wait()
    for t, out in enumerate((q_o, k_o, v_o)):
        out[...] = dot_nt(na_o[...], w[t]).astype(BF)
    scale = 1.0 / math.sqrt(HD)
    for p in range(3):
        scores = [
            split_dot(q_o[places[p]].astype(F32) * k_o[places[s]].astype(F32), table[...]) * scale
            for s in range(p + 1)
        ]
        top = scores[0]
        for x in scores[1:]:
            top = jnp.maximum(top, x)
        ex = [jnp.exp(x - top) for x in scores]
        total = ex[0]
        for x in ex[1:]:
            total = total + x
        mixed = None
        for s in range(p + 1):
            prob = ex[s] / total
            pr_o[PAIRS.index((p, s))] = prob
            term = dot_nt(prob.astype(BF), table[...]) * v_o[places[s]].astype(F32)
            mixed = term if mixed is None else mixed + term
        mix_o[places[p]] = mixed.astype(BF)
    for p in places:
        mid = s_o[p] + dot_nn(mix_o[p], w[3])
        mid_o[p] = mid
        nb_o[p] = (mid * rsq(mid) * gb[...]).astype(BF)


def token_back_kernel(ids, g, gnb, mid, s_in, ga, gb, q, k, v, mix, pr, table, own_qkv, own_out, *rest):
    bufs, (ml_o, left_o, gf_o, da_o, db_o, w, gm, gx, sem) = rest[:8], rest[8:]
    copies = attn_weight_copies(ids, own_qkv, own_out, bufs, w, sem)
    for c in copies:
        c.start()
    frames, feats = gf_o.shape[0], q.shape[1]
    places = [pl.ds(p * frames, frames) for p in range(3)]
    lanes = [pl.ds(t * feats, feats) for t in range(4)]
    total = None
    for p in places:
        dx, dg = norm_back(gnb[p], mid[p], gb[...])
        grad = g[p].astype(F32) + dx
        gm[p] = grad
        ml_o[p] = grad.astype(BF)
        row = jnp.sum(dg, axis=0, keepdims=True)
        total = row if total is None else total + row
    db_o[...] = total
    left_o[:, lanes[3]] = mix[...]
    for c in copies:
        c.wait()
    gx[...] = dot_nt(ml_o[...], w[3]).astype(BF)
    scale = 1.0 / math.sqrt(HD)
    kg, vg = {}, {}
    for p in range(3):
        gp = [
            split_dot(gx[places[p]].astype(F32) * v[places[s]].astype(F32), table[...])
            for s in range(p + 1)
        ]
        probs = [pr[PAIRS.index((p, s))] for s in range(p + 1)]
        delta = probs[0] * gp[0]
        for s in range(1, p + 1):
            delta = delta + probs[s] * gp[s]
        query = None
        for s in range(p + 1):
            wide = dot_nt((probs[s] * (gp[s] - delta)).astype(BF), table[...])
            term = wide * k[places[s]].astype(F32)
            query = term if query is None else query + term
            key = wide * q[places[p]].astype(F32) * scale
            value = dot_nt(probs[s].astype(BF), table[...]) * gx[places[p]].astype(F32)
            if p == s:
                kg[s], vg[s] = key, value
            else:
                kg[s], vg[s] = kg[s] + key, vg[s] + value
        left_o[places[p], lanes[0]] = (query * scale).astype(BF)
    for s in range(3):
        left_o[places[s], lanes[1]] = kg[s].astype(BF)
        left_o[places[s], lanes[2]] = vg[s].astype(BF)
    gna = dot_nn(left_o[:, lanes[0]], w[0]) + dot_nn(left_o[:, lanes[1]], w[1]) + dot_nn(left_o[:, lanes[2]], w[2])
    total = out = None
    for i, p in enumerate(places):
        dx, dg = norm_back(gna[i * frames : (i + 1) * frames], s_in[p], ga[...])
        grad = gm[p] + dx
        row = jnp.sum(dg, axis=0, keepdims=True)
        total = row if total is None else total + row
        out = grad if out is None else out + grad
    da_o[...] = total
    gf_o[...] = out


GELU_S = math.sqrt(2.0 / math.pi)


def gelu_both(u):
    u2 = u * u
    t = jnp.tanh(GELU_S * (u + 0.044715 * (u2 * u)))
    h = 0.5 * (1.0 + t)
    return u * h, h + 0.5 * u * (1.0 - t * t) * (GELU_S * (1.0 + 3.0 * 0.044715 * u2))


def token_ff_kernel(step, ids, nb, g, mid, valid, bias, bdown, own_up, own_down, *rest):
    bufs, (out_o, gnb_o, left_o, gb_o, wuo, wdo, w, acc, sem) = rest[:8], rest[8:]
    n, frames = own_down.shape[0], valid.shape[0]
    own = [
        pltpu.make_async_copy(own_up, wuo, sem.at[0]),
        pltpu.make_async_copy(own_down, wdo, sem.at[1]),
    ]
    copies = weight_copies(ids, n // INNER, bufs, w, sem, 2)
    z = ids[1]
    for c in own + copies:
        c.start()
    acc[...] = jnp.zeros_like(acc)
    gnb_o[...] = jnp.zeros_like(gnb_o)

    def middle(at, size, pre, back):
        cols = pl.ds(at, size)
        h, dh = gelu_both(pre + bias[:, cols])
        h = h.astype(BF)
        gp = (dh * back).astype(BF)
        left_o[:, cols] = h
        left_o[:, pl.ds(pl.multiple_of(4 * n + at, 128), size)] = gp
        gb_o[:, cols] = jnp.sum(gp.astype(F32), axis=0, keepdims=True)
        return h, gp

    for c in own:
        c.wait()
    own_step = n // 2

    def own_block(j, carry):
        cols = pl.ds(pl.multiple_of(j * own_step, own_step), own_step)
        pre = dot_nn(nb[...], wuo[:, cols])
        back = dot_nt(g[...], wdo[cols, :])
        h, gp = middle(pl.multiple_of(z * n + j * own_step, own_step), own_step, pre, back)
        acc[...] += dot_nn(h, wdo[cols, :])
        gnb_o[...] += dot_nt(gp, wuo[:, cols])
        return carry

    lax.fori_loop(0, n // own_step, own_block, 0)
    for c in copies:
        c.wait()

    def block(j, carry):
        at = pl.multiple_of(j * step + jnp.where(j * step >= z * n, n, 0), step)
        rows = pl.ds(at, step)
        pre = dot_nt(nb[...], w[0, rows, :])
        back = dot_nt(g[...], w[1, rows, :])
        h, gp = middle(at, step, pre, back)
        acc[...] += dot_nn(h, w[1, rows, :])
        gnb_o[...] += dot_nn(gp, w[0, rows, :])
        return carry

    lax.fori_loop(0, 3 * n // step, block, 0)
    out = None
    for p in range(3):
        rows = pl.ds(p * frames, frames)
        val = jnp.where(valid[...] > 0.0, acc[rows] + mid[rows] + bdown[...], 0.0).astype(BF)
        term = dot_nn(place_put(p, frames), val)
        out = term if out is None else out + term
    out_o[...] = out.astype(BF)


def lay_right(dst, row, col, right, core, block):
    for i in range(INNER // 2):
        at = pl.multiple_of((2 * i + core) * block, block)
        dst[pl.ds(row + i * block, block), pl.ds(col, right.shape[1])] = right[pl.ds(at, block), :]


def pair_grad_kernel(new, ids, lm, lt, rm, rt, out, tmp, am):
    @pl.when(new(pl.program_id(0)))
    def _():
        for i, src in enumerate((rm, rt)):
            tmp[...] = jnp.transpose(src[0])
            lay_right(am, 0, i * src.shape[1], tmp, ids[0] & 1, src.shape[2] // INNER)

    out[...] = dot_nn(am[...], jnp.concatenate([lm[...], lt[...]], axis=0)).astype(BF)


def frame_grad_kernel(new, ids, left, right, same, cross, tmp, am):
    d = right.shape[2]

    @pl.when(new(pl.program_id(0)))
    def _():
        tmp[...] = jnp.transpose(right[0])
        for i in range(2):
            lay_right(am, i * (d // 2), 0, tmp, (ids[0] & 1) ^ i, d // INNER)

    total = dot_nn(am[...], left[...])
    same[...] = total[: d // 2].astype(BF)
    cross[...] = total[d // 2 :].astype(BF)


VMEM_LIMIT = 60 * 1024 * 1024


def arr(shape, dtype):
    return jax.ShapeDtypeStruct(shape, dtype)


def cost(flops, ins, outs):
    size = sum(a.size * a.dtype.itemsize for a in ins) + sum(
        math.prod(o.shape) * o.dtype.itemsize for o in outs
    )
    return pl.CostEstimate(flops=flops, bytes_accessed=size, transcendentals=0)


def call(kernel, outs, ins, scratch, any_from, flops, smem=0):
    def space(i):
        return pltpu.SMEM if i < smem else pltpu.VMEM if i < any_from else pl.ANY

    return pl.pallas_call(
        kernel,
        out_shape=outs,
        in_specs=[pl.BlockSpec(memory_space=space(i)) for i in range(len(ins))],
        out_specs=[pl.BlockSpec(memory_space=pltpu.VMEM)] * len(outs),
        scratch_shapes=scratch,
        compiler_params=pltpu.CompilerParams(vmem_limit_bytes=VMEM_LIMIT),
        cost_estimate=cost(flops, ins, outs),
    )(*ins)


def frame_out(ids, mixed, frames, gain, own, bufs):
    rows, d = frames.shape
    ins = [ids, *mixed, frames, gain, own, *bufs]
    scratch = [pltpu.VMEM((4, *own.shape), BF), pltpu.SemaphoreType.DMA((FRAME_OUT_COPIES,))]
    outs = [arr((rows, d), F32), arr((rows, d), BF)]
    return call(frame_out_kernel, outs, ins, scratch, 7, 8 * rows * own.size, smem=1)


def frame_mid(ids, gnb, mid, grad_out, gain, own, bufs):
    rows, d = mid.shape
    ins = [ids, gnb, mid, grad_out, gain, own, *bufs]
    scratch = [pltpu.VMEM((4, *own.shape), BF), pltpu.SemaphoreType.DMA((FRAME_OUT_COPIES,))]
    outs = [arr((rows, d), F32), arr((rows, d), BF), arr((1, d), F32), arr((4, rows, own.shape[0]), BF)]
    return call(frame_mid_kernel, outs, ins, scratch, 5, 8 * rows * own.size, smem=1)


def token_attn(ids, fo, emb, cot, valid, ga, gb, table, own_qkv, own_out, bufs):
    frames, d = fo.shape
    rows, feats = 3 * frames, table.shape[0]
    outs = (
        [arr((rows, d), F32), arr((rows, d), BF), arr((rows, d), BF)]
        + [arr((rows, feats), BF)] * 4
        + [arr((rows, d), F32), arr((rows, d), BF), arr((len(PAIRS), frames, table.shape[1]), F32)]
    )
    return call(
        token_attn_kernel,
        outs,
        [ids, fo, emb, cot, valid, ga, gb, table, own_qkv, own_out, *bufs],
        [pltpu.VMEM((4, feats, d), BF), pltpu.SemaphoreType.DMA((2 + COPIES,))],
        8,
        8 * rows * feats * d,
        smem=1,
    )


def token_back(ids, g, gnb, mid, s, ga, gb, q, k, v, mix, pr, table, own_qkv, own_out, bufs):
    rows, d = s.shape
    frames, feats = rows // 3, table.shape[0]
    outs = [
        arr((rows, d), BF),
        arr((rows, 4 * feats), BF),
        arr((frames, d), F32),
        arr((1, d), F32),
        arr((1, d), F32),
    ]
    return call(
        token_back_kernel,
        outs,
        [ids, g, gnb, mid, s, ga, gb, q, k, v, mix, pr, table, own_qkv, own_out, *bufs],
        [
            pltpu.VMEM((4, feats, d), BF),
            pltpu.VMEM((rows, d), F32),
            pltpu.VMEM((rows, feats), BF),
            pltpu.SemaphoreType.DMA((2 + COPIES,)),
        ],
        13,
        8 * rows * feats * d,
        smem=1,
    )


def token_ff(ids, nb, g, mid, valid, bias, bdown, own_up, own_down, bufs):
    rows, d = nb.shape
    n = own_down.shape[0]
    outs = [
        arr((rows, d), BF),
        arr((rows, d), F32),
        arr((rows, 8 * n), BF),
        arr((1, 4 * n), F32),
    ]
    return call(
        functools.partial(token_ff_kernel, 512),
        outs,
        [ids, nb, g, mid, valid, bias, bdown, own_up, own_down, *bufs],
        [
            pltpu.VMEM((d, n), BF),
            pltpu.VMEM((n, d), BF),
            pltpu.VMEM((2, 4 * n, d), BF),
            pltpu.VMEM((rows, d), F32),
            pltpu.SemaphoreType.DMA((2 + COPIES,)),
        ],
        7,
        32 * rows * n * d,
        smem=1,
    )


def smem_spec():
    return pl.BlockSpec(memory_space=pltpu.SMEM)


def pair_grad(ids, left, left_other, rights, rights_other, split):
    rows, units = left.shape
    d = rights.shape[2]
    step = d
    at = split // step
    pick = lambda j: jnp.where(j < at, 0, 1)
    outs = [arr((d // 2, units), BF)]
    [out] = pl.pallas_call(
        functools.partial(pair_grad_kernel, lambda j: (j == 0) | (j == at)),
        grid=(units // step,),
        in_specs=[smem_spec()]
        + [pl.BlockSpec((rows, step), lambda j: (0, j))] * 2
        + [pl.BlockSpec((1, rows, d), lambda j: (pick(j), 0, 0))] * 2,
        out_specs=[pl.BlockSpec((d // 2, step), lambda j: (0, j))],
        out_shape=outs,
        scratch_shapes=[pltpu.VMEM((d, rows), BF), pltpu.VMEM((d // 2, 2 * rows), BF)],
        compiler_params=pltpu.CompilerParams(vmem_limit_bytes=VMEM_LIMIT),
        cost_estimate=cost(2 * rows * units * d, [left, left_other, rights, rights_other], outs),
    )(ids, left, left_other, rights, rights_other)
    return out


def frame_grad(ids, left, rights, split):
    rows, units = left.shape
    d = rights.shape[2]
    step = units // 4
    at = split // step
    outs = [arr((d // 2, units), BF)] * 2
    return pl.pallas_call(
        functools.partial(frame_grad_kernel, lambda j: (j == 0) | (j == at)),
        grid=(4,),
        in_specs=[
            smem_spec(),
            pl.BlockSpec((rows, step), lambda j: (0, j)),
            pl.BlockSpec((1, rows, d), lambda j: (jnp.where(j < at, 0, 1), 0, 0)),
        ],
        out_specs=[pl.BlockSpec((d // 2, step), lambda j: (0, j))] * 2,
        out_shape=outs,
        scratch_shapes=[pltpu.VMEM((d, rows), BF)] * 2,
        compiler_params=pltpu.CompilerParams(vmem_limit_bytes=VMEM_LIMIT),
        cost_estimate=cost(2 * rows * units * d, [left, rights], outs),
    )(ids, left, rights)


def segments(lengths, whole_rows):
    count = lengths.shape[1]
    order = jnp.arange(count, dtype=jnp.int32)
    item_ends = jnp.sum(
        jnp.where(order[None, :] <= order[:, None], lengths[0][None, :], 0), axis=1, dtype=jnp.int32
    )
    positions = jnp.arange(whole_rows, dtype=jnp.int32)
    segment = jnp.sum(
        (positions[:, None] >= item_ends[None, :]).astype(jnp.int32), axis=1, dtype=jnp.int32
    )
    is_valid = positions < jnp.sum(lengths[0], dtype=jnp.int32)
    segment = jnp.where(is_valid, segment, positions + count)
    return (segment, is_valid)


def frame_allowed(segment):
    positions = jnp.arange(segment.shape[0], dtype=jnp.int32)
    return (positions[None, :] <= positions[:, None]) & (segment[None, :] == segment[:, None])


def split_heads(rows):
    return rows.reshape(rows.shape[0], rows.shape[1] // HD, HD)


def frame_forward(qkv_rows, segment):
    queries, key_rows, value_rows = (split_heads(qkv_rows[t]) for t in range(3))
    raw_scores = jnp.einsum("qhe,khe->hqk", queries, key_rows, preferred_element_type=F32) * (
        1.0 / math.sqrt(HD)
    )
    scores = jnp.where(frame_allowed(segment)[None], raw_scores, -1e30)
    top_score = jnp.max(scores, axis=-1, keepdims=True)
    exp_scores = jnp.exp(scores - top_score)
    exp_total = jnp.sum(exp_scores, axis=-1, keepdims=True)
    attn_probs = (exp_scores / exp_total).astype(BF)
    mixed = jnp.einsum("hqk,khe->qhe", attn_probs, value_rows, preferred_element_type=F32)
    log_total = top_score[:, :, 0] + jnp.log(exp_total[:, :, 0])
    return (mixed.astype(BF).reshape(qkv_rows.shape[1], -1), log_total)


def frame_backward(qkv_rows, log_total, grad_mixed, segment):
    queries, key_rows, value_rows = (split_heads(qkv_rows[t]) for t in range(3))
    grad_heads = split_heads(grad_mixed)
    scale = 1.0 / math.sqrt(HD)
    raw_scores = jnp.einsum("qhe,khe->hqk", queries, key_rows, preferred_element_type=F32) * scale
    scores = jnp.where(frame_allowed(segment)[None], raw_scores, -1e30)
    attn_probs = jnp.exp(scores - log_total[:, :, None])
    value_grad = jnp.einsum(
        "hqk,qhe->khe", attn_probs.astype(BF), grad_heads, preferred_element_type=F32
    )
    grad_probs = jnp.einsum("qhe,khe->hqk", grad_heads, value_rows, preferred_element_type=F32)
    row_delta = jnp.sum(attn_probs * grad_probs, axis=-1, keepdims=True)
    grad_scores = (attn_probs * (grad_probs - row_delta)).astype(BF)
    query_grad = jnp.einsum("hqk,khe->qhe", grad_scores, key_rows, preferred_element_type=F32) * scale
    key_grad = jnp.einsum("hqk,qhe->khe", grad_scores, queries, preferred_element_type=F32) * scale
    rows = qkv_rows.shape[1]
    return [g.reshape(rows, -1).astype(BF) for g in (query_grad, key_grad, value_grad)]


def head_table(features):
    at = jnp.arange(features, dtype=jnp.int32)
    return ((at // HD)[:, None] == jnp.arange(128, dtype=jnp.int32)[None, :]).astype(BF)


def shards(frames, codes_embed, lengths, cotangent, *params):
    gain_a, w_qkv, w_out, gain_b, w_up, b_up, w_down, b_down = params[:8]
    t_gain_a, t_qkv, t_out, t_gain_b, t_up, t_bup, t_down, t_bdown = params[8:]
    dp, parts = lax.axis_size("dp"), lax.axis_size("mp")
    z = lax.axis_index("mp")
    ids = jnp.stack([my_place(), z]).astype(jnp.int32)
    local, d = frames.shape
    n_attn, n_ff = w_out.shape[0], w_down.shape[0]
    block = d // INNER
    segment, is_valid = segments(lengths, local * parts)
    valid = lax.dynamic_slice_in_dim(is_valid, z * local, local, 0).astype(F32)[:, None]

    stream = frames.astype(F32)
    gain_a32, gain_b32 = gain_a.astype(F32), gain_b.astype(F32)
    normed_a = normalize(stream, gain_a32).astype(BF)
    gathered_a = gather_rows(normed_a)

    attn_w = Gather(jnp.concatenate([own_cols(t_qkv), own_rows(t_out)[None]], axis=0))
    ff_w = Gather(jnp.stack([own_cols(t_up), own_rows(t_down)]))
    out_w = Gather(own_rows(w_out)[None])
    out_w.shards()
    out_w.plane_first()
    out_w.plane_last()
    out_w.cores()
    attn_w.shards()
    gathered_a = after(gathered_a, *out_w.held, *attn_w.held)

    qkv_rows = jnp.einsum("rd,tde->tre", gathered_a, w_qkv, preferred_element_type=F32).astype(BF)
    mixed_rows, log_total = frame_forward(qkv_rows, segment)
    by_rows = [
        lax.dynamic_slice_in_dim(mixed_rows, (z ^ r) * local, local, 0) for r in range(parts)
    ]
    mixed_own = [by_rows[0]] + [swap_mp(by_rows[r], r) for r in range(1, parts)]

    attn_w.plane_first(mixed_rows)
    middle, normed_b = frame_out(ids, mixed_own, frames, gain_b32[None], w_out, out_w.held)
    ff_w.shards(normed_b)
    gathered_b = gather_rows(normed_b)

    attn_w.plane_last(normed_b)
    ff_w.plane_first(normed_b)
    gathered_b = after(gathered_b, *attn_w.marks(), *ff_w.marks())

    hidden_pre = dot_nn(gathered_b, w_up) + b_up.astype(F32)
    hidden = activate(hidden_pre).astype(BF)
    part_b = dot_nn(hidden, w_down).astype(BF)
    branch_b = scatter_rows(part_b)

    attn_w.cores(part_b)
    ff_w.plane_last(part_b)
    f_result = middle + after(branch_b, *attn_w.held, *ff_w.marks()) + b_down.astype(F32)

    t_bias = jnp.concatenate(gather_all(t_bup)).astype(F32)[None]
    own_qkv = jnp.transpose(t_qkv, (0, 2, 1))
    table = head_table(n_attn * parts)
    tga, tgb = t_gain_a.astype(F32)[None], t_gain_b.astype(F32)[None]

    attn_bufs = attn_w.held
    t_stream, g_low, t_na, q, k, v, mixed, t_middle, t_nb, probs = token_attn(
        ids, f_result, codes_embed, cotangent, valid, tga, tgb, table, own_qkv, t_out, attn_bufs
    )
    ff_w.cores()
    output, t_gnb, t_left, t_gbup = token_ff(
        ids, t_nb, g_low, t_middle, valid, t_bias, t_bdown.astype(F32)[None], t_up, t_down, ff_w.held
    )
    rights = jnp.stack([d_order(g_low), d_order(t_nb)])
    rights_other = swap_dp(rights, 1)
    left_other = swap_dp(t_left, 1)
    m_low, a_left, grad_frame, t_da, t_db = token_back(
        ids, g_low, t_gnb, t_middle, t_stream, tga, tgb, q, k, v, mixed, probs, table, own_qkv, t_out, attn_bufs
    )
    t_dbd = jnp.sum(g_low.astype(F32), axis=0)

    ff_grad = pair_grad(ids, after(t_left, grad_frame), left_other, rights, rights_other, 4 * n_ff)
    ff_sum = scatter_plane(ff_grad)
    grad_low = grad_frame.astype(BF)
    gathered_down = gather_rows_p(grad_low)
    a_rights = jnp.stack([d_order(t_na), d_order(m_low)])
    a_rights_other = swap_dp(a_rights, 1)
    a_other = swap_dp(a_left, 1)
    gathered_down = after(gathered_down, ff_grad)
    grad_hidden = dot_nt(gathered_down, w_down)
    grad_pre = jax.vjp(activate, hidden_pre)[1](grad_hidden)[0].astype(BF)
    part_c = dot_nt(grad_pre, w_up).astype(BF)
    grad_nb = shards_total(*scatter_rows_p(part_c))

    attn_grad = pair_grad(ids, after(a_left, part_c), a_other, a_rights, a_rights_other, 3 * n_attn * parts)
    f_left = jnp.concatenate([hidden, grad_pre], axis=1)
    ff_same, ff_cross = frame_grad(
        ids, after(f_left, part_c), jnp.stack([d_order(gathered_down), d_order(gathered_b)]), n_ff
    )
    ff_cross = swap_dp(ff_cross, 1)
    grad_nb = after(grad_nb, attn_grad, ff_same)
    grad_middle, mid_low, f_db, pieces = frame_mid(
        ids, grad_nb, middle, grad_frame, gain_b32[None], w_out, out_w.held
    )
    gathered_mid = gather_rows_p(mid_low)
    grad_mixed = jnp.concatenate(
        by_xor_mp([pieces[0]] + [swap_mp(pieces[r], r) for r in range(1, parts)]), axis=0
    )
    grad_qkv = jnp.concatenate(frame_backward(qkv_rows, log_total, grad_mixed, segment), axis=1)
    w_all = jnp.concatenate([w_qkv[0], w_qkv[1], w_qkv[2]], axis=1)
    part_d32 = dot_nt(grad_qkv, w_all)
    part_d = after(part_d32.astype(BF), ff_sum, gathered_mid)
    attn_sum = scatter_plane(after(attn_grad, ff_sum))
    attn_same, attn_cross = frame_grad(
        ids,
        jnp.concatenate([grad_qkv, mixed_rows], axis=1),
        jnp.stack([d_order(gathered_a), d_order(gathered_mid)]),
        3 * n_attn,
    )
    attn_cross = swap_dp(attn_cross, 1)
    part_d = after(part_d, attn_same)
    f_ff_value = (ff_same.astype(F32) + ff_cross.astype(F32)).astype(BF)
    f_attn_value = (attn_same.astype(F32) + attn_cross.astype(F32)).astype(BF)
    na_parts = scatter_rows_p(part_d)
    ff_z = scatter_shards(ff_sum, n_ff, part_d)
    f_ff_parts = plane_parts(f_ff_value, part_d)
    f_attn_parts = plane_parts(f_attn_value, part_d)
    grad_na = shards_total(*na_parts)
    first = jax.vjp(normalize, stream, gain_a32)[1](grad_na)
    frames_grad = grad_middle + first[0]
    attn_z = scatter_shards(after(attn_sum, grad_na), n_attn)
    f_da = jnp.sum(part_d32 * gathered_a.astype(F32), axis=0) / gain_a32

    wide = lax.dynamic_update_slice_in_dim(
        jnp.zeros((parts, n_ff), F32), jnp.sum(grad_pre.astype(F32), axis=0)[None], z, 0
    )

    def by_owner(full):
        return jnp.transpose(full.reshape(dp, parts, -1), (1, 0, 2)).reshape(parts, -1)

    vec = jnp.concatenate(
        [
            jnp.stack([f_da, f_db[0], jnp.sum(grad_frame, axis=0), t_da[0], t_db[0], t_dbd]),
            by_owner(wide),
            by_owner(t_gbup[0]),
        ],
        axis=0,
    )
    vec = d_order(after(vec, part_d))
    vec = jnp.concatenate(by_xor([vec[:, i * block : (i + 1) * block] for i in range(INNER)]), axis=1)
    for bit in (4, 2, 1):
        half = vec.shape[1] // 2
        vec = vec[:, :half] + swap_dp(vec[:, half:], bit)
    vec = outer_sum(vec, 1)
    width = vec.shape[1]
    quarter = width // parts
    rows = by_xor_mp(
        [
            jnp.concatenate(
                [vec[:6, i * quarter : (i + 1) * quarter].reshape(-1), vec[6 + i], vec[6 + parts + i]]
            )
            for i in range(parts)
        ]
    )
    mine = rows[0] + sum(swap_mp(rows[r], r) for r in (1, 2, 3))
    vectors = [mine[i * quarter : (i + 1) * quarter] for i in range(6)]
    f_bup, t_bup_grad = mine[6 * quarter : 6 * quarter + width], mine[6 * quarter + width :]

    t_ff = shards_total(*ff_z, mine)
    f_ff = shards_total(*f_ff_parts, mine)

    def ff_split(total):
        return total[:, :n_ff].T, total[:, n_ff:]

    def attn_split(total):
        rows = total.reshape(block, 4, n_attn)
        return jnp.transpose(rows[:, :3], (1, 0, 2)), total[:, 3 * n_attn :].T

    t_down_grad, t_up_grad = ff_split(t_ff)
    f_down_grad, f_up_grad = ff_split(f_ff)
    f_qkv_grad, f_out_grad = attn_split(shards_total(*f_attn_parts, mine))
    t_qkv_grad, t_out_grad = attn_split(shards_total(*attn_z, t_ff))

    def owned(qkv_grad, out_grad, up_grad, down_grad):
        return (
            outer_sum(qkv_grad, 1),
            outer_sum(out_grad, 1),
            outer_sum(up_grad, 0),
            outer_sum(down_grad, 1),
        )

    f = owned(f_qkv_grad, f_out_grad, f_up_grad, f_down_grad)
    t = owned(t_qkv_grad, t_out_grad, t_up_grad, t_down_grad)
    return (
        output,
        frames_grad,
        vectors[0],
        f[0],
        f[1],
        vectors[1],
        f[2],
        f_bup,
        f[3],
        vectors[2],
        vectors[3],
        t[0],
        t[1],
        vectors[4],
        t[2],
        t_bup_grad,
        t[3],
        vectors[5],
    )


def solution(mesh):
    rows = P(("dp", "mp"), None)
    block = (
        P(),
        P(None, None, "mp"),
        P("mp", None),
        P(),
        P(None, "mp"),
        P("mp"),
        P("mp", None),
        P(),
    )
    vec = P(("dp", "mp"))
    block_out = (
        vec,
        P(None, "dp", "mp"),
        P("mp", "dp"),
        vec,
        P("dp", "mp"),
        vec,
        P("mp", "dp"),
        vec,
    )
    return jax.shard_map(
        shards,
        mesh=mesh,
        in_specs=(rows, rows, P("dp", None), rows) + block + block,
        out_specs=(rows, rows) + block_out + block_out,
        check_vma=False,
    )
```

time: 539 us -> 533 us (0.989)
  Pallas kernels: 143 us -> 102 us
  starting transfers between devices: 74 us -> 97.4 us
  local copies, waits for them, and re-layouts: 33.9 us -> 55 us
  waiting for transfers between devices: 196 us -> 180 us
  other arithmetic: 37.8 us -> 48.3 us
    pallas_call x10 -> x2, Pallas kernels: 62.4 us -> 25.4 us  [pair_grad(): pl.pallas_call(functools.partial(pair_grad_kernel, lambda j: (j == 0) | (...]
    ppermute x16 -> x36, starting transfers between devices: 28.5 us -> 50 us  [swap_mp(): return lax.ppermute(value, 'mp', [(i, i ^ mask) for i in range(size)])]
    ppermute x16 -> x36, waiting for transfers between devices: 106 us -> 89.3 us  [swap_mp(): return lax.ppermute(value, 'mp', [(i, i ^ mask) for i in range(size)])]
    ppermute x2 -> x3, waiting for transfers between devices: 0.01 us -> 10.6 us  [shards(): outer = lax.ppermute(after(far, *then), 'mp', [(2, 3), (1, 0)])]
    ppermute x41 -> x39, waiting for transfers between devices: 77.1 us -> 67.4 us  [swap_dp(): return lax.ppermute(value, 'dp', [(i, i ^ bit) for i in range(size)])]
    unnamed x136 -> x154, local copies, waits for them, and re-layouts: 13.7 us -> 21 us
    add x0 -> x5, other arithmetic: none -> 6.84 us  [shards_total(): own.astype(F32) + sent[0].astype(F32) + sent[1].astype(F32)]
    dynamic_slice x0 -> x7, local copies, waits for them, and re-layouts: none -> 6.16 us  [the longest x2 2.41 us: cut(): lax.dynamic_slice_in_dim(value, (4 * i + at) * n, n, 1)]
  transfers between devices with their start and end apart: 69 -> 86, of which waited for: 26 -> 36; matrix products, arithmetic and copies ran while one was open for 13% -> 19% of each run, Pallas kernels for 21% -> 11%
where the time goes in v3:
time: 533 us; the launch traced here: 523 us
  waiting for transfers between devices  180 us (34%)
  Pallas kernels  102 us (19%)
  starting transfers between devices  97.4 us (18%)
  local copies, waits for them, and re-layouts  55 us (10%)
  other arithmetic  48.3 us (9%)
  matrix products  24.5 us (5%)
  between operations  15.7 us (3%)
    ppermute x36, waiting for transfers between devices, swap_mp(): return lax.ppermute(value, 'mp', [(i, i ^ mask) for i in range(size)])  89.3 us
    ppermute x39, waiting for transfers between devices, swap_dp(): return lax.ppermute(value, 'dp', [(i, i ^ bit) for i in range(size)])  67.4 us
    pallas_call x5, Pallas kernels, call(): pl.pallas_call(kernel, out_shape=outs, in_specs=[pl.BlockSpec(memory_spac...  63.4 us
    ppermute x36, starting transfers between devices, swap_mp(): return lax.ppermute(value, 'mp', [(i, i ^ mask) for i in range(size)])  50 us
    ppermute x39, starting transfers between devices, swap_dp(): return lax.ppermute(value, 'dp', [(i, i ^ bit) for i in range(size)])  28.4 us
    pallas_call x2, Pallas kernels, pair_grad(): pl.pallas_call(functools.partial(pair_grad_kernel, lambda j: (j == 0) | (...  25.4 us
    unnamed x154, local copies, waits for them, and re-layouts  21 us
    pallas_call x2, Pallas kernels, frame_grad(): pl.pallas_call(functools.partial(frame_grad_kernel, lambda j: (j == 0) |...  13.5 us
  transfers between devices with their start and end apart: 86, of which 36 were waited for; matrix products, arithmetic and copies ran while one was open for 19% of the time, Pallas kernels for 11%

profile of v3, /device:TPU:8, one launch (start us, length us, event | category | flops | bytes accessed | tf_op | source)
XLA Modules:
  0.0 522.8 jit_solution(3786181444576567897)
XLA Ops:
  40.4 4.6 collective-permute-start.15
  46.8 7.6 %collective-permute-done.14 = bf16[4,32,1024]{2,1,0:T(8,128)(2,1)S(1)} collective-permute-done((bf16[4,32,1024]{2,1,0:T(8,128)(2,1)}, bf16[4,32,1024]{2,1,0:T(8,128)(2,1)S(1)}, u32[]{:S(2)}, u32[]{:S(2)}) %collective-permute-start.14) | collective-permute-done | bytes 262176 | tf_op jit(solution)/shard_map/ppermute | solution.py:85
  89.8 14.8 %collective-permute-done.24 = bf16[2,128,1024]{2,1,0:T(8,128)(2,1)} collective-permute-done((bf16[2,128,1024]{2,1,0:T(8,128)(2,1)}, bf16[2,128,1024]{2,1,0:T(8,128)(2,1)}, u32[]{:S(2)}, u32[]{:S(2)}) %collective-permute-start.24) | collective-permute-done | bytes 524320 | tf_op jit(solution)/shard_map/ppermute | solution.py:57
  104.6 5.0 collective-permute-start.26
  115.9 10.3 %collective-permute-done.26 = bf16[2,128,1024]{2,1,0:T(8,128)(2,1)} collective-permute-done((bf16[2,128,1024]{2,1,0:T(8,128)(2,1)}, bf16[2,128,1024]{2,1,0:T(8,128)(2,1)}, u32[]{:S(2)}, u32[]{:S(2)}) %collective-permute-start.26) | collective-permute-done | bytes 524320 | tf_op jit(solution)/shard_map/ppermute | solution.py:86
  137.8 10.0 %collective-permute-done.27 = bf16[2,384,512]{2,1,0:T(8,128)(2,1)} collective-permute-done((bf16[2,384,512]{2,1,0:T(8,128)(2,1)S(1)}, bf16[2,384,512]{2,1,0:T(8,128)(2,1)}, u32[]{:S(2)}, u32[]{:S(2)}) %collective-permute-start.27) | collective-permute-done | bytes 786464 | tf_op jit(solution)/shard_map/ppermute | solution.py:52
  169.0 23.0 %collective-permute-done.33.rest_1_ = bf16[2,768,512]{2,1,0:T(8,128)(2,1)} collective-permute-done((bf16[2,768,512]{2,1,0:T(8,128)(2,1)}, bf16[2,768,512]{2,1,0:T(8,128)(2,1)}, u32[]{:S(2)}, u32[]{:S(2)}) %collective-permute-start.33) | collective-permute-done | bytes 1572896 | tf_op jit(solution)/shard_map/ppermute | solution.py:52
  192.0 4.4 collective-permute-done.34.rest_5_
  210.3 12.4 %shard_map.332 = (f32[384,1024]{1,0:T(8,128)}, bf16[384,1024]{1,0:T(8,128)(2,1)}, bf16[384,1024]{1,0:T(8,128)(2,1)}, bf16[384,1024]{1,0:T(8,128)(2,1)}, bf16[384...) custom-call(s32[2]{0:T(128)} %pad_add_fusion.ids, ...), custom_call_target="tpu_custom_call" | custom-call | flops 3221225472 | bytes 19800584 | tf_op jit(solution)/shard_map/pallas_call | solution.py:560
  222.8 27.3 %shard_map.333 = (bf16[384,1024]{1,0:T(8,128)(2,1)}, f32[384,1024]{1,0:T(8,128)}, bf16[384,8192]{1,0:T(8,128)(2,1)}, f32[1,4096]{1,0:T(1,128)}) custom-call(s32[2]{0:T(128)} %pad_add_fusion.ids, bf16[384,1024]{1,0:T(8,128)(2,1)} %get-tuple-element.156.nb, bf16[384,1024]{1,0:T(8,128)(2,1)} %get-tuple-element.157.g, f32[384,1024]{1,0:T(8,128)} %get-tuple-element.158.mid, ...), custom_call_target="tpu_custom_call" | custom-call | flops 12884901888 | bytes 28611080 | tf_op jit(solution)/shard_map/pallas_call | solution.py:560
  252.0 14.6 %shard_map.334 = (bf16[384,1024]{1,0:T(8,128)(2,1)}, bf16[384,4096]{1,0:T(8,128)(2,1)}, f32[128,1024]{1,0:T(8,128)}, f32[1,1024]{1,0:T(1,128)}, f32[1,1024]{1,0:T(1,128)}) custom-call(s32[2]{0:T(128)} %pad_add_fusion.ids, bf16[384,1024]{1,0:T(8,128)(2,1)} %get-tuple-element.157.g, f32[384,1024]{1,0:T(8,128)} %get-tuple-element.164.gnb, ...), custom_call_target="tpu_custom_call" | custom-call | flops 3221225472 | bytes 22167560 | tf_op jit(solution)/shard_map/pallas_call | solution.py:560
  267.8 15.7 %shard_map.335 = bf16[512,8192]{1,0:T(8,128)(2,1)} custom-call(s32[2]{0:T(128)} %pad_add_fusion.ids, bf16[384,8192]{1,0:T(8,128)(2,1)} %get-tuple-element.173.lm, bf16[384,8192]{1,0:T(8,128)(2,1)} %collective-permute-done.45.lt, bf16[2,384,1024]{2,1,0:T(8,128)(2,1)} %pad_maximum_fusion.3.rm, bf16[2,384,1024]{2,1,0:T(8,128)(2,1)} %copy-done.19), custom_call_target="tpu_custom_call" | custom-call | flops 6442450944 | bytes 24117248 | tf_op jit(solution)/shard_map/pallas_call | solution.py:669
  290.8 15.2 %collective-permute-done.42 = bf16[128,1024]{1,0:T(8,128)(2,1)} collective-permute-done((bf16[128,1024]{1,0:T(8,128)(2,1)}, bf16[128,1024]{1,0:T(8,128)(2,1)}, u32[]{:S(2)}, u32[]{:S(2)}) %collective-permute-start.42) | collective-permute-done | bytes 262176 | tf_op jit(solution)/shard_map/ppermute | solution.py:57
  323.9 7.6 %shard_map.337 = (bf16[512,2048]{1,0:T(8,128)(2,1)}, bf16[512,2048]{1,0:T(8,128)(2,1)}) custom-call(s32[2]{0:T(128)} %pad_add_fusion.ids, bf16[512,2048]{1,0:T(8,128)(2,1)} %pad_maximum_fusion.left, bf16[2,512,1024]{2,1,0:T(8,128)(2,1)} %pad_maximum_fusion.1.right), custom_call_target="tpu_custom_call" | custom-call | flops 2147483648 | bytes 8388608 | tf_op jit(solution)/shard_map/pallas_call | solution.py:690
  331.5 9.8 %shard_map.336 = bf16[512,4096]{1,0:T(8,128)(2,1)} custom-call(s32[2]{0:T(128)} %pad_add_fusion.ids, bf16[384,4096]{1,0:T(8,128)(2,1)} %get-tuple-element.179.lm, bf16[384,4096]{1,0:T(8,128)(2,1)} %collective-permute-done.50.lt, bf16[2,384,1024]{2,1,0:T(8,128)(2,1)} %copy-done.8, bf16[2,384,1024]{2,1,0:T(8,128)(2,1)} %collective-permute-done.51.rt), custom_call_target="tpu_custom_call" | custom-call | flops 3221225472 | bytes 13631488 | tf_op jit(solution)/shard_map/pallas_call | solution.py:669
  345.7 4.8 shard_map.338
  370.9 4.9 collective-permute-done.55
  382.2 5.9 %shard_map.339 = (bf16[512,1024]{1,0:T(8,128)(2,1)}, bf16[512,1024]{1,0:T(8,128)(2,1)}) custom-call(s32[2]{0:T(128)} %pad_add_fusion.ids, bf16[512,1024]{1,0:T(8,128)(2,1)} %pad_maximum_fusion.7.left, bf16[2,512,1024]{2,1,0:T(8,128)(2,1)} %pad_maximum_fusion.2.right), custom_call_target="tpu_custom_call" | custom-call | flops 1073741824 | bytes 5242880 | tf_op jit(solution)/shard_map/pallas_call | solution.py:690
  436.4 6.0 %collective-permute-start.78 = (bf16[128,2048]{1,0:T(8,128)(2,1)}, bf16[128,2048]{1,0:T(8,128)(2,1)}, u32[]{:S(2)}, u32[]{:S(2)}) collective-permute-start(bf16[128,2048]{1,0:T(8,128)(2,1)} %pad_maximum_fusion.11), channel_id=1, source_target_pairs={{0,1},{1,0},{2,3},{3,2},{4,5},{5,4},{6,7},{7,6},{8,9},{9,8},{10,11... | collective-permute-start | bytes 1572872 | tf_op jit(solution)/shard_map/ppermute | solution.py:57
  449.3 9.8 %collective-permute-done.72 = bf16[128,2048]{1,0:T(8,128)(2,1)} collective-permute-done((bf16[128,2048]{1,0:T(8,128)(2,1)}, bf16[128,2048]{1,0:T(8,128)(2,1)}, u32[]{:S(2)}, u32[]{:S(2)}) %collective-permute-start.72) | collective-permute-done | bytes 524320 | tf_op jit(solution)/shard_map/ppermute | solution.py:52
  460.5 8.8 %collective-permute-done.73 = bf16[128,2048]{1,0:T(8,128)(2,1)} collective-permute-done((bf16[128,2048]{1,0:T(8,128)(2,1)}, bf16[128,2048]{1,0:T(8,128)(2,1)}, u32[]{:S(2)}, u32[]{:S(2)}) %collective-permute-start.73) | collective-permute-done | bytes 524320 | tf_op jit(solution)/shard_map/ppermute | solution.py:52
  474.2 12.5 %collective-permute-done.80 = bf16[128,2048]{1,0:T(8,128)(2,1)S(1)} collective-permute-done((bf16[128,2048]{1,0:T(8,128)(2,1)S(1)}, bf16[128,2048]{1,0:T(8,128)(2,1)S(1)}, u32[]{:S(2)}, u32[]{:S(2)}) %collective-permute-start.80) | collective-permute-done | bytes 524320 | tf_op jit(solution)/shard_map/ppermute | solution.py:57
  499.1 8.8 %collective-permute-done.76 = bf16[128,1024]{1,0:T(8,128)(2,1)} collective-permute-done((bf16[128,1024]{1,0:T(8,128)(2,1)S(1)}, bf16[128,1024]{1,0:T(8,128)(2,1)}, u32[]{:S(2)}, u32[]{:S(2)}) %collective-permute-start.76) | collective-permute-done | bytes 262176 | tf_op jit(solution)/shard_map/ppermute | solution.py:57
  507.9 5.0 collective-permute-done.77
  (467 shorter events, 258.3 us)
Async XLA Ops:
  7.2 49.7 %all-gather.3.cloned.1.call-start = ((), (), s32[]{:S(2)}) async-start(), calls=%async_computation.3 | async-start | bytes 1310720 | tf_op jit(solution)/shard_map/all_gather | solution.py:38
  18.9 27.8 %collective-permute-start.12 = (bf16[4,32,1024]{2,1,0:T(8,128)(2,1)}, bf16[4,32,1024]{2,1,0:T(8,128)(2,1)}, u32[]{:S(2)}, u32[]{:S(2)}) collective-permute-start(bf16[4,32,1024]{2,1,0:T(8,128)(2,1)} %pad_maximum_fusion.16), channel_id=1, source_target_pairs={{0,1},{1,0},{2,3},{3,2},{4,5},{5,4},{6,7},{7,6},{8,9},{9,8},{10,11... | collective-permute-start | bytes 786440 | tf_op jit(solution)/shard_map/ppermute | solution.py:57
  23.4 114.4 %all-gather.5.cloned.1.call-start = ((), (), s32[]{:S(2)}) async-start(), calls=%async_computation.4 | async-start | bytes 1310720 | tf_op jit(solution)/shard_map/all_gather | solution.py:38
  82.5 27.1 %collective-permute-start.19 = (bf16[4,96,512]{2,1,0:T(8,128)(2,1)S(1)}, bf16[4,96,512]{2,1,0:T(8,128)(2,1)}, u32[]{:S(2)}, u32[]{:S(2)}) collective-permute-start(bf16[4,96,512]{2,1,0:T(8,128)(2,1)S(1)} %pad_maximum_fusion.14), channel_id=1, source_target_pairs={{0,8},{4,12},{8,0},{12,4},{16,24},{20,28},{24,16},{28,20},{1,9},{5... | collective-permute-start | bytes 1179656 | tf_op jit(solution)/shard_map/ppermute | solution.py:52
  84.1 28.2 %collective-permute-start.21 = (bf16[4,96,512]{2,1,0:T(8,128)(2,1)S(1)}, bf16[4,96,512]{2,1,0:T(8,128)(2,1)}, u32[]{:S(2)}, u32[]{:S(2)}) collective-permute-start(bf16[4,96,512]{2,1,0:T(8,128)(2,1)S(1)} %pad_maximum_fusion.15), channel_id=1, source_target_pairs={{0,16},{4,20},{8,24},{12,28},{16,0},{20,4},{24,8},{28,12},{1,17},{... | collective-permute-start | bytes 1179656 | tf_op jit(solution)/shard_map/ppermute | solution.py:52
  85.7 29.2 %collective-permute-start.23 = (bf16[2,128,1024]{2,1,0:T(8,128)(2,1)}, bf16[2,128,1024]{2,1,0:T(8,128)(2,1)}, u32[]{:S(2)}, u32[]{:S(2)}) collective-permute-start(bf16[2,128,1024]{2,1,0:T(8,128)(2,1)} %pad_maximum_fusion.10), channel_id=1, source_target_pairs={{0,1},{1,0},{2,3},{3,2},{4,5},{5,4},{6,7},{7,6},{8,9},{9,8},{10,11... | collective-permute-start | bytes 1572872 | tf_op jit(solution)/shard_map/ppermute | solution.py:57
  87.5 28.3 %collective-permute-start.25 = (bf16[2,128,1024]{2,1,0:T(8,128)(2,1)}, bf16[2,128,1024]{2,1,0:T(8,128)(2,1)}, u32[]{:S(2)}, u32[]{:S(2)}) collective-permute-start(bf16[2,128,1024]{2,1,0:T(8,128)(2,1)} %pad_maximum_fusion.10), channel_id=1, source_target_pairs={{1,2},{2,1},{5,6},{6,5},{9,10},{10,9},{13,14},{14,13},{17,18},{18,... | collective-permute-start | bytes 1572872 | tf_op jit(solution)/shard_map/ppermute | solution.py:85
  109.6 96.4 %reduce-scatter.4.cloned.1.call-start = ((), (), s32[]{:S(2)}) async-start(), calls=%async_computation.5 | async-start | bytes 1310720 | tf_op jit(solution)/shard_map/reduce_scatter | solution.py:42
  158.3 33.7 %collective-permute-start.33 = (bf16[2,768,512]{2,1,0:T(8,128)(2,1)}, bf16[2,768,512]{2,1,0:T(8,128)(2,1)}, u32[]{:S(2)}, u32[]{:S(2)}) collective-permute-start(bf16[2,768,512]{2,1,0:T(8,128)(2,1)} %constant_dynamic-update-slice_fusion.8.rest_0_), channel_id=1, source_target_pairs={{0,16},{4,20},{8,24},{12,28},{16,0},{20,4},{24,8},{28,12},{1,17},{... | collective-permute-start | bytes 4718600 | tf_op jit(solution)/shard_map/ppermute | solution.py:52
  163.1 33.4 %collective-permute-start.34 = (bf16[2,768,512]{2,1,0:T(8,128)(2,1)}, bf16[2,768,512]{2,1,0:T(8,128)(2,1)}, u32[]{:S(2)}, u32[]{:S(2)}) collective-permute-start(bf16[2,768,512]{2,1,0:T(8,128)(2,1)} %constant_dynamic-update-slice_fusion.10.rest_4_), channel_id=1, source_target_pairs={{0,8},{4,12},{8,0},{12,4},{16,24},{20,28},{24,16},{28,20},{1,9},{5... | collective-permute-start | bytes 4718600 | tf_op jit(solution)/shard_map/ppermute | solution.py:52
  164.6 226.5 %reduce-scatter.6.cloned.1.call-start = ((), (), s32[]{:S(2)}) async-start(), calls=%async_computation.6 | async-start | bytes 10485760 | tf_op jit(solution)/shard_map/reduce_scatter | solution.py:180
  164.8 35.2 %collective-permute-start.29 = (bf16[4,192,512]{2,1,0:T(8,128)(2,1)}, bf16[4,192,512]{2,1,0:T(8,128)(2,1)}, u32[]{:S(2)}, u32[]{:S(2)}) collective-permute-start(bf16[4,192,512]{2,1,0:T(8,128)(2,1)} %copy-done.17), channel_id=1, source_target_pairs={{0,4},{4,0},{8,12},{12,8},{16,20},{20,16},{24,28},{28,24},{1,5},{5... | collective-permute-start | bytes 2359304 | tf_op jit(solution)/shard_map/ppermute | solution.py:52
  164.9 35.7 %collective-permute-start.30 = (bf16[4,192,512]{2,1,0:T(8,128)(2,1)}, bf16[4,192,512]{2,1,0:T(8,128)(2,1)}, u32[]{:S(2)}, u32[]{:S(2)}) collective-permute-start(bf16[4,192,512]{2,1,0:T(8,128)(2,1)} %copy-done.34), channel_id=1, source_target_pairs={{0,4},{4,0},{8,12},{12,8},{16,20},{20,16},{24,28},{28,24},{1,5},{5... | collective-permute-start | bytes 2359304 | tf_op jit(solution)/shard_map/ppermute | solution.py:52
  169.0 32.6 %collective-permute-start.31 = (bf16[4,192,512]{2,1,0:T(8,128)(2,1)}, bf16[4,192,512]{2,1,0:T(8,128)(2,1)}, u32[]{:S(2)}, u32[]{:S(2)}) collective-permute-start(bf16[4,192,512]{2,1,0:T(8,128)(2,1)} %copy-done.18), channel_id=1, source_target_pairs={{0,4},{4,0},{8,12},{12,8},{16,20},{20,16},{24,28},{28,24},{1,5},{5... | collective-permute-start | bytes 2359304 | tf_op jit(solution)/shard_map/ppermute | solution.py:52
  283.5 204.7 %reduce-scatter.8.cloned.1.call-start = ((), (), s32[]{:S(2)}) async-start(), calls=%async_computation.7 | async-start | bytes 5242880 | tf_op jit(solution)/shard_map/reduce_scatter | solution.py:180
  283.6 47.9 %collective-permute-start.50 = (bf16[384,4096]{1,0:T(8,128)(2,1)}, bf16[384,4096]{1,0:T(8,128)(2,1)}, u32[]{:S(2)}, u32[]{:S(2)}) collective-permute-start(bf16[384,4096]{1,0:T(8,128)(2,1)} %get-tuple-element.179.lm), channel_id=1, source_target_pairs={{0,4},{4,0},{8,12},{12,8},{16,20},{20,16},{24,28},{28,24},{1,5},{5... | collective-permute-start | bytes 9437192 | tf_op jit(solution)/shard_map/ppermute | solution.py:52
  290.7 40.8 %collective-permute-start.51 = (bf16[2,384,1024]{2,1,0:T(8,128)(2,1)S(1)}, bf16[2,384,1024]{2,1,0:T(8,128)(2,1)}, u32[]{:S(2)}, u32[]{:S(2)}) collective-permute-start(bf16[2,384,1024]{2,1,0:T(8,128)(2,1)S(1)} %pad_maximum_fusion.4.rm), channel_id=1, source_target_pairs={{0,4},{4,0},{8,12},{12,8},{16,20},{20,16},{24,28},{28,24},{1,5},{5... | collective-permute-start | bytes 4718600 | tf_op jit(solution)/shard_map/ppermute | solution.py:52
  355.0 41.7 %collective-permute-start.71 = (bf16[512,2048]{1,0:T(8,128)(2,1)}, bf16[512,2048]{1,0:T(8,128)(2,1)}, u32[]{:S(2)}, u32[]{:S(2)}) collective-permute-start(bf16[512,2048]{1,0:T(8,128)(2,1)} %get-tuple-element.204), channel_id=1, source_target_pairs={{0,4},{4,0},{8,12},{12,8},{16,20},{20,16},{24,28},{28,24},{1,5},{5... | collective-permute-start | bytes 6291464 | tf_op jit(solution)/shard_map/ppermute | solution.py:52
  428.4 30.6 %collective-permute-start.72 = (bf16[128,2048]{1,0:T(8,128)(2,1)}, bf16[128,2048]{1,0:T(8,128)(2,1)}, u32[]{:S(2)}, u32[]{:S(2)}) collective-permute-start(bf16[128,2048]{1,0:T(8,128)(2,1)} %get-tuple-element.296), channel_id=1, source_target_pairs={{0,8},{4,12},{8,0},{12,4},{16,24},{20,28},{24,16},{28,20},{1,9},{5... | collective-permute-start | bytes 1572872 | tf_op jit(solution)/shard_map/ppermute | solution.py:52
  433.3 35.9 %collective-permute-start.73 = (bf16[128,2048]{1,0:T(8,128)(2,1)}, bf16[128,2048]{1,0:T(8,128)(2,1)}, u32[]{:S(2)}, u32[]{:S(2)}) collective-permute-start(bf16[128,2048]{1,0:T(8,128)(2,1)} %get-tuple-element.295), channel_id=1, source_target_pairs={{0,16},{4,20},{8,24},{12,28},{16,0},{20,4},{24,8},{28,12},{1,17},{... | collective-permute-start | bytes 1572872 | tf_op jit(solution)/shard_map/ppermute | solution.py:52
  434.9 35.7 %collective-permute-start.74 = (bf16[128,2048]{1,0:T(8,128)(2,1)}, bf16[128,2048]{1,0:T(8,128)(2,1)}, u32[]{:S(2)}, u32[]{:S(2)}) collective-permute-start(bf16[128,2048]{1,0:T(8,128)(2,1)} %get-tuple-element.294), channel_id=1, source_target_pairs={{0,24},{4,28},{8,16},{12,20},{16,8},{20,12},{24,0},{28,4},{1,25},{... | collective-permute-start | bytes 1572872 | tf_op jit(solution)/shard_map/ppermute | solution.py:52
  436.4 37.8 %collective-permute-start.78 = (bf16[128,2048]{1,0:T(8,128)(2,1)}, bf16[128,2048]{1,0:T(8,128)(2,1)}, u32[]{:S(2)}, u32[]{:S(2)}) collective-permute-start(bf16[128,2048]{1,0:T(8,128)(2,1)} %pad_maximum_fusion.11), channel_id=1, source_target_pairs={{0,1},{1,0},{2,3},{3,2},{4,5},{5,4},{6,7},{7,6},{8,9},{9,8},{10,11... | collective-permute-start | bytes 1572872 | tf_op jit(solution)/shard_map/ppermute | solution.py:57
  442.4 31.8 %collective-permute-start.79 = (bf16[128,2048]{1,0:T(8,128)(2,1)}, bf16[128,2048]{1,0:T(8,128)(2,1)}, u32[]{:S(2)}, u32[]{:S(2)}) collective-permute-start(bf16[128,2048]{1,0:T(8,128)(2,1)} %pad_maximum_fusion.12), channel_id=1, source_target_pairs={{0,2},{1,3},{2,0},{3,1},{4,6},{5,7},{6,4},{7,5},{8,10},{9,11},{10,... | collective-permute-start | bytes 1572872 | tf_op jit(solution)/shard_map/ppermute | solution.py:57
  459.0 27.6 %collective-permute-start.80 = (bf16[128,2048]{1,0:T(8,128)(2,1)S(1)}, bf16[128,2048]{1,0:T(8,128)(2,1)S(1)}, u32[]{:S(2)}, u32[]{:S(2)}) collective-permute-start(bf16[128,2048]{1,0:T(8,128)(2,1)S(1)} %copy-done.40), channel_id=1, source_target_pairs={{0,3},{1,2},{2,1},{3,0},{4,7},{5,6},{6,5},{7,4},{8,11},{9,10},{10,... | collective-permute-start | bytes 1572872 | tf_op jit(solution)/shard_map/ppermute | solution.py:57
  (132 other events, 1808.0 us)
Sparse Core Ops, SparseCore 0:
  23.5 32.3 all-gather.2
  109.7 28.0 all-gather.4
  164.7 23.6 reduce-scatter.3
  283.6 85.5 reduce-scatter.5
  391.2 69.4 reduce-scatter.7

commit v4 on v3

--- a/solution.py
+++ b/solution.py
@@ -525,14 +525,15 @@
     out[...] = dot_nn(am[...], jnp.concatenate([lm[...], lt[...]], axis=0)).astype(BF)
 
 
-def frame_grad_kernel(new, ids, left, right, same, cross, tmp, am):
-    d = right.shape[2]
-
-    @pl.when(new(pl.program_id(0)))
-    def _():
-        tmp[...] = jnp.transpose(right[0])
-        for i in range(2):
-            lay_right(am, i * (d // 2), 0, tmp, (ids[0] & 1) ^ i, d // INNER)
+def frame_grad_kernel(second, ids, left, right0, right1, same, cross, tmp, am):
+    d = right0.shape[1]
+    for first, right in ((0, right0), (second, right1)):
+
+        @pl.when(pl.program_id(0) == first)
+        def _(right=right):
+            tmp[...] = jnp.transpose(right[...])
+            for i in range(2):
+                lay_right(am, i * (d // 2), 0, tmp, (ids[0] & 1) ^ i, d // INNER)
 
     total = dot_nn(am[...], left[...])
     same[...] = total[: d // 2].astype(BF)
@@ -683,24 +684,21 @@
 
 def frame_grad(ids, left, rights, split):
     rows, units = left.shape
-    d = rights.shape[2]
+    d = rights[0].shape[1]
     step = units // 4
-    at = split // step
     outs = [arr((d // 2, units), BF)] * 2
+    ins = [left, *rights]
     return pl.pallas_call(
-        functools.partial(frame_grad_kernel, lambda j: (j == 0) | (j == at)),
+        functools.partial(frame_grad_kernel, split // step),
         grid=(4,),
-        in_specs=[
-            smem_spec(),
-            pl.BlockSpec((rows, step), lambda j: (0, j)),
-            pl.BlockSpec((1, rows, d), lambda j: (jnp.where(j < at, 0, 1), 0, 0)),
-        ],
+        in_specs=[smem_spec(), pl.BlockSpec((rows, step), lambda j: (0, j))]
+        + [pl.BlockSpec((rows, d), lambda j: (0, 0))] * 2,
         out_specs=[pl.BlockSpec((d // 2, step), lambda j: (0, j))] * 2,
         out_shape=outs,
         scratch_shapes=[pltpu.VMEM((d, rows), BF)] * 2,
         compiler_params=pltpu.CompilerParams(vmem_limit_bytes=VMEM_LIMIT),
-        cost_estimate=cost(2 * rows * units * d, [left, rights], outs),
-    )(ids, left, rights)
+        cost_estimate=cost(2 * rows * units * d, ins, outs),
+    )(ids, *ins)
 
 
 def segments(lengths, whole_rows):
@@ -855,7 +853,7 @@
     attn_grad = pair_grad(ids, after(a_left, part_c), a_other, a_rights, a_rights_other, 3 * n_attn * parts)
     f_left = jnp.concatenate([hidden, grad_pre], axis=1)
     ff_same, ff_cross = frame_grad(
-        ids, after(f_left, part_c), jnp.stack([d_order(gathered_down), d_order(gathered_b)]), n_ff
+        ids, after(f_left, part_c), [d_order(gathered_down), d_order(gathered_b)], n_ff
     )
     ff_cross = swap_dp(ff_cross, 1)
     grad_nb = after(grad_nb, attn_grad, ff_same)
@@ -870,11 +868,11 @@
     w_all = jnp.concatenate([w_qkv[0], w_qkv[1], w_qkv[2]], axis=1)
     part_d32 = dot_nt(grad_qkv, w_all)
     part_d = after(part_d32.astype(BF), ff_sum, gathered_mid)
-    attn_sum = scatter_plane(after(attn_grad, ff_sum))
+    attn_sum = scatter_plane(after(attn_grad, grad_mixed))
     attn_same, attn_cross = frame_grad(
         ids,
         jnp.concatenate([grad_qkv, mixed_rows], axis=1),
-        jnp.stack([d_order(gathered_a), d_order(gathered_mid)]),
+        [d_order(gathered_a), d_order(gathered_mid)],
         3 * n_attn,
     )
     attn_cross = swap_dp(attn_cross, 1)
@@ -926,8 +924,10 @@
     vectors = [mine[i * quarter : (i + 1) * quarter] for i in range(6)]
     f_bup, t_bup_grad = mine[6 * quarter : 6 * quarter + width], mine[6 * quarter + width :]
 
-    t_ff = shards_total(*ff_z, mine)
     f_ff = shards_total(*f_ff_parts, mine)
+    f_attn = shards_total(*f_attn_parts, mine)
+    t_attn = shards_total(*attn_z, f_ff, f_attn)
+    t_ff = shards_total(*ff_z, t_attn)
 
     def ff_split(total):
         return total[:, :n_ff].T, total[:, n_ff:]
@@ -938,8 +938,8 @@
 
     t_down_grad, t_up_grad = ff_split(t_ff)
     f_down_grad, f_up_grad = ff_split(f_ff)
-    f_qkv_grad, f_out_grad = attn_split(shards_total(*f_attn_parts, mine))
-    t_qkv_grad, t_out_grad = attn_split(shards_total(*attn_z, t_ff))
+    f_qkv_grad, f_out_grad = attn_split(f_attn)
+    t_qkv_grad, t_out_grad = attn_split(t_attn)
 
     def owned(qkv_grad, out_grad, up_grad, down_grad):
         return (

time: 533 us -> 530 us (level)
  waiting for transfers between devices: 180 us -> 173 us
    ppermute x39, waiting for transfers between devices: 67.4 us -> 51.1 us  [swap_dp(): return lax.ppermute(value, 'dp', [(i, i ^ bit) for i in range(size)])]
    ppermute x36, waiting for transfers between devices: 89.3 us -> 98.6 us  [swap_mp(): return lax.ppermute(value, 'mp', [(i, i ^ mask) for i in range(size)])]
    unnamed x154 -> x158, local copies, waits for them, and re-layouts: 21 us -> 22.9 us
  transfers between devices with their start and end apart: 86 -> 86, of which waited for: 36 -> 33; matrix products, arithmetic and copies ran while one was open for 19% -> 20% of each run, Pallas kernels for 11% -> 10%
where the time goes in v4:
time: 530 us; the launch traced here: 520 us
  waiting for transfers between devices  173 us (33%)
  Pallas kernels  102 us (19%)
  starting transfers between devices  96 us (18%)
  local copies, waits for them, and re-layouts  59.2 us (11%)
  other arithmetic  47.5 us (9%)
  matrix products  27 us (5%)
  between operations  15.7 us (3%)
    ppermute x36, waiting for transfers between devices, swap_mp(): return lax.ppermute(value, 'mp', [(i, i ^ mask) for i in range(size)])  98.6 us
    pallas_call x5, Pallas kernels, call(): pl.pallas_call(kernel, out_shape=outs, in_specs=[pl.BlockSpec(memory_spac...  63.3 us
    ppermute x39, waiting for transfers between devices, swap_dp(): return lax.ppermute(value, 'dp', [(i, i ^ bit) for i in range(size)])  51.1 us
    ppermute x36, starting transfers between devices, swap_mp(): return lax.ppermute(value, 'mp', [(i, i ^ mask) for i in range(size)])  47.7 us
    ppermute x39, starting transfers between devices, swap_dp(): return lax.ppermute(value, 'dp', [(i, i ^ bit) for i in range(size)])  29.3 us
    pallas_call x2, Pallas kernels, pair_grad(): pl.pallas_call(functools.partial(pair_grad_kernel, lambda j: (j == 0) | (...  25.4 us
    unnamed x158, local copies, waits for them, and re-layouts  22.9 us
    pallas_call x2, Pallas kernels, frame_grad(): pl.pallas_call(functools.partial(frame_grad_kernel, split // step), grid=...  13 us
  transfers between devices with their start and end apart: 86, of which 33 were waited for; matrix products, arithmetic and copies ran while one was open for 20% of the time, Pallas kernels for 10%

profile of v4, /device:TPU:8, one launch (start us, length us, event | category | flops | bytes accessed | tf_op | source)
XLA Modules:
  0.0 519.7 jit_solution(4400381451059491557)
XLA Ops:
  40.4 4.6 collective-permute-start.15
  46.8 7.6 %collective-permute-done.14 = bf16[4,32,1024]{2,1,0:T(8,128)(2,1)S(1)} collective-permute-done((bf16[4,32,1024]{2,1,0:T(8,128)(2,1)}, bf16[4,32,1024]{2,1,0:T(8,128)(2,1)S(1)}, u32[]{:S(2)}, u32[]{:S(2)}) %collective-permute-start.14) | collective-permute-done | bytes 262176 | tf_op jit(solution)/shard_map/ppermute | solution.py:85
  74.9 4.3 shard_map.331
  89.8 14.8 %collective-permute-done.24 = bf16[2,128,1024]{2,1,0:T(8,128)(2,1)} collective-permute-done((bf16[2,128,1024]{2,1,0:T(8,128)(2,1)}, bf16[2,128,1024]{2,1,0:T(8,128)(2,1)}, u32[]{:S(2)}, u32[]{:S(2)}) %collective-permute-start.24) | collective-permute-done | bytes 524320 | tf_op jit(solution)/shard_map/ppermute | solution.py:57
  104.6 5.0 collective-permute-start.26
  115.9 10.3 %collective-permute-done.26 = bf16[2,128,1024]{2,1,0:T(8,128)(2,1)} collective-permute-done((bf16[2,128,1024]{2,1,0:T(8,128)(2,1)}, bf16[2,128,1024]{2,1,0:T(8,128)(2,1)}, u32[]{:S(2)}, u32[]{:S(2)}) %collective-permute-start.26) | collective-permute-done | bytes 524320 | tf_op jit(solution)/shard_map/ppermute | solution.py:86
  137.9 10.0 %collective-permute-done.27 = bf16[2,384,512]{2,1,0:T(8,128)(2,1)} collective-permute-done((bf16[2,384,512]{2,1,0:T(8,128)(2,1)S(1)}, bf16[2,384,512]{2,1,0:T(8,128)(2,1)}, u32[]{:S(2)}, u32[]{:S(2)}) %collective-permute-start.27) | collective-permute-done | bytes 786464 | tf_op jit(solution)/shard_map/ppermute | solution.py:52
  147.9 4.2 multiply_convert_fusion.1
  169.1 23.0 %collective-permute-done.33.rest_1_ = bf16[2,768,512]{2,1,0:T(8,128)(2,1)} collective-permute-done((bf16[2,768,512]{2,1,0:T(8,128)(2,1)}, bf16[2,768,512]{2,1,0:T(8,128)(2,1)}, u32[]{:S(2)}, u32[]{:S(2)}) %collective-permute-start.33) | collective-permute-done | bytes 1572896 | tf_op jit(solution)/shard_map/ppermute | solution.py:52
  192.1 4.5 collective-permute-done.34.rest_5_
  210.4 12.4 %shard_map.332 = (f32[384,1024]{1,0:T(8,128)}, bf16[384,1024]{1,0:T(8,128)(2,1)}, bf16[384,1024]{1,0:T(8,128)(2,1)}, bf16[384,1024]{1,0:T(8,128)(2,1)}, bf16[384...) custom-call(s32[2]{0:T(128)} %pad_add_fusion.ids, ...), custom_call_target="tpu_custom_call" | custom-call | flops 3221225472 | bytes 19800584 | tf_op jit(solution)/shard_map/pallas_call | solution.py:561
  222.9 27.3 %shard_map.333 = (bf16[384,1024]{1,0:T(8,128)(2,1)}, f32[384,1024]{1,0:T(8,128)}, bf16[384,8192]{1,0:T(8,128)(2,1)}, f32[1,4096]{1,0:T(1,128)}) custom-call(s32[2]{0:T(128)} %pad_add_fusion.ids, bf16[384,1024]{1,0:T(8,128)(2,1)} %get-tuple-element.156.nb, bf16[384,1024]{1,0:T(8,128)(2,1)} %get-tuple-element.157.g, f32[384,1024]{1,0:T(8,128)} %get-tuple-element.158.mid, ...), custom_call_target="tpu_custom_call" | custom-call | flops 12884901888 | bytes 28611080 | tf_op jit(solution)/shard_map/pallas_call | solution.py:561
  252.1 14.6 %shard_map.334 = (bf16[384,1024]{1,0:T(8,128)(2,1)}, bf16[384,4096]{1,0:T(8,128)(2,1)}, f32[128,1024]{1,0:T(8,128)}, f32[1,1024]{1,0:T(1,128)}, f32[1,1024]{1,0:T(1,128)}) custom-call(s32[2]{0:T(128)} %pad_add_fusion.ids, bf16[384,1024]{1,0:T(8,128)(2,1)} %get-tuple-element.157.g, f32[384,1024]{1,0:T(8,128)} %get-tuple-element.164.gnb, ...), custom_call_target="tpu_custom_call" | custom-call | flops 3221225472 | bytes 22167560 | tf_op jit(solution)/shard_map/pallas_call | solution.py:561
  267.9 15.7 %shard_map.335 = bf16[512,8192]{1,0:T(8,128)(2,1)} custom-call(s32[2]{0:T(128)} %pad_add_fusion.ids, bf16[384,8192]{1,0:T(8,128)(2,1)} %get-tuple-element.173.lm, bf16[384,8192]{1,0:T(8,128)(2,1)} %collective-permute-done.45.lt, bf16[2,384,1024]{2,1,0:T(8,128)(2,1)} %pad_maximum_fusion.1.rm, bf16[2,384,1024]{2,1,0:T(8,128)(2,1)} %copy-done.19), custom_call_target="tpu_custom_call" | custom-call | flops 6442450944 | bytes 24117248 | tf_op jit(solution)/shard_map/pallas_call | solution.py:670
  290.9 15.2 %collective-permute-done.42 = bf16[128,1024]{1,0:T(8,128)(2,1)} collective-permute-done((bf16[128,1024]{1,0:T(8,128)(2,1)}, bf16[128,1024]{1,0:T(8,128)(2,1)}, u32[]{:S(2)}, u32[]{:S(2)}) %collective-permute-start.42) | collective-permute-done | bytes 262176 | tf_op jit(solution)/shard_map/ppermute | solution.py:57
  321.7 7.1 %shard_map.337 = (bf16[512,2048]{1,0:T(8,128)(2,1)}, bf16[512,2048]{1,0:T(8,128)(2,1)}) custom-call(s32[2]{0:T(128)} %pad_add_fusion.ids, bf16[512,2048]{1,0:T(8,128)(2,1)} %pad_maximum_fusion.left, bf16[512,1024]{1,0:T(8,128)(2,1)} %copy-done.27, bf16[512,1024]{1,0:T(8,128)(2,1)} %all-gather.5.cloned.1.call-done.right1), custom_call_target="tpu_custom_call" | custom-call | flops 2147483648 | bytes 8388608 | tf_op jit(solution)/shard_map/pallas_call | solution.py:691
  328.7 9.8 %shard_map.336 = bf16[512,4096]{1,0:T(8,128)(2,1)} custom-call(s32[2]{0:T(128)} %pad_add_fusion.ids, bf16[384,4096]{1,0:T(8,128)(2,1)} %get-tuple-element.179.lm, bf16[384,4096]{1,0:T(8,128)(2,1)} %collective-permute-done.50.lt, bf16[2,384,1024]{2,1,0:T(8,128)(2,1)} %copy-done.8, bf16[2,384,1024]{2,1,0:T(8,128)(2,1)} %collective-permute-done.51.rt), custom_call_target="tpu_custom_call" | custom-call | flops 3221225472 | bytes 13631488 | tf_op jit(solution)/shard_map/pallas_call | solution.py:670
  344.8 4.8 shard_map.338
  380.6 5.9 %shard_map.339 = (bf16[512,1024]{1,0:T(8,128)(2,1)}, bf16[512,1024]{1,0:T(8,128)(2,1)}) custom-call(s32[2]{0:T(128)} %pad_add_fusion.ids, bf16[512,1024]{1,0:T(8,128)(2,1)} %pad_maximum_fusion.5.left, bf16[512,1024]{1,0:T(8,128)(2,1)} %all-gather.3.cloned.1.call-done.right0, bf16[512,1024]{1,0:T(8,128)(2,1)} %pad_maximum_fusion.4.right1), custom_call_target="tpu_custom_call" | custom-call | flops 1073741824 | bytes 5242880 | tf_op jit(solution)/shard_map/pallas_call | solution.py:691
  428.8 4.6 collective-permute-done.60
  436.7 4.1 collective-permute-start.78
  463.2 18.8 %collective-permute-done.75 = bf16[128,1024]{1,0:T(8,128)(2,1)S(1)} collective-permute-done((bf16[128,1024]{1,0:T(8,128)(2,1)S(1)}, bf16[128,1024]{1,0:T(8,128)(2,1)S(1)}, u32[]{:S(2)}, u32[]{:S(2)}) %collective-permute-start.75) | collective-permute-done | bytes 262176 | tf_op jit(solution)/shard_map/ppermute | solution.py:57
  483.9 18.1 %collective-permute-done.76 = bf16[128,1024]{1,0:T(8,128)(2,1)} collective-permute-done((bf16[128,1024]{1,0:T(8,128)(2,1)}, bf16[128,1024]{1,0:T(8,128)(2,1)}, u32[]{:S(2)}, u32[]{:S(2)}) %collective-permute-start.76) | collective-permute-done | bytes 262176 | tf_op jit(solution)/shard_map/ppermute | solution.py:57
  502.0 4.4 collective-permute-done.77
  (469 shorter events, 253.1 us)
Async XLA Ops:
  7.2 49.7 %all-gather.3.cloned.1.call-start = ((), (), s32[]{:S(2)}) async-start(), calls=%async_computation.3 | async-start | bytes 1310720 | tf_op jit(solution)/shard_map/all_gather | solution.py:38
  18.9 27.8 %collective-permute-start.12 = (bf16[4,32,1024]{2,1,0:T(8,128)(2,1)}, bf16[4,32,1024]{2,1,0:T(8,128)(2,1)}, u32[]{:S(2)}, u32[]{:S(2)}) collective-permute-start(bf16[4,32,1024]{2,1,0:T(8,128)(2,1)} %pad_maximum_fusion.14), channel_id=1, source_target_pairs={{0,1},{1,0},{2,3},{3,2},{4,5},{5,4},{6,7},{7,6},{8,9},{9,8},{10,11... | collective-permute-start | bytes 786440 | tf_op jit(solution)/shard_map/ppermute | solution.py:57
  23.4 114.5 %all-gather.5.cloned.1.call-start = ((), (), s32[]{:S(2)}) async-start(), calls=%async_computation.4 | async-start | bytes 1310720 | tf_op jit(solution)/shard_map/all_gather | solution.py:38
  82.6 27.1 %collective-permute-start.19 = (bf16[4,96,512]{2,1,0:T(8,128)(2,1)S(1)}, bf16[4,96,512]{2,1,0:T(8,128)(2,1)}, u32[]{:S(2)}, u32[]{:S(2)}) collective-permute-start(bf16[4,96,512]{2,1,0:T(8,128)(2,1)S(1)} %pad_maximum_fusion.12), channel_id=1, source_target_pairs={{0,8},{4,12},{8,0},{12,4},{16,24},{20,28},{24,16},{28,20},{1,9},{5... | collective-permute-start | bytes 1179656 | tf_op jit(solution)/shard_map/ppermute | solution.py:52
  84.1 28.2 %collective-permute-start.21 = (bf16[4,96,512]{2,1,0:T(8,128)(2,1)S(1)}, bf16[4,96,512]{2,1,0:T(8,128)(2,1)}, u32[]{:S(2)}, u32[]{:S(2)}) collective-permute-start(bf16[4,96,512]{2,1,0:T(8,128)(2,1)S(1)} %pad_maximum_fusion.13), channel_id=1, source_target_pairs={{0,16},{4,20},{8,24},{12,28},{16,0},{20,4},{24,8},{28,12},{1,17},{... | collective-permute-start | bytes 1179656 | tf_op jit(solution)/shard_map/ppermute | solution.py:52
  85.7 29.2 %collective-permute-start.23 = (bf16[2,128,1024]{2,1,0:T(8,128)(2,1)}, bf16[2,128,1024]{2,1,0:T(8,128)(2,1)}, u32[]{:S(2)}, u32[]{:S(2)}) collective-permute-start(bf16[2,128,1024]{2,1,0:T(8,128)(2,1)} %pad_maximum_fusion.8), channel_id=1, source_target_pairs={{0,1},{1,0},{2,3},{3,2},{4,5},{5,4},{6,7},{7,6},{8,9},{9,8},{10,11... | collective-permute-start | bytes 1572872 | tf_op jit(solution)/shard_map/ppermute | solution.py:57
  87.5 28.3 %collective-permute-start.25 = (bf16[2,128,1024]{2,1,0:T(8,128)(2,1)}, bf16[2,128,1024]{2,1,0:T(8,128)(2,1)}, u32[]{:S(2)}, u32[]{:S(2)}) collective-permute-start(bf16[2,128,1024]{2,1,0:T(8,128)(2,1)} %pad_maximum_fusion.8), channel_id=1, source_target_pairs={{1,2},{2,1},{5,6},{6,5},{9,10},{10,9},{13,14},{14,13},{17,18},{18,... | collective-permute-start | bytes 1572872 | tf_op jit(solution)/shard_map/ppermute | solution.py:85
  109.6 96.4 %reduce-scatter.4.cloned.1.call-start = ((), (), s32[]{:S(2)}) async-start(), calls=%async_computation.5 | async-start | bytes 1310720 | tf_op jit(solution)/shard_map/reduce_scatter | solution.py:42
  158.3 33.7 %collective-permute-start.33 = (bf16[2,768,512]{2,1,0:T(8,128)(2,1)}, bf16[2,768,512]{2,1,0:T(8,128)(2,1)}, u32[]{:S(2)}, u32[]{:S(2)}) collective-permute-start(bf16[2,768,512]{2,1,0:T(8,128)(2,1)} %constant_dynamic-update-slice_fusion.8.rest_0_), channel_id=1, source_target_pairs={{0,16},{4,20},{8,24},{12,28},{16,0},{20,4},{24,8},{28,12},{1,17},{... | collective-permute-start | bytes 4718600 | tf_op jit(solution)/shard_map/ppermute | solution.py:52
  163.2 33.4 %collective-permute-start.34 = (bf16[2,768,512]{2,1,0:T(8,128)(2,1)}, bf16[2,768,512]{2,1,0:T(8,128)(2,1)}, u32[]{:S(2)}, u32[]{:S(2)}) collective-permute-start(bf16[2,768,512]{2,1,0:T(8,128)(2,1)} %constant_dynamic-update-slice_fusion.10.rest_4_), channel_id=1, source_target_pairs={{0,8},{4,12},{8,0},{12,4},{16,24},{20,28},{24,16},{28,20},{1,9},{5... | collective-permute-start | bytes 4718600 | tf_op jit(solution)/shard_map/ppermute | solution.py:52
  164.7 232.9 %reduce-scatter.6.cloned.1.call-start = ((), (), s32[]{:S(2)}) async-start(), calls=%async_computation.6 | async-start | bytes 10485760 | tf_op jit(solution)/shard_map/reduce_scatter | solution.py:180
  164.9 35.3 %collective-permute-start.29 = (bf16[4,192,512]{2,1,0:T(8,128)(2,1)}, bf16[4,192,512]{2,1,0:T(8,128)(2,1)}, u32[]{:S(2)}, u32[]{:S(2)}) collective-permute-start(bf16[4,192,512]{2,1,0:T(8,128)(2,1)} %copy-done.17), channel_id=1, source_target_pairs={{0,4},{4,0},{8,12},{12,8},{16,20},{20,16},{24,28},{28,24},{1,5},{5... | collective-permute-start | bytes 2359304 | tf_op jit(solution)/shard_map/ppermute | solution.py:52
  165.0 35.7 %collective-permute-start.30 = (bf16[4,192,512]{2,1,0:T(8,128)(2,1)}, bf16[4,192,512]{2,1,0:T(8,128)(2,1)}, u32[]{:S(2)}, u32[]{:S(2)}) collective-permute-start(bf16[4,192,512]{2,1,0:T(8,128)(2,1)} %copy-done.32), channel_id=1, source_target_pairs={{0,4},{4,0},{8,12},{12,8},{16,20},{20,16},{24,28},{28,24},{1,5},{5... | collective-permute-start | bytes 2359304 | tf_op jit(solution)/shard_map/ppermute | solution.py:52
  169.0 32.6 %collective-permute-start.31 = (bf16[4,192,512]{2,1,0:T(8,128)(2,1)}, bf16[4,192,512]{2,1,0:T(8,128)(2,1)}, u32[]{:S(2)}, u32[]{:S(2)}) collective-permute-start(bf16[4,192,512]{2,1,0:T(8,128)(2,1)} %copy-done.18), channel_id=1, source_target_pairs={{0,4},{4,0},{8,12},{12,8},{16,20},{20,16},{24,28},{28,24},{1,5},{5... | collective-permute-start | bytes 2359304 | tf_op jit(solution)/shard_map/ppermute | solution.py:52
  196.6 26.2 %collective-permute-start.38 = (bf16[2,768,512]{2,1,0:T(8,128)(2,1)}, bf16[2,768,512]{2,1,0:T(8,128)(2,1)}, u32[]{:S(2)}, u32[]{:S(2)}) collective-permute-start(bf16[2,768,512]{2,1,0:T(8,128)(2,1)} %constant_dynamic-update-slice_fusion.8.rest_0_), channel_id=1, source_target_pairs={{0,4},{4,0},{8,12},{12,8},{16,20},{20,16},{24,28},{28,24},{1,5},{5... | collective-permute-start | bytes 4718600 | tf_op jit(solution)/shard_map/ppermute | solution.py:52
  283.6 159.7 %reduce-scatter.8.cloned.1.call-start = ((), (), s32[]{:S(2)}) async-start(), calls=%async_computation.7 | async-start | bytes 5242880 | tf_op jit(solution)/shard_map/reduce_scatter | solution.py:180
  283.6 45.1 %collective-permute-start.50 = (bf16[384,4096]{1,0:T(8,128)(2,1)}, bf16[384,4096]{1,0:T(8,128)(2,1)}, u32[]{:S(2)}, u32[]{:S(2)}) collective-permute-start(bf16[384,4096]{1,0:T(8,128)(2,1)} %get-tuple-element.179.lm), channel_id=1, source_target_pairs={{0,4},{4,0},{8,12},{12,8},{16,20},{20,16},{24,28},{28,24},{1,5},{5... | collective-permute-start | bytes 9437192 | tf_op jit(solution)/shard_map/ppermute | solution.py:52
  290.8 37.9 %collective-permute-start.51 = (bf16[2,384,1024]{2,1,0:T(8,128)(2,1)S(1)}, bf16[2,384,1024]{2,1,0:T(8,128)(2,1)}, u32[]{:S(2)}, u32[]{:S(2)}) collective-permute-start(bf16[2,384,1024]{2,1,0:T(8,128)(2,1)S(1)} %pad_maximum_fusion.2.rm), channel_id=1, source_target_pairs={{0,4},{4,0},{8,12},{12,8},{16,20},{20,16},{24,28},{28,24},{1,5},{5... | collective-permute-start | bytes 4718600 | tf_op jit(solution)/shard_map/ppermute | solution.py:52
  354.1 40.2 %collective-permute-start.71 = (bf16[512,2048]{1,0:T(8,128)(2,1)}, bf16[512,2048]{1,0:T(8,128)(2,1)}, u32[]{:S(2)}, u32[]{:S(2)}) collective-permute-start(bf16[512,2048]{1,0:T(8,128)(2,1)} %get-tuple-element.204), channel_id=1, source_target_pairs={{0,4},{4,0},{8,12},{12,8},{16,20},{20,16},{24,28},{28,24},{1,5},{5... | collective-permute-start | bytes 6291464 | tf_op jit(solution)/shard_map/ppermute | solution.py:52
  433.8 27.6 %collective-permute-start.74 = (bf16[128,2048]{1,0:T(8,128)(2,1)}, bf16[128,2048]{1,0:T(8,128)(2,1)}, u32[]{:S(2)}, u32[]{:S(2)}) collective-permute-start(bf16[128,2048]{1,0:T(8,128)(2,1)} %get-tuple-element.294), channel_id=1, source_target_pairs={{0,24},{4,28},{8,16},{12,20},{16,8},{20,12},{24,0},{28,4},{1,25},{... | collective-permute-start | bytes 1572872 | tf_op jit(solution)/shard_map/ppermute | solution.py:52
  436.7 72.6 %collective-permute-start.78 = (bf16[128,2048]{1,0:T(8,128)(2,1)}, bf16[128,2048]{1,0:T(8,128)(2,1)}, u32[]{:S(2)}, u32[]{:S(2)}) collective-permute-start(bf16[128,2048]{1,0:T(8,128)(2,1)} %pad_maximum_fusion.9), channel_id=1, source_target_pairs={{0,1},{1,0},{2,3},{3,2},{4,5},{5,4},{6,7},{7,6},{8,9},{9,8},{10,11... | collective-permute-start | bytes 1572872 | tf_op jit(solution)/shard_map/ppermute | solution.py:57
  440.8 68.5 %collective-permute-start.79 = (bf16[128,2048]{1,0:T(8,128)(2,1)}, bf16[128,2048]{1,0:T(8,128)(2,1)}, u32[]{:S(2)}, u32[]{:S(2)}) collective-permute-start(bf16[128,2048]{1,0:T(8,128)(2,1)} %pad_maximum_fusion.10), channel_id=1, source_target_pairs={{0,2},{1,3},{2,0},{3,1},{4,6},{5,7},{6,4},{7,5},{8,10},{9,11},{10,... | collective-permute-start | bytes 1572872 | tf_op jit(solution)/shard_map/ppermute | solution.py:57
  453.3 56.1 %collective-permute-start.80 = (bf16[128,2048]{1,0:T(8,128)(2,1)}, bf16[128,2048]{1,0:T(8,128)(2,1)S(1)}, u32[]{:S(2)}, u32[]{:S(2)}) collective-permute-start(bf16[128,2048]{1,0:T(8,128)(2,1)} %pad_maximum_fusion.11), channel_id=1, source_target_pairs={{0,3},{1,2},{2,1},{3,0},{4,7},{5,6},{6,5},{7,4},{8,11},{9,10},{10,... | collective-permute-start | bytes 1572872 | tf_op jit(solution)/shard_map/ppermute | solution.py:57
  461.4 40.6 %collective-permute-start.76 = (bf16[128,1024]{1,0:T(8,128)(2,1)}, bf16[128,1024]{1,0:T(8,128)(2,1)}, u32[]{:S(2)}, u32[]{:S(2)}) collective-permute-start(bf16[128,1024]{1,0:T(8,128)(2,1)} %pad_maximum_fusion.17), channel_id=1, source_target_pairs={{0,2},{1,3},{2,0},{3,1},{4,6},{5,7},{6,4},{7,5},{8,10},{9,11},{10,... | collective-permute-start | bytes 786440 | tf_op jit(solution)/shard_map/ppermute | solution.py:57
  (134 other events, 1984.5 us)
Sparse Core Ops, SparseCore 0:
  23.5 32.3 all-gather.2
  109.7 28.0 all-gather.4
  164.8 23.6 reduce-scatter.3
  283.7 85.5 reduce-scatter.5
  372.1 53.0 reduce-scatter.7

commit v5 on v4

--- a/solution.py
+++ b/solution.py
@@ -86,10 +86,13 @@
         outer = lax.ppermute(after(far, *then), "mp", [(2, 3), (1, 0)])
         self.held = (near, far, inner, outer)
 
+    def shards_straight(self):
+        self.held = tuple(swap_mp(self.piece, r) for r in (1, 2, 3))
+
     def plane_first(self, *marks):
-        near, far, inner, outer = all_after(self.held, *marks)
+        near, far, *hops = all_after(self.held, *marks)
         z = lax.axis_index("mp")
-        last = jnp.where((z == 1) | (z == 2), inner, outer)
+        last = hops[0] if len(hops) == 1 else jnp.where((z == 1) | (z == 2), *hops)
         half = near.shape[2] // 2
         self.held = []
         for h, side in enumerate(SIDES):
@@ -784,7 +787,7 @@
     attn_w = Gather(jnp.concatenate([own_cols(t_qkv), own_rows(t_out)[None]], axis=0))
     ff_w = Gather(jnp.stack([own_cols(t_up), own_rows(t_down)]))
     out_w = Gather(own_rows(w_out)[None])
-    out_w.shards()
+    out_w.shards_straight()
     out_w.plane_first()
     out_w.plane_last()
     out_w.cores()

time: 530 us -> 527 us (level)
  starting transfers between devices: 96 us -> 89.7 us
    ppermute x3 -> x2, starting transfers between devices: 11.6 us -> 7.04 us  [shards(): outer = lax.ppermute(after(far, *then), 'mp', [(2, 3), (1, 0)])]
    ppermute x36 -> x37, waiting for transfers between devices: 98.6 us -> 101 us  [swap_mp(): return lax.ppermute(value, 'mp', [(i, i ^ mask) for i in range(size)])]
    ppermute x3 -> x2, waiting for transfers between devices: 8.47 us -> 10.9 us  [shards(): inner = lax.ppermute(piece, 'mp', [(1, 2), (2, 1)])]
    ppermute x36 -> x37, starting transfers between devices: 47.7 us -> 48.5 us  [swap_mp(): return lax.ppermute(value, 'mp', [(i, i ^ mask) for i in range(size)])]
  transfers between devices with their start and end apart: 86 -> 85, of which waited for: 33 -> 33; matrix products, arithmetic and copies ran while one was open for 20% -> 20% of each run, Pallas kernels for 10% -> 11%
where the time goes in v5:
time: 527 us; the launch traced here: 517 us
  waiting for transfers between devices  176 us (33%)
  Pallas kernels  102 us (19%)
  starting transfers between devices  89.7 us (17%)
  local copies, waits for them, and re-layouts  59.4 us (11%)
  other arithmetic  47.8 us (9%)
  matrix products  27.1 us (5%)
  between operations  15.6 us (3%)
    ppermute x37, waiting for transfers between devices, swap_mp(): return lax.ppermute(value, 'mp', [(i, i ^ mask) for i in range(size)])  101 us
    pallas_call x5, Pallas kernels, call(): pl.pallas_call(kernel, out_shape=outs, in_specs=[pl.BlockSpec(memory_spac...  63.3 us
    ppermute x39, waiting for transfers between devices, swap_dp(): return lax.ppermute(value, 'dp', [(i, i ^ bit) for i in range(size)])  54.3 us
    ppermute x37, starting transfers between devices, swap_mp(): return lax.ppermute(value, 'mp', [(i, i ^ mask) for i in range(size)])  48.5 us
    ppermute x39, starting transfers between devices, swap_dp(): return lax.ppermute(value, 'dp', [(i, i ^ bit) for i in range(size)])  29 us
    pallas_call x2, Pallas kernels, pair_grad(): pl.pallas_call(functools.partial(pair_grad_kernel, lambda j: (j == 0) | (...  25.4 us
    unnamed x158, local copies, waits for them, and re-layouts  23 us
    pallas_call x2, Pallas kernels, frame_grad(): pl.pallas_call(functools.partial(frame_grad_kernel, split // step), grid=...  13 us
  transfers between devices with their start and end apart: 85, of which 33 were waited for; matrix products, arithmetic and copies ran while one was open for 20% of the time, Pallas kernels for 11%

profile of v5, /device:TPU:8, one launch (start us, length us, event | category | flops | bytes accessed | tf_op | source)
XLA Modules:
  0.0 517.2 jit_solution(16976498164609518045)
XLA Ops:
  43.4 10.3 %collective-permute-done.13 = bf16[4,32,1024]{2,1,0:T(8,128)(2,1)S(1)} collective-permute-done((bf16[4,32,1024]{2,1,0:T(8,128)(2,1)}, bf16[4,32,1024]{2,1,0:T(8,128)(2,1)S(1)}, u32[]{:S(2)}, u32[]{:S(2)}) %collective-permute-start.13) | collective-permute-done | bytes 262176 | tf_op jit(solution)/shard_map/ppermute | solution.py:85
  74.2 4.3 shard_map.331
  88.9 15.0 %collective-permute-done.23 = bf16[2,128,1024]{2,1,0:T(8,128)(2,1)} collective-permute-done((bf16[2,128,1024]{2,1,0:T(8,128)(2,1)}, bf16[2,128,1024]{2,1,0:T(8,128)(2,1)}, u32[]{:S(2)}, u32[]{:S(2)}) %collective-permute-start.23) | collective-permute-done | bytes 524320 | tf_op jit(solution)/shard_map/ppermute | solution.py:57
  103.9 5.0 collective-permute-start.25
  114.8 5.7 %collective-permute-done.25 = bf16[2,128,1024]{2,1,0:T(8,128)(2,1)} collective-permute-done((bf16[2,128,1024]{2,1,0:T(8,128)(2,1)}, bf16[2,128,1024]{2,1,0:T(8,128)(2,1)}, u32[]{:S(2)}, u32[]{:S(2)}) %collective-permute-start.25) | collective-permute-done | bytes 524320 | tf_op jit(solution)/shard_map/ppermute | solution.py:86
  125.0 5.7 %collective-permute-done.19.rest_1_ = bf16[4,192,512]{2,1,0:T(8,128)(2,1)S(1)} collective-permute-done((bf16[4,192,512]{2,1,0:T(8,128)(2,1)S(1)}, bf16[4,192,512]{2,1,0:T(8,128)(2,1)S(1)}, u32[]{:S(2)}, u32[]{:S(2)}) %collective-permute-start.19) | collective-permute-done | bytes 786464 | tf_op jit(solution)/shard_map/ppermute | solution.py:52
  137.0 9.1 %collective-permute-done.26 = bf16[2,384,512]{2,1,0:T(8,128)(2,1)} collective-permute-done((bf16[2,384,512]{2,1,0:T(8,128)(2,1)S(1)}, bf16[2,384,512]{2,1,0:T(8,128)(2,1)}, u32[]{:S(2)}, u32[]{:S(2)}) %collective-permute-start.26) | collective-permute-done | bytes 786464 | tf_op jit(solution)/shard_map/ppermute | solution.py:52
  146.1 4.2 multiply_convert_fusion.1
  167.4 22.0 %collective-permute-done.32.rest_1_ = bf16[2,768,512]{2,1,0:T(8,128)(2,1)} collective-permute-done((bf16[2,768,512]{2,1,0:T(8,128)(2,1)}, bf16[2,768,512]{2,1,0:T(8,128)(2,1)}, u32[]{:S(2)}, u32[]{:S(2)}) %collective-permute-start.32) | collective-permute-done | bytes 1572896 | tf_op jit(solution)/shard_map/ppermute | solution.py:52
  189.4 4.9 collective-permute-done.33.rest_5_
  208.2 12.4 %shard_map.332 = (f32[384,1024]{1,0:T(8,128)}, bf16[384,1024]{1,0:T(8,128)(2,1)}, bf16[384,1024]{1,0:T(8,128)(2,1)}, bf16[384,1024]{1,0:T(8,128)(2,1)}, bf16[384...) custom-call(s32[2]{0:T(128)} %pad_add_fusion.ids, ...), custom_call_target="tpu_custom_call" | custom-call | flops 3221225472 | bytes 19800584 | tf_op jit(solution)/shard_map/pallas_call | solution.py:564
  220.6 27.3 %shard_map.333 = (bf16[384,1024]{1,0:T(8,128)(2,1)}, f32[384,1024]{1,0:T(8,128)}, bf16[384,8192]{1,0:T(8,128)(2,1)}, f32[1,4096]{1,0:T(1,128)}) custom-call(s32[2]{0:T(128)} %pad_add_fusion.ids, bf16[384,1024]{1,0:T(8,128)(2,1)} %get-tuple-element.154.nb, bf16[384,1024]{1,0:T(8,128)(2,1)} %get-tuple-element.155.g, f32[384,1024]{1,0:T(8,128)} %get-tuple-element.156.mid, ...), custom_call_target="tpu_custom_call" | custom-call | flops 12884901888 | bytes 28611080 | tf_op jit(solution)/shard_map/pallas_call | solution.py:564
  249.9 14.6 %shard_map.334 = (bf16[384,1024]{1,0:T(8,128)(2,1)}, bf16[384,4096]{1,0:T(8,128)(2,1)}, f32[128,1024]{1,0:T(8,128)}, f32[1,1024]{1,0:T(1,128)}, f32[1,1024]{1,0:T(1,128)}) custom-call(s32[2]{0:T(128)} %pad_add_fusion.ids, bf16[384,1024]{1,0:T(8,128)(2,1)} %get-tuple-element.155.g, f32[384,1024]{1,0:T(8,128)} %get-tuple-element.162.gnb, ...), custom_call_target="tpu_custom_call" | custom-call | flops 3221225472 | bytes 22167560 | tf_op jit(solution)/shard_map/pallas_call | solution.py:564
  265.7 15.7 %shard_map.335 = bf16[512,8192]{1,0:T(8,128)(2,1)} custom-call(s32[2]{0:T(128)} %pad_add_fusion.ids, bf16[384,8192]{1,0:T(8,128)(2,1)} %get-tuple-element.171.lm, bf16[384,8192]{1,0:T(8,128)(2,1)} %collective-permute-done.44.lt, bf16[2,384,1024]{2,1,0:T(8,128)(2,1)} %pad_maximum_fusion.1.rm, bf16[2,384,1024]{2,1,0:T(8,128)(2,1)} %copy-done.19), custom_call_target="tpu_custom_call" | custom-call | flops 6442450944 | bytes 24117248 | tf_op jit(solution)/shard_map/pallas_call | solution.py:673
  288.7 15.1 %collective-permute-done.41 = bf16[128,1024]{1,0:T(8,128)(2,1)} collective-permute-done((bf16[128,1024]{1,0:T(8,128)(2,1)}, bf16[128,1024]{1,0:T(8,128)(2,1)}, u32[]{:S(2)}, u32[]{:S(2)}) %collective-permute-start.41) | collective-permute-done | bytes 262176 | tf_op jit(solution)/shard_map/ppermute | solution.py:57
  319.6 7.1 %shard_map.337 = (bf16[512,2048]{1,0:T(8,128)(2,1)}, bf16[512,2048]{1,0:T(8,128)(2,1)}) custom-call(s32[2]{0:T(128)} %pad_add_fusion.ids, bf16[512,2048]{1,0:T(8,128)(2,1)} %pad_maximum_fusion.left, bf16[512,1024]{1,0:T(8,128)(2,1)} %copy-done.27, bf16[512,1024]{1,0:T(8,128)(2,1)} %all-gather.5.cloned.1.call-done.right1), custom_call_target="tpu_custom_call" | custom-call | flops 2147483648 | bytes 8388608 | tf_op jit(solution)/shard_map/pallas_call | solution.py:694
  326.6 9.8 %shard_map.336 = bf16[512,4096]{1,0:T(8,128)(2,1)} custom-call(s32[2]{0:T(128)} %pad_add_fusion.ids, bf16[384,4096]{1,0:T(8,128)(2,1)} %get-tuple-element.177.lm, bf16[384,4096]{1,0:T(8,128)(2,1)} %collective-permute-done.49.lt, bf16[2,384,1024]{2,1,0:T(8,128)(2,1)} %copy-done.8, bf16[2,384,1024]{2,1,0:T(8,128)(2,1)} %collective-permute-done.50.rt), custom_call_target="tpu_custom_call" | custom-call | flops 3221225472 | bytes 13631488 | tf_op jit(solution)/shard_map/pallas_call | solution.py:673
  342.7 4.8 shard_map.338
  378.4 5.9 %shard_map.339 = (bf16[512,1024]{1,0:T(8,128)(2,1)}, bf16[512,1024]{1,0:T(8,128)(2,1)}) custom-call(s32[2]{0:T(128)} %pad_add_fusion.ids, bf16[512,1024]{1,0:T(8,128)(2,1)} %pad_maximum_fusion.5.left, bf16[512,1024]{1,0:T(8,128)(2,1)} %all-gather.3.cloned.1.call-done.right0, bf16[512,1024]{1,0:T(8,128)(2,1)} %pad_maximum_fusion.4.right1), custom_call_target="tpu_custom_call" | custom-call | flops 1073741824 | bytes 5242880 | tf_op jit(solution)/shard_map/pallas_call | solution.py:694
  426.3 4.6 collective-permute-done.59
  434.2 4.1 collective-permute-start.77
  460.7 18.8 %collective-permute-done.74 = bf16[128,1024]{1,0:T(8,128)(2,1)S(1)} collective-permute-done((bf16[128,1024]{1,0:T(8,128)(2,1)S(1)}, bf16[128,1024]{1,0:T(8,128)(2,1)S(1)}, u32[]{:S(2)}, u32[]{:S(2)}) %collective-permute-start.74) | collective-permute-done | bytes 262176 | tf_op jit(solution)/shard_map/ppermute | solution.py:57
  481.4 18.1 %collective-permute-done.75 = bf16[128,1024]{1,0:T(8,128)(2,1)} collective-permute-done((bf16[128,1024]{1,0:T(8,128)(2,1)}, bf16[128,1024]{1,0:T(8,128)(2,1)}, u32[]{:S(2)}, u32[]{:S(2)}) %collective-permute-start.75) | collective-permute-done | bytes 262176 | tf_op jit(solution)/shard_map/ppermute | solution.py:57
  499.5 4.4 collective-permute-done.76
  (466 shorter events, 252.7 us)
Async XLA Ops:
  7.2 48.9 %all-gather.3.cloned.1.call-start = ((), (), s32[]{:S(2)}) async-start(), calls=%async_computation.3 | async-start | bytes 1310720 | tf_op jit(solution)/shard_map/all_gather | solution.py:38
  17.0 26.3 %collective-permute-start.11 = (bf16[4,32,1024]{2,1,0:T(8,128)(2,1)}, bf16[4,32,1024]{2,1,0:T(8,128)(2,1)}, u32[]{:S(2)}, u32[]{:S(2)}) collective-permute-start(bf16[4,32,1024]{2,1,0:T(8,128)(2,1)} %pad_maximum_fusion.14), channel_id=1, source_target_pairs={{0,1},{1,0},{2,3},{3,2},{4,5},{5,4},{6,7},{7,6},{8,9},{9,8},{10,11... | collective-permute-start | bytes 786440 | tf_op jit(solution)/shard_map/ppermute | solution.py:57
  21.9 115.1 %all-gather.5.cloned.1.call-start = ((), (), s32[]{:S(2)}) async-start(), calls=%async_computation.4 | async-start | bytes 1310720 | tf_op jit(solution)/shard_map/all_gather | solution.py:38
  25.6 28.0 %collective-permute-start.13 = (bf16[4,32,1024]{2,1,0:T(8,128)(2,1)}, bf16[4,32,1024]{2,1,0:T(8,128)(2,1)S(1)}, u32[]{:S(2)}, u32[]{:S(2)}) collective-permute-start(bf16[4,32,1024]{2,1,0:T(8,128)(2,1)} %pad_maximum_fusion.14), channel_id=1, source_target_pairs={{1,2},{2,1},{5,6},{6,5},{9,10},{10,9},{13,14},{14,13},{17,18},{18,... | collective-permute-start | bytes 786440 | tf_op jit(solution)/shard_map/ppermute | solution.py:85
  82.2 26.8 %collective-permute-start.18 = (bf16[4,96,512]{2,1,0:T(8,128)(2,1)S(1)}, bf16[4,96,512]{2,1,0:T(8,128)(2,1)}, u32[]{:S(2)}, u32[]{:S(2)}) collective-permute-start(bf16[4,96,512]{2,1,0:T(8,128)(2,1)S(1)} %pad_maximum_fusion.12), channel_id=1, source_target_pairs={{0,8},{4,12},{8,0},{12,4},{16,24},{20,28},{24,16},{28,20},{1,9},{5... | collective-permute-start | bytes 1179656 | tf_op jit(solution)/shard_map/ppermute | solution.py:52
  83.6 28.0 %collective-permute-start.20 = (bf16[4,96,512]{2,1,0:T(8,128)(2,1)S(1)}, bf16[4,96,512]{2,1,0:T(8,128)(2,1)}, u32[]{:S(2)}, u32[]{:S(2)}) collective-permute-start(bf16[4,96,512]{2,1,0:T(8,128)(2,1)S(1)} %pad_maximum_fusion.13), channel_id=1, source_target_pairs={{0,16},{4,20},{8,24},{12,28},{16,0},{20,4},{24,8},{28,12},{1,17},{... | collective-permute-start | bytes 1179656 | tf_op jit(solution)/shard_map/ppermute | solution.py:52
  85.2 29.0 %collective-permute-start.22 = (bf16[2,128,1024]{2,1,0:T(8,128)(2,1)}, bf16[2,128,1024]{2,1,0:T(8,128)(2,1)}, u32[]{:S(2)}, u32[]{:S(2)}) collective-permute-start(bf16[2,128,1024]{2,1,0:T(8,128)(2,1)} %pad_maximum_fusion.8), channel_id=1, source_target_pairs={{0,1},{1,0},{2,3},{3,2},{4,5},{5,4},{6,7},{7,6},{8,9},{9,8},{10,11... | collective-permute-start | bytes 1572872 | tf_op jit(solution)/shard_map/ppermute | solution.py:57
  86.7 28.1 %collective-permute-start.24 = (bf16[2,128,1024]{2,1,0:T(8,128)(2,1)}, bf16[2,128,1024]{2,1,0:T(8,128)(2,1)}, u32[]{:S(2)}, u32[]{:S(2)}) collective-permute-start(bf16[2,128,1024]{2,1,0:T(8,128)(2,1)} %pad_maximum_fusion.8), channel_id=1, source_target_pairs={{1,2},{2,1},{5,6},{6,5},{9,10},{10,9},{13,14},{14,13},{17,18},{18,... | collective-permute-start | bytes 1572872 | tf_op jit(solution)/shard_map/ppermute | solution.py:85
  109.0 94.9 %reduce-scatter.4.cloned.1.call-start = ((), (), s32[]{:S(2)}) async-start(), calls=%async_computation.5 | async-start | bytes 1310720 | tf_op jit(solution)/shard_map/reduce_scatter | solution.py:42
  156.7 32.8 %collective-permute-start.32 = (bf16[2,768,512]{2,1,0:T(8,128)(2,1)}, bf16[2,768,512]{2,1,0:T(8,128)(2,1)}, u32[]{:S(2)}, u32[]{:S(2)}) collective-permute-start(bf16[2,768,512]{2,1,0:T(8,128)(2,1)} %constant_dynamic-update-slice_fusion.8.rest_0_), channel_id=1, source_target_pairs={{0,16},{4,20},{8,24},{12,28},{16,0},{20,4},{24,8},{28,12},{1,17},{... | collective-permute-start | bytes 4718600 | tf_op jit(solution)/shard_map/ppermute | solution.py:52
  161.8 32.6 %collective-permute-start.33 = (bf16[2,768,512]{2,1,0:T(8,128)(2,1)}, bf16[2,768,512]{2,1,0:T(8,128)(2,1)}, u32[]{:S(2)}, u32[]{:S(2)}) collective-permute-start(bf16[2,768,512]{2,1,0:T(8,128)(2,1)} %constant_dynamic-update-slice_fusion.10.rest_4_), channel_id=1, source_target_pairs={{0,8},{4,12},{8,0},{12,4},{16,24},{20,28},{24,16},{28,20},{1,9},{5... | collective-permute-start | bytes 4718600 | tf_op jit(solution)/shard_map/ppermute | solution.py:52
  163.0 232.6 %reduce-scatter.6.cloned.1.call-start = ((), (), s32[]{:S(2)}) async-start(), calls=%async_computation.6 | async-start | bytes 10485760 | tf_op jit(solution)/shard_map/reduce_scatter | solution.py:183
  163.2 34.7 %collective-permute-start.28 = (bf16[4,192,512]{2,1,0:T(8,128)(2,1)}, bf16[4,192,512]{2,1,0:T(8,128)(2,1)}, u32[]{:S(2)}, u32[]{:S(2)}) collective-permute-start(bf16[4,192,512]{2,1,0:T(8,128)(2,1)} %copy-done.17), channel_id=1, source_target_pairs={{0,4},{4,0},{8,12},{12,8},{16,20},{20,16},{24,28},{28,24},{1,5},{5... | collective-permute-start | bytes 2359304 | tf_op jit(solution)/shard_map/ppermute | solution.py:52
  163.3 35.1 %collective-permute-start.29 = (bf16[4,192,512]{2,1,0:T(8,128)(2,1)}, bf16[4,192,512]{2,1,0:T(8,128)(2,1)}, u32[]{:S(2)}, u32[]{:S(2)}) collective-permute-start(bf16[4,192,512]{2,1,0:T(8,128)(2,1)} %copy-done.32), channel_id=1, source_target_pairs={{0,4},{4,0},{8,12},{12,8},{16,20},{20,16},{24,28},{28,24},{1,5},{5... | collective-permute-start | bytes 2359304 | tf_op jit(solution)/shard_map/ppermute | solution.py:52
  167.4 32.0 %collective-permute-start.30 = (bf16[4,192,512]{2,1,0:T(8,128)(2,1)}, bf16[4,192,512]{2,1,0:T(8,128)(2,1)}, u32[]{:S(2)}, u32[]{:S(2)}) collective-permute-start(bf16[4,192,512]{2,1,0:T(8,128)(2,1)} %copy-done.18), channel_id=1, source_target_pairs={{0,4},{4,0},{8,12},{12,8},{16,20},{20,16},{24,28},{28,24},{1,5},{5... | collective-permute-start | bytes 2359304 | tf_op jit(solution)/shard_map/ppermute | solution.py:52
  281.4 159.4 %reduce-scatter.8.cloned.1.call-start = ((), (), s32[]{:S(2)}) async-start(), calls=%async_computation.7 | async-start | bytes 5242880 | tf_op jit(solution)/shard_map/reduce_scatter | solution.py:183
  281.4 45.2 %collective-permute-start.49 = (bf16[384,4096]{1,0:T(8,128)(2,1)}, bf16[384,4096]{1,0:T(8,128)(2,1)}, u32[]{:S(2)}, u32[]{:S(2)}) collective-permute-start(bf16[384,4096]{1,0:T(8,128)(2,1)} %get-tuple-element.177.lm), channel_id=1, source_target_pairs={{0,4},{4,0},{8,12},{12,8},{16,20},{20,16},{24,28},{28,24},{1,5},{5... | collective-permute-start | bytes 9437192 | tf_op jit(solution)/shard_map/ppermute | solution.py:52
  288.6 38.0 %collective-permute-start.50 = (bf16[2,384,1024]{2,1,0:T(8,128)(2,1)S(1)}, bf16[2,384,1024]{2,1,0:T(8,128)(2,1)}, u32[]{:S(2)}, u32[]{:S(2)}) collective-permute-start(bf16[2,384,1024]{2,1,0:T(8,128)(2,1)S(1)} %pad_maximum_fusion.2.rm), channel_id=1, source_target_pairs={{0,4},{4,0},{8,12},{12,8},{16,20},{20,16},{24,28},{28,24},{1,5},{5... | collective-permute-start | bytes 4718600 | tf_op jit(solution)/shard_map/ppermute | solution.py:52
  352.0 40.3 %collective-permute-start.70 = (bf16[512,2048]{1,0:T(8,128)(2,1)}, bf16[512,2048]{1,0:T(8,128)(2,1)}, u32[]{:S(2)}, u32[]{:S(2)}) collective-permute-start(bf16[512,2048]{1,0:T(8,128)(2,1)} %get-tuple-element.202), channel_id=1, source_target_pairs={{0,4},{4,0},{8,12},{12,8},{16,20},{20,16},{24,28},{28,24},{1,5},{5... | collective-permute-start | bytes 6291464 | tf_op jit(solution)/shard_map/ppermute | solution.py:52
  431.8 27.1 %collective-permute-start.73 = (bf16[128,2048]{1,0:T(8,128)(2,1)}, bf16[128,2048]{1,0:T(8,128)(2,1)}, u32[]{:S(2)}, u32[]{:S(2)}) collective-permute-start(bf16[128,2048]{1,0:T(8,128)(2,1)} %get-tuple-element.292), channel_id=1, source_target_pairs={{0,24},{4,28},{8,16},{12,20},{16,8},{20,12},{24,0},{28,4},{1,25},{... | collective-permute-start | bytes 1572872 | tf_op jit(solution)/shard_map/ppermute | solution.py:52
  434.2 72.6 %collective-permute-start.77 = (bf16[128,2048]{1,0:T(8,128)(2,1)}, bf16[128,2048]{1,0:T(8,128)(2,1)}, u32[]{:S(2)}, u32[]{:S(2)}) collective-permute-start(bf16[128,2048]{1,0:T(8,128)(2,1)} %pad_maximum_fusion.9), channel_id=1, source_target_pairs={{0,1},{1,0},{2,3},{3,2},{4,5},{5,4},{6,7},{7,6},{8,9},{9,8},{10,11... | collective-permute-start | bytes 1572872 | tf_op jit(solution)/shard_map/ppermute | solution.py:57
  438.3 68.5 %collective-permute-start.78 = (bf16[128,2048]{1,0:T(8,128)(2,1)}, bf16[128,2048]{1,0:T(8,128)(2,1)}, u32[]{:S(2)}, u32[]{:S(2)}) collective-permute-start(bf16[128,2048]{1,0:T(8,128)(2,1)} %pad_maximum_fusion.10), channel_id=1, source_target_pairs={{0,2},{1,3},{2,0},{3,1},{4,6},{5,7},{6,4},{7,5},{8,10},{9,11},{10,... | collective-permute-start | bytes 1572872 | tf_op jit(solution)/shard_map/ppermute | solution.py:57
  450.8 56.0 %collective-permute-start.79 = (bf16[128,2048]{1,0:T(8,128)(2,1)}, bf16[128,2048]{1,0:T(8,128)(2,1)S(1)}, u32[]{:S(2)}, u32[]{:S(2)}) collective-permute-start(bf16[128,2048]{1,0:T(8,128)(2,1)} %pad_maximum_fusion.11), channel_id=1, source_target_pairs={{0,3},{1,2},{2,1},{3,0},{4,7},{5,6},{6,5},{7,4},{8,11},{9,10},{10,... | collective-permute-start | bytes 1572872 | tf_op jit(solution)/shard_map/ppermute | solution.py:57
  458.9 40.5 %collective-permute-start.75 = (bf16[128,1024]{1,0:T(8,128)(2,1)}, bf16[128,1024]{1,0:T(8,128)(2,1)}, u32[]{:S(2)}, u32[]{:S(2)}) collective-permute-start(bf16[128,1024]{1,0:T(8,128)(2,1)} %pad_maximum_fusion.17), channel_id=1, source_target_pairs={{0,2},{1,3},{2,0},{3,1},{4,6},{5,7},{6,4},{7,5},{8,10},{9,11},{10,... | collective-permute-start | bytes 786440 | tf_op jit(solution)/shard_map/ppermute | solution.py:57
  (133 other events, 1977.0 us)
Sparse Core Ops, SparseCore 0:
  22.1 32.9 all-gather.2
  109.1 27.9 all-gather.4
  163.1 23.7 reduce-scatter.3
  281.5 85.2 reduce-scatter.5
  369.6 53.0 reduce-scatter.7
